TPU v7x, 32 devices: a whole 2x2x4 slice. The times are simulated.
32 devices in a mesh: dp: 4 (over x, core), ctx: 8 (over z, y).
Axes of the slice: x: 2, y: 2, z: 4, core: 2. Of those that a mesh axis runs over, the one named last changes fastest.
Arguments:
- queries: bfloat16 [4, 4096, 512], P('dp', 'ctx'), may hold values from -12 to 12
- keys: bfloat16 [4, 4096, 128], P('dp', 'ctx'), may hold values from -12 to 12
- values: bfloat16 [4, 4096, 128], P('dp', 'ctx'), may hold values from -6 to 6
- doc_lengths: int32 [4, 8], P('dp'), may hold values from 1 to 2048, as said below
- owner: int32 [4, 64], P('dp'), may hold values from 0 to 7, as said below
- out_weight: bfloat16 [512, 4096], replicated, may hold values from -0.25 to 0.25
- out_grad: bfloat16 [4, 4096, 4096], P('dp', 'ctx'), may hold values from -6 to 6
Outputs:
- attn_out: bfloat16 [4, 4096, 512], P('dp', 'ctx')
- q_grad: bfloat16 [4, 4096, 512], P('dp', 'ctx')
- k_grad: bfloat16 [4, 4096, 128], P('dp', 'ctx')
- v_grad: bfloat16 [4, 4096, 128], P('dp', 'ctx')
- wo_grad: float32 [512, 4096], P(None, ('dp', 'ctx'))
- owner_lse: float32 [4, 8, 512, 4], P('dp', 'ctx')
Inputs may be any that keep to these rules, and one draw needn't show every extreme that they name: `doc_lengths`: the 8 lengths of a sequence sum to 4096; the largest is exactly 2048. owner[s, b] names the device of ctx that handles block b of 64 tokens of sequence s; the blocks that lie on one device go to distinct devices, one to each.
All inputs are finite; a program needn't handle non-finite values.
Results may differ from a plain program's by a relative error of at most 0.014.
Values may be sent and summed in bfloat16 or wider, within the bound.
No kernel may reach another device: no remote copies, remote signals or barrier semaphores. Data moves between devices by JAX's collectives and lax.ppermute only.
A program may use at most 256 MiB of HBM per device.

v0:
```python
import math

import jax
import jax.numpy as jnp
from jax import lax
from jax.sharding import PartitionSpec as P

HEAD = 128
GROUP = 4
KV_HEADS = 1
WIN = 4096


NEG = -1e30


def rotate(values_in, offsets, sign):
    half = values_in.shape[-1] // 2
    ladder = jnp.arange(half, dtype=jnp.int32).astype(jnp.float32)
    freq = 10000.0 ** (-2.0 * ladder / values_in.shape[-1])
    angle = offsets.astype(jnp.float32)[:, None] * freq[None, :]
    cosine = jnp.cos(angle)[:, None, :]
    sine = sign * jnp.sin(angle)[:, None, :]
    first = values_in[..., :half]
    second = values_in[..., half:]
    return jnp.concatenate(
        [first * cosine - second * sine, second * cosine + first * sine], axis=-1
    )


def doc_start(lengths, positions):
    ends = jnp.cumsum(lengths)
    starts = ends - lengths
    inside = (positions[:, None] >= starts[None, :]) & (positions[:, None] < ends[None, :])
    return jnp.sum(jnp.where(inside, starts[None, :], 0), axis=1)


def on_device(queries, keys, values, doc_lengths, owner, out_weight, out_grad):
    ctx_size = lax.axis_size("ctx")
    device = lax.axis_index("ctx")
    tok_rows = queries.shape[1]
    block_len = tok_rows // ctx_size
    width_q = queries.shape[2]
    width_k = keys.shape[2]
    heads = width_q // HEAD
    seq_len = tok_rows * ctx_size
    scale = 1.0 / math.sqrt(HEAD)
    span_len = WIN + block_len
    lengths = doc_lengths[0]
    grid = owner[0].reshape(ctx_size, ctx_size)
    counter = jnp.arange(ctx_size, dtype=jnp.int32)
    home_pos = device * tok_rows + jnp.arange(tok_rows, dtype=jnp.int32)
    home_rel = home_pos - doc_start(lengths, home_pos)
    key_rot = rotate(keys[0].astype(jnp.float32).reshape(tok_rows, KV_HEADS, HEAD), home_rel, 1.0)
    key_rot = key_rot.astype(jnp.bfloat16).reshape(tok_rows, width_k)
    kv_home = jnp.concatenate([key_rot, values[0]], axis=1)
    kv_all = lax.all_gather(kv_home, "ctx", axis=0, tiled=True)
    kv_all = jnp.concatenate([jnp.zeros((WIN, 2 * width_k), jnp.bfloat16), kv_all], axis=0)
    d_out = lax.dot_general(
        out_grad[0], out_weight, (((1,), (1,)), ((), ())), preferred_element_type=jnp.float32
    ).astype(jnp.bfloat16)
    own_row = lax.dynamic_index_in_dim(grid, device, 0, keepdims=False)
    dest_slot = jnp.sum(
        jnp.where(own_row[:, None] == counter[None, :], counter[:, None], 0), axis=0
    )
    send_q = queries[0].reshape(ctx_size, block_len, width_q)[dest_slot]
    send_grad = d_out.reshape(ctx_size, block_len, width_q)[dest_slot]
    recv_q, recv_grad = (
        lax.all_to_all(send_q, "ctx", split_axis=0, concat_axis=0, tiled=True),
        lax.all_to_all(send_grad, "ctx", split_axis=0, concat_axis=0, tiled=True),
    )
    src_slot = jnp.sum(jnp.where(grid == device, counter[None, :], 0), axis=1)
    firsts = counter * tok_rows + src_slot * block_len
    query_pos = firsts[:, None] + jnp.arange(block_len, dtype=jnp.int32)[None, :]
    query_start = doc_start(lengths, query_pos.reshape(-1)).reshape(ctx_size, block_len)
    query_rel = (query_pos - query_start).reshape(-1)
    query_rot = rotate(
        recv_q.astype(jnp.float32).reshape(ctx_size * block_len, heads, HEAD), query_rel, 1.0
    )
    query_rot = query_rot.astype(jnp.bfloat16).reshape(ctx_size, block_len, KV_HEADS, GROUP, HEAD)
    grad_heads = recv_grad.reshape(ctx_size, block_len, KV_HEADS, GROUP, HEAD)
    group_size = math.gcd(ctx_size, max(1, 128 // block_len))
    group_count = ctx_size // group_size
    span_ladder = jnp.arange(span_len, dtype=jnp.int32)

    def run_group(index, carry):
        attn_own, qgrad_own, lse_own, grads = carry
        members = index * group_size + jnp.arange(group_size, dtype=jnp.int32)
        group_q = query_rot[members]
        group_grad = grad_heads[members]
        group_pos = query_pos[members]
        group_start = query_start[members]
        begin = firsts[members]
        tiles = jax.vmap(lambda offset: lax.dynamic_slice_in_dim(kv_all, offset, span_len, 0))(
            begin
        )
        key_part = tiles[:, :, :width_k].reshape(group_size, span_len, KV_HEADS, HEAD)
        value_part = tiles[:, :, width_k:].reshape(group_size, span_len, KV_HEADS, HEAD)
        key_pos = begin[:, None] - WIN + span_ladder[None, :]
        valid = (
            (key_pos[:, None, :] >= group_start[:, :, None])
            & (key_pos[:, None, :] <= group_pos[:, :, None])
            & (key_pos[:, None, :] > group_pos[:, :, None] - WIN)
        )
        valid = valid[:, None, None]
        scores = (
            jnp.einsum("gqhed,gkhd->gheqk", group_q, key_part, preferred_element_type=jnp.float32)
            * scale
        )
        scores = jnp.where(valid, scores, NEG)
        top = jnp.max(scores, axis=-1)
        total = jnp.sum(jnp.where(valid, jnp.exp(scores - top[..., None]), 0.0), axis=-1)
        lse = top + jnp.log(total)
        prob = jnp.where(valid, jnp.exp(scores - lse[..., None]), 0.0)
        prob_r = prob.astype(jnp.bfloat16)
        accum = jnp.einsum(
            "gheqk,gkhd->gheqd", prob_r, value_part, preferred_element_type=jnp.float32
        )
        attn = accum.transpose(0, 3, 1, 2, 4).astype(jnp.bfloat16)
        delta = jnp.sum(
            attn.astype(jnp.float32) * group_grad.astype(jnp.float32), axis=-1
        ).transpose(0, 2, 3, 1)
        grad_t = group_grad.transpose(0, 2, 3, 1, 4)
        dprob = jnp.einsum(
            "gheqd,gkhd->gheqk", grad_t, value_part, preferred_element_type=jnp.float32
        )
        dscore = (prob * (dprob - delta[..., None])).astype(jnp.bfloat16)
        dq_accum = jnp.einsum(
            "gheqk,gkhd->gheqd", dscore, key_part, preferred_element_type=jnp.float32
        )
        dkey = (
            jnp.einsum("gheqk,gqhed->gkhd", dscore, group_q, preferred_element_type=jnp.float32)
            * scale
        )
        dvalue = jnp.einsum("gheqk,gheqd->gkhd", prob_r, grad_t, preferred_element_type=jnp.float32)
        piece = jnp.concatenate(
            [
                dkey.reshape(group_size, span_len, width_k),
                dvalue.reshape(group_size, span_len, width_k),
            ],
            axis=2,
        )
        target = (begin[:, None] + span_ladder[None, :]).reshape(-1)
        grads = grads.at[target].add(piece.reshape(group_size * span_len, 2 * width_k))
        dq_rot = (
            (dq_accum * scale).transpose(0, 3, 1, 2, 4).reshape(group_size * block_len, heads, HEAD)
        )
        group_rel = (group_pos - group_start).reshape(-1)
        dq_pre = (
            rotate(dq_rot, group_rel, -1.0)
            .astype(jnp.bfloat16)
            .reshape(group_size, block_len, width_q)
        )
        attn_own = attn_own.at[members].set(attn.reshape(group_size, block_len, width_q))
        qgrad_own = qgrad_own.at[members].set(dq_pre)
        lse_own = lse_own.at[members].set(
            lse.transpose(0, 3, 1, 2).reshape(group_size, block_len, heads)
        )
        return (attn_own, qgrad_own, lse_own, grads)

    start_carry = (
        jnp.zeros((ctx_size, block_len, width_q), jnp.bfloat16),
        jnp.zeros((ctx_size, block_len, width_q), jnp.bfloat16),
        jnp.zeros((ctx_size, block_len, heads), jnp.float32),
        jnp.zeros((WIN + seq_len, 2 * width_k), jnp.float32),
    )
    attn_own, qgrad_own, lse_own, grads = lax.fori_loop(0, group_count, run_group, start_carry)
    back_attn, back_qgrad = (
        lax.all_to_all(attn_own, "ctx", split_axis=0, concat_axis=0, tiled=True),
        lax.all_to_all(qgrad_own, "ctx", split_axis=0, concat_axis=0, tiled=True),
    )
    attn_home = back_attn[own_row].reshape(tok_rows, width_q)
    qgrad_home = back_qgrad[own_row].reshape(tok_rows, width_q)
    grads_part = grads[WIN:].astype(jnp.bfloat16)
    summed = lax.psum_scatter(grads_part, "ctx", scatter_dimension=0, tiled=True).astype(
        jnp.float32
    )
    kgrad_home = (
        rotate(summed[:, :width_k].reshape(tok_rows, KV_HEADS, HEAD), home_rel, -1.0)
        .astype(jnp.bfloat16)
        .reshape(tok_rows, width_k)
    )
    vgrad_home = summed[:, width_k:].astype(jnp.bfloat16)
    partial_value = lax.dot_general(
        attn_home, out_grad[0], (((0,), (0,)), ((), ())), preferred_element_type=jnp.float32
    )
    wgrad = lax.psum_scatter(partial_value, ("dp", "ctx"), scatter_dimension=1, tiled=True)
    return (
        attn_home[None],
        qgrad_home[None],
        kgrad_home[None],
        vgrad_home[None],
        wgrad,
        lse_own.reshape(1, 1, tok_rows, heads),
    )


def solution(mesh):
    in_specs = (
        P("dp", "ctx", None),
        P("dp", "ctx", None),
        P("dp", "ctx", None),
        P("dp", None),
        P("dp", None),
        P(),
        P("dp", "ctx", None),
    )
    out_specs = (
        P("dp", "ctx", None),
        P("dp", "ctx", None),
        P("dp", "ctx", None),
        P("dp", "ctx", None),
        P(None, ("dp", "ctx")),
        P("dp", "ctx", None, None),
    )
    return jax.shard_map(
        on_device, mesh=mesh, in_specs=in_specs, out_specs=out_specs, check_vma=False
    )
```

profile of v0, /device:TPU:0, one launch (start us, length us, event | category | flops | bytes accessed | tf_op | source)
XLA Modules:
  0.0 788.8 jit_solution(15850903850437223291)
XLA Ops:
  22.3 7.3 all-to-all-start.1
  31.0 18.7 %all-to-all-done.1 = bf16[8,64,512]{2,1,0:T(8,128)(2,1)S(1)} async-done(((bf16[8,64,512]{2,1,0:T(8,128)(2,1)}), bf16[8,64,512]{2,1,0:T(8,128)(2,1)S(1)}, u32[]{:S(2)}, u32[]{:S(2)}) %all-to-all-start.1) | async-done | bytes 524320 | tf_op jit(solution)/shard_map/all_to_all | solution.py:70
  54.6 27.1 %all-to-all-done = bf16[8,64,512]{2,1,0:T(8,128)(2,1)S(1)} async-done(((bf16[8,64,512]{2,1,0:T(8,128)(2,1)}), bf16[8,64,512]{2,1,0:T(8,128)(2,1)S(1)}, u32[]{:S(2)}, u32[]{:S(2)}) %all-to-all-start) | async-done | bytes 524320 | tf_op jit(solution)/shard_map/all_to_all | solution.py:69
  93.0 422.9 %while.31 = (s32[]{:T(128)}, bf16[8,64,512]{2,1,0:T(8,128)(2,1)}, bf16[8,64,512]{2,1,0:T(8,128)(2,1)}, f32[8,64,4]{1,2,0:T(4,128)S(1)}, f32[8192,256]{1,0:T(8,12...) while((s32[]{:T(128)}, bf16[8,64,512]{2,1,0:T(8,128)(2,1)}, ...), condition=%wide.region_13.14_spmd.clone.clone.clone, body=%wide.region_5.13_spmd.clone.clone.clone.sunk | while | flops 3316729344 | bytes 165945488 | solution.py:167
  94.3 7.2 while.32
  129.9 8.0 %fusion.115 = f32[2,128,4160,1]{1,2,3,0:T(8,128)} fusion(f32[2,1,4,64,4160]{4,3,2,0,1:T(8,128)} %copy-done.2, f32[2,4,64]{2,1,0:T(4,128)S(1)} %bitcast.229, pred[2,64,4160]{2,1,0:T(8,128)(4,1)S(1)} %compare_and_fusion.2, bf16[2,64,4,128]{3,1,2,0:T(8,128)(2,1)S(1)} %gather_fusion), kind=kOutput, calls=%fused_computation.46.clone.1 | convolution fusion | flops 551649280 | bytes 13445120 | tf_op jit(solution)/shard_map/while/body/eval_jaxpr/gheqk,gheqd->gkhd/dot_general | solution.py:135
  138.0 6.0 fusion.116
  143.9 54.8 %scatter_custom_fusion.22 = f32[8192,256]{1,0:T(8,128)} fusion(f32[8192,256]{1,0:T(8,128)} %get-tuple-element.666, s32[8320]{0:T(1024)S(1)} %fusion.114, f32[8320,128]{1,0:T(8,128)} %bitcast.223, f32[]{:T(128)} %constant.169.clone.5..sunk, f32[8320,128]{1,0:T(8,128)} %bitcast.224), kind=kCustom, calls=%fused_computation.22.clone.1 | custom fusion | flops 4259840 | bytes 16908800 | tf_op jit(solution)/shard_map/while/body/eval_jaxpr/scatter-add | solution.py:144
  200.1 7.2 while.32
  235.7 8.0 %fusion.115 = f32[2,128,4160,1]{1,2,3,0:T(8,128)} fusion(f32[2,1,4,64,4160]{4,3,2,0,1:T(8,128)} %copy-done.2, f32[2,4,64]{2,1,0:T(4,128)S(1)} %bitcast.229, pred[2,64,4160]{2,1,0:T(8,128)(4,1)S(1)} %compare_and_fusion.2, bf16[2,64,4,128]{3,1,2,0:T(8,128)(2,1)S(1)} %gather_fusion), kind=kOutput, calls=%fused_computation.46.clone.1 | convolution fusion | flops 551649280 | bytes 13445120 | tf_op jit(solution)/shard_map/while/body/eval_jaxpr/gheqk,gheqd->gkhd/dot_general | solution.py:135
  243.7 6.0 fusion.116
  249.7 54.8 %scatter_custom_fusion.22 = f32[8192,256]{1,0:T(8,128)} fusion(f32[8192,256]{1,0:T(8,128)} %get-tuple-element.666, s32[8320]{0:T(1024)S(1)} %fusion.114, f32[8320,128]{1,0:T(8,128)} %bitcast.223, f32[]{:T(128)} %constant.169.clone.5..sunk, f32[8320,128]{1,0:T(8,128)} %bitcast.224), kind=kCustom, calls=%fused_computation.22.clone.1 | custom fusion | flops 4259840 | bytes 16908800 | tf_op jit(solution)/shard_map/while/body/eval_jaxpr/scatter-add | solution.py:144
  305.8 7.2 while.32
  341.4 8.0 %fusion.115 = f32[2,128,4160,1]{1,2,3,0:T(8,128)} fusion(f32[2,1,4,64,4160]{4,3,2,0,1:T(8,128)} %copy-done.2, f32[2,4,64]{2,1,0:T(4,128)S(1)} %bitcast.229, pred[2,64,4160]{2,1,0:T(8,128)(4,1)S(1)} %compare_and_fusion.2, bf16[2,64,4,128]{3,1,2,0:T(8,128)(2,1)S(1)} %gather_fusion), kind=kOutput, calls=%fused_computation.46.clone.1 | convolution fusion | flops 551649280 | bytes 13445120 | tf_op jit(solution)/shard_map/while/body/eval_jaxpr/gheqk,gheqd->gkhd/dot_general | solution.py:135
  349.4 6.0 fusion.116
  355.4 54.8 %scatter_custom_fusion.22 = f32[8192,256]{1,0:T(8,128)} fusion(f32[8192,256]{1,0:T(8,128)} %get-tuple-element.666, s32[8320]{0:T(1024)S(1)} %fusion.114, f32[8320,128]{1,0:T(8,128)} %bitcast.223, f32[]{:T(128)} %constant.169.clone.5..sunk, f32[8320,128]{1,0:T(8,128)} %bitcast.224), kind=kCustom, calls=%fused_computation.22.clone.1 | custom fusion | flops 4259840 | bytes 16908800 | tf_op jit(solution)/shard_map/while/body/eval_jaxpr/scatter-add | solution.py:144
  411.5 7.2 while.32
  447.1 8.0 %fusion.115 = f32[2,128,4160,1]{1,2,3,0:T(8,128)} fusion(f32[2,1,4,64,4160]{4,3,2,0,1:T(8,128)} %copy-done.2, f32[2,4,64]{2,1,0:T(4,128)S(1)} %bitcast.229, pred[2,64,4160]{2,1,0:T(8,128)(4,1)S(1)} %compare_and_fusion.2, bf16[2,64,4,128]{3,1,2,0:T(8,128)(2,1)S(1)} %gather_fusion), kind=kOutput, calls=%fused_computation.46.clone.1 | convolution fusion | flops 551649280 | bytes 13445120 | tf_op jit(solution)/shard_map/while/body/eval_jaxpr/gheqk,gheqd->gkhd/dot_general | solution.py:135
  461.1 54.8 %scatter_custom_fusion.22 = f32[8192,256]{1,0:T(8,128)} fusion(f32[8192,256]{1,0:T(8,128)} %get-tuple-element.666, s32[8320]{0:T(1024)S(1)} %fusion.114, f32[8320,128]{1,0:T(8,128)} %bitcast.223, f32[]{:T(128)} %constant.169.clone.5..sunk, f32[8320,128]{1,0:T(8,128)} %bitcast.224), kind=kCustom, calls=%fused_computation.22.clone.1 | custom fusion | flops 4259840 | bytes 16908800 | tf_op jit(solution)/shard_map/while/body/eval_jaxpr/scatter-add | solution.py:144
  523.9 24.1 %all-to-all-done.2 = bf16[8,64,512]{2,1,0:T(8,128)(2,1)S(1)} async-done(((bf16[8,64,512]{2,1,0:T(8,128)(2,1)}), bf16[8,64,512]{2,1,0:T(8,128)(2,1)S(1)}, u32[]{:S(2)}, u32[]{:S(2)}) %all-to-all-start.2) | async-done | bytes 524320 | tf_op jit(solution)/shard_map/all_to_all | solution.py:169
  548.6 8.0 %fusion.47 = f32[512,4096]{1,0:T(8,128)} fusion(bf16[512,512]{1,0:T(8,128)(2,1)S(1)} %bitcast.236, bf16[1,512,4096]{2,1,0:T(8,128)(2,1)} %param.15), kind=kOutput, calls=%fused_computation.75 | convolution fusion | flops 2147483648 | bytes 13107200 | tf_op jit(solution)/shard_map/dot_general | solution.py:184
  560.9 13.2 %all-to-all-done.3 = bf16[8,64,512]{2,1,0:T(8,128)(2,1)S(1)} async-done(((bf16[8,64,512]{2,1,0:T(8,128)(2,1)}), bf16[8,64,512]{2,1,0:T(8,128)(2,1)S(1)}, u32[]{:S(2)}, u32[]{:S(2)}) %all-to-all-start.3) | async-done | bytes 524320 | tf_op jit(solution)/shard_map/all_to_all | solution.py:170
  575.5 20.3 %reduce-scatter.3.cloned.1.call-done = bf16[512,256]{1,0:T(8,128)(2,1)} async-done(((bf16[4096,256]{1,0:T(8,128)(2,1)}), bf16[512,256]{1,0:T(8,128)(2,1)}) %reduce-scatter.3.cloned.1.call-update) | async-done | bytes 262160 | tf_op jit(solution)/shard_map/reduce_scatter | solution.py:175
  599.4 182.8 %reduce-scatter.5.cloned.1.call-done = f32[512,128]{1,0:T(8,128)} async-done(((f32[512,4096]{1,0:T(8,128)}), f32[512,128]{1,0:T(8,128)}) %reduce-scatter.5.cloned.1.call-update) | async-done | bytes 262160 | tf_op jit(solution)/shard_map/reduce_scatter | solution.py:187
  (276 shorter events, 203.5 us)
Async XLA Ops:
  7.2 22.5 %copy-start = (bf16[1,512,512]{2,1,0:T(8,128)(2,1)S(1)}, bf16[1,512,512]{2,1,0:T(8,128)(2,1)}, u32[]{:S(2)}) copy-start(bf16[1,512,512]{2,1,0:T(8,128)(2,1)} %param.9) | copy-start | bytes 1572868
  7.2 76.4 %all-gather.2.cloned.1.call-start = ((), (), s32[]{:S(2)}) async-start(), calls=%async_computation.6 | async-start | bytes 2359296 | tf_op jit(solution)/shard_map/all_gather | solution.py:57
  7.2 46.2 %copy-start.8 = (f32[64]{0:T(128)}, f32[64]{0:T(128)S(1)}, u32[]{:S(2)}) copy-start(f32[64]{0:T(128)S(1)} %multiply_power_fusion.1) | copy-start | bytes 772
  9.2 6.0 copy-start.7
  22.3 27.4 %all-to-all-start.1 = ((bf16[8,64,512]{2,1,0:T(8,128)(2,1)}), bf16[8,64,512]{2,1,0:T(8,128)(2,1)S(1)}, u32[]{:S(2)}, u32[]{:S(2)}) async-start(bf16[8,64,512]{2,1,0:T(8,128)(2,1)} %gather_fusion.6), calls=%async_computation.1 | async-start | bytes 1048576 | tf_op jit(solution)/shard_map/all_to_all | solution.py:70
  49.8 31.9 %all-to-all-start = ((bf16[8,64,512]{2,1,0:T(8,128)(2,1)}), bf16[8,64,512]{2,1,0:T(8,128)(2,1)S(1)}, u32[]{:S(2)}, u32[]{:S(2)}) async-start(bf16[8,64,512]{2,1,0:T(8,128)(2,1)} %gather_fusion.5), calls=%async_computation | async-start | bytes 1048576 | tf_op jit(solution)/shard_map/all_to_all | solution.py:69
  53.3 542.5 %reduce-scatter.3.cloned.1.call-start = ((), (), s32[]{:S(2)}) async-start(), calls=%async_computation.7 | async-start | bytes 2359296 | tf_op jit(solution)/shard_map/reduce_scatter | solution.py:175
  103.5 7.8 slice-start
  104.1 7.1 slice-start.1
  107.9 3.3 copy-start.2
  209.2 7.8 slice-start
  209.8 7.1 slice-start.1
  213.6 3.3 copy-start.2
  314.9 7.8 slice-start
  315.5 7.1 slice-start.1
  420.6 7.8 slice-start
  421.3 7.1 slice-start.1
  519.6 28.4 %all-to-all-start.2 = ((bf16[8,64,512]{2,1,0:T(8,128)(2,1)}), bf16[8,64,512]{2,1,0:T(8,128)(2,1)S(1)}, u32[]{:S(2)}, u32[]{:S(2)}) async-start(bf16[8,64,512]{2,1,0:T(8,128)(2,1)} %get-tuple-element.331), calls=%async_computation.2 | async-start | bytes 1048576 | tf_op jit(solution)/shard_map/all_to_all | solution.py:169
  523.1 259.1 %reduce-scatter.5.cloned.1.call-start = ((), (), s32[]{:S(2)}) async-start(), calls=%async_computation.8 | async-start | bytes 8650752 | tf_op jit(solution)/shard_map/reduce_scatter | solution.py:187
  548.6 8.0 %copy-start.4 = (bf16[8,64,512]{2,1,0:T(8,128)(2,1)}, bf16[8,64,512]{2,1,0:T(8,128)(2,1)S(1)}, u32[]{:S(2)}) copy-start(bf16[8,64,512]{2,1,0:T(8,128)(2,1)S(1)} %gather_fusion.7) | copy-start | bytes 1572868
  556.6 225.7 %copy-start.1 = (bf16[1,512,512]{2,1,0:T(8,128)(2,1)S(1)}, bf16[1,512,512]{2,1,0:T(8,128)(2,1)}, u32[]{:S(2)}) copy-start(bf16[1,512,512]{2,1,0:T(8,128)(2,1)} %param.9) | copy-start | bytes 1572868
  556.6 40.9 %copy-start.6 = (f32[512]{0:T(512)S(1)}, f32[512]{0:T(512)}, u32[]{:S(2)}) copy-start(f32[512]{0:T(512)} %copy-done.5) | copy-start | bytes 6148
  556.6 40.9 %copy-start.9 = (f32[64]{0:T(128)S(1)}, f32[64]{0:T(128)}, u32[]{:S(2)}) copy-start(f32[64]{0:T(128)} %copy-done.8) | copy-start | bytes 772
  556.6 17.6 %all-to-all-start.3 = ((bf16[8,64,512]{2,1,0:T(8,128)(2,1)}), bf16[8,64,512]{2,1,0:T(8,128)(2,1)S(1)}, u32[]{:S(2)}, u32[]{:S(2)}) async-start(bf16[8,64,512]{2,1,0:T(8,128)(2,1)} %get-tuple-element.332), calls=%async_computation.3 | async-start | bytes 1048576 | tf_op jit(solution)/shard_map/all_to_all | solution.py:170
  (7 other events, 15.8 us)
Sparse Core Ops, SparseCore 0:
  15.1 68.0 all-gather.1
  519.7 76.0 reduce-scatter.2
  598.7 183.5 reduce-scatter.4
where the time goes:
time: 791 us; the launch traced here: 789 us
  waiting for transfers between devices  286 us (36%)
  other arithmetic  247 us (31%)
  matrix products  127 us (16%)
  local copies, waits for them, and re-layouts  95.1 us (12%)
  starting transfers between devices  18.1 us (2%)
  between operations  14 us (2%)
    scatter-add x4, other arithmetic, run_group(): grads.at[target].add(piece.reshape(group_size * span_len, 2 * width_k))  219 us
    reduce_scatter x1, waiting for transfers between devices, on_device(): lax.psum_scatter(partial_value, ('dp', 'ctx'), scatter_dimension=1, tiled...  183 us
    dot_general x4, matrix products, run_group(): jnp.einsum('gheqk,gheqd->gkhd', prob_r, grad_t, preferred_element_type=jn...  32.1 us
    gather x16, local copies, waits for them, and re-layouts  28.6 us
    all_to_all x1, waiting for transfers between devices, on_device(): lax.all_to_all(send_q, 'ctx', split_axis=0, concat_axis=0, tiled=True)  27.1 us
    all_to_all x1, waiting for transfers between devices, on_device(): lax.all_to_all(attn_own, 'ctx', split_axis=0, concat_axis=0, tiled=True)  24.1 us
    dot_general x4, matrix products, run_group(): jnp.einsum('gheqk,gqhed->gkhd', dscore, group_q, preferred_element_type=j...  23.9 us
    dot_general x4, matrix products, run_group(): jnp.einsum('gheqd,gkhd->gheqk', grad_t, value_part, preferred_element_typ...  22.3 us
  transfers between devices with their start and end apart: 7, of which 6 were waited for; matrix products, arithmetic and copies ran while one was open for 3% of the time, Pallas kernels for 0%

commit v1 on v0

v1 whole, which is shorter than its diff:
```python
import functools
import math

import numpy as np

import jax
import jax.numpy as jnp
from jax import lax
from jax.experimental import pallas as pl
from jax.experimental.pallas import tpu as pltpu
from jax.sharding import PartitionSpec as P

HEAD = 128
WIN = 4096
NEG = -1e30
LOG2E = math.log2(math.e)
LN2 = math.log(2.0)
SCALE = 1.0 / math.sqrt(HEAD)
VMEM_LIMIT = 56 * 1024 * 1024
F32 = jnp.float32
BF16 = jnp.bfloat16


def doc_starts(lens_ref, pos):
    begin = jnp.int32(0)
    found = jnp.zeros_like(pos)
    for d in range(lens_ref.shape[1]):
        found = jnp.where(pos >= begin, begin, found)
        begin = begin + lens_ref[0, d]
    return found


def sincos(angle):
    turns = jnp.floor(angle * (2.0 / math.pi) + 0.5)
    rest = angle - turns * 1.5703125
    rest = rest - turns * 4.83751296997070312e-4
    rest = rest - turns * 7.54978995489188216e-8
    square = rest * rest
    sine = rest + rest * square * (
        -1.6666654611e-1 + square * (8.3321608736e-3 + square * -1.9515295891e-4)
    )
    cosine = (
        1.0
        - 0.5 * square
        + square
        * square
        * (4.166664568298827e-2 + square * (-1.388731625493765e-3 + square * 2.443315711809948e-5))
    )
    quarter = turns.astype(jnp.int32) & 3
    odd = (quarter & 1) == 1
    out_sin = jnp.where(odd, cosine, sine)
    out_cos = jnp.where(odd, sine, cosine)
    out_sin = jnp.where(quarter >= 2, -out_sin, out_sin)
    out_cos = jnp.where((quarter == 1) | (quarter == 2), -out_cos, out_cos)
    return out_sin, out_cos


def prep_kernel(meta_ref, lens_ref, freq_ref, q_ref, k_ref, qrot_ref, krot_ref, cos_ref, sin_ref):
    rows = q_ref.shape[0]
    pos = meta_ref[0] + lax.broadcasted_iota(jnp.int32, (rows, HEAD), 0)
    rel = pos - doc_starts(lens_ref, pos)
    sine, cosine = sincos(rel.astype(F32) * freq_ref[...])
    lane = lax.broadcasted_iota(jnp.int32, (rows, HEAD), 1)
    sine = jnp.where(lane < HEAD // 2, -sine, sine)
    cos_ref[...] = cosine
    sin_ref[...] = sine
    k = k_ref[...].astype(F32)
    krot_ref[...] = (k * cosine + pltpu.roll(k, HEAD // 2, 1) * sine).astype(BF16)
    for h in range(q_ref.shape[1] // HEAD):
        q = q_ref[:, h * HEAD : (h + 1) * HEAD].astype(F32)
        out = q * cosine + pltpu.roll(q, HEAD // 2, 1) * sine
        qrot_ref[:, h * HEAD : (h + 1) * HEAD] = out.astype(BF16)


def load_slots(meta_ref, refs, scratch, sem, rows):
    for start in (True, False):
        for i, ref in enumerate(refs):
            slot = meta_ref[2 + i]

            @pl.when(slot >= 0)
            def _():
                at = pl.multiple_of(slot * rows, rows)
                copy = pltpu.make_async_copy(ref, scratch.at[pl.ds(at, rows)], sem.at[i])
                if start:
                    copy.start()
                else:
                    copy.wait()


def key_range(meta_ref, lens_ref, first, qb, kb, slots_base):
    low = jnp.maximum(doc_starts(lens_ref, first), first - WIN + 1)
    lo_blk = jnp.maximum(low - slots_base, 0) // kb
    hi_blk = (first + qb - 1 - slots_base) // kb + 1
    return lo_blk, hi_blk


def fwd_kernel(n_refs, meta_ref, lens_ref, owner_ref, q_ref, *rest):
    k_refs, v_refs = rest[:n_refs], rest[n_refs : 2 * n_refs]
    o_ref, lse_ref, send_ref, s_scr, k_scr, v_scr, sem_k, sem_v = rest[2 * n_refs :]
    step = pl.program_id(0)
    qb, width = q_ref.shape
    heads = width // HEAD
    rows = heads * qb
    tok = k_refs[0].shape[0]
    kb = s_scr.shape[2]

    @pl.when(step == 0)
    def _():
        load_slots(meta_ref, k_refs, k_scr, sem_k, tok)
        load_slots(meta_ref, v_refs, v_scr, sem_v, tok)

    home = meta_ref[0]
    base = home - (k_scr.shape[0] - tok)
    first = home + step * qb
    q = jnp.concatenate([q_ref[:, h * HEAD : (h + 1) * HEAD] for h in range(heads)], axis=0)
    pos = first + lax.broadcasted_iota(jnp.int32, (qb, 1), 0)
    low = jnp.maximum(doc_starts(lens_ref, pos), pos - WIN + 1)
    pos_rows = jnp.concatenate([pos] * heads, axis=0)
    low_rows = jnp.concatenate([low] * heads, axis=0)
    lo_blk, hi_blk = key_range(meta_ref, lens_ref, first, qb, kb, base)

    def score(j, top):
        at = pl.multiple_of(j * kb, kb)
        k = k_scr[pl.ds(at, kb), :]
        s = lax.dot_general(q, k, (((1,), (1,)), ((), ())), preferred_element_type=F32)
        key = base + at + lax.broadcasted_iota(jnp.int32, (1, kb), 1)
        s = jnp.where((key >= low_rows) & (key <= pos_rows), s * (SCALE * LOG2E), NEG)
        s_scr[j] = s
        for c in range(kb // 128):
            top = jnp.maximum(top, s[:, c * 128 : (c + 1) * 128])
        return top

    top = lax.fori_loop(lo_blk, hi_blk, score, jnp.full((rows, 128), NEG, F32))
    top = jnp.max(top, axis=1, keepdims=True)

    def weigh(j, carry):
        total, acc = carry
        at = pl.multiple_of(j * kb, kb)
        p = jnp.exp2(s_scr[j] - top)
        for c in range(kb // 128):
            total = total + p[:, c * 128 : (c + 1) * 128]
        acc = acc + lax.dot_general(
            p.astype(BF16), v_scr[pl.ds(at, kb), :], (((1,), (0,)), ((), ())),
            preferred_element_type=F32,
        )
        return total, acc

    zero = jnp.zeros((rows, 128), F32)
    total, acc = lax.fori_loop(lo_blk, hi_blk, weigh, (zero, zero))
    total = jnp.sum(total, axis=1, keepdims=True)
    out = (acc / total).astype(BF16)
    lse = (top + jnp.log2(total)) * LN2
    for h in range(heads):
        o_ref[:, h * HEAD : (h + 1) * HEAD] = out[h * qb : (h + 1) * qb, :]
        wide = jnp.broadcast_to(lse[h * qb : (h + 1) * qb, :], (qb, 128))
        lse_ref[h : h + 1, :] = jnp.transpose(wide)[:1, :]
    block_len = send_ref.shape[2]
    for b in range(qb // block_len):
        to = owner_ref[meta_ref[1] + step * (qb // block_len) + b]
        send_ref[to] = lse_ref[:, b * block_len : (b + 1) * block_len]


def bwd_kernel(n_refs, kb, meta_ref, lens_ref, q_ref, dy_ref, o_ref, lse_ref, cos_ref, sin_ref, *rest):
    k_refs, v_refs = rest[:n_refs], rest[n_refs : 2 * n_refs]
    dq_ref, far_ref, own_ref, k_scr, v_scr, dk_scr, dv_scr, sem_k, sem_v = rest[2 * n_refs :]
    step = pl.program_id(0)
    qb, width = q_ref.shape
    heads = width // HEAD
    rows = heads * qb
    tok = k_refs[0].shape[0]

    @pl.when(step == 0)
    def _():
        load_slots(meta_ref, k_refs, k_scr, sem_k, tok)
        load_slots(meta_ref, v_refs, v_scr, sem_v, tok)
        dk_scr[...] = jnp.zeros_like(dk_scr)
        dv_scr[...] = jnp.zeros_like(dv_scr)

    home = meta_ref[0]
    base = home - (k_scr.shape[0] - tok)
    first = home + step * qb

    def stack(ref):
        return jnp.concatenate([ref[:, h * HEAD : (h + 1) * HEAD] for h in range(heads)], axis=0)

    q, dy = stack(q_ref), stack(dy_ref)
    prod = dy.astype(F32) * stack(o_ref).astype(F32)
    delta = jnp.concatenate(
        [
            jnp.sum(jnp.transpose(prod[h * qb : (h + 1) * qb, :]), axis=0, keepdims=True)
            for h in range(heads)
        ],
        axis=1,
    )
    lse = jnp.concatenate([lse_ref[h : h + 1, :] for h in range(heads)], axis=1) * LOG2E
    pos = first + lax.broadcasted_iota(jnp.int32, (1, qb), 1)
    low = jnp.maximum(doc_starts(lens_ref, pos), pos - WIN + 1)
    pos_rows = jnp.concatenate([pos] * heads, axis=1)
    low_rows = jnp.concatenate([low] * heads, axis=1)
    lo_blk, hi_blk = key_range(meta_ref, lens_ref, first, qb, kb, base)

    def visit(j, dq):
        at = pl.multiple_of(j * kb, kb)
        k = k_scr[pl.ds(at, kb), :]
        v = v_scr[pl.ds(at, kb), :]
        s = lax.dot_general(k, q, (((1,), (1,)), ((), ())), preferred_element_type=F32)
        dp = lax.dot_general(v, dy, (((1,), (1,)), ((), ())), preferred_element_type=F32)
        key = base + at + lax.broadcasted_iota(jnp.int32, (kb, 1), 0)
        s = jnp.where((key >= low_rows) & (key <= pos_rows), s * (SCALE * LOG2E) - lse, NEG)
        p = jnp.exp2(s)
        ds = (p * (dp - delta)).astype(BF16)
        dv_scr[pl.ds(at, kb), :] += lax.dot_general(
            p.astype(BF16), dy, (((1,), (0,)), ((), ())), preferred_element_type=F32
        )
        dk_scr[pl.ds(at, kb), :] += lax.dot_general(
            ds, q, (((1,), (0,)), ((), ())), preferred_element_type=F32
        )
        return dq + lax.dot_general(ds, k, (((0,), (0,)), ((), ())), preferred_element_type=F32)

    dq = lax.fori_loop(lo_blk, hi_blk, visit, jnp.zeros((rows, HEAD), F32)) * SCALE
    for h in range(heads):
        part = dq[h * qb : (h + 1) * qb, :]
        part = part * cos_ref[...] - pltpu.roll(part, HEAD // 2, 1) * sin_ref[...]
        dq_ref[:, h * HEAD : (h + 1) * HEAD] = part.astype(BF16)

    @pl.when(step == pl.num_programs(0) - 1)
    def _():
        for r in range(far_ref.shape[0]):
            far_ref[r, :, :HEAD] = dk_scr[r * tok : (r + 1) * tok, :].astype(BF16)
            far_ref[r, :, HEAD:] = dv_scr[r * tok : (r + 1) * tok, :].astype(BF16)
        own_ref[:, :HEAD] = dk_scr[far_ref.shape[0] * tok :, :]
        own_ref[:, HEAD:] = dv_scr[far_ref.shape[0] * tok :, :]


def wo_kernel(meta_ref, a_ref, g_ref, out_ref, at_scr):
    @pl.when(pl.program_id(0) == 0)
    def _():
        at_scr[...] = jnp.transpose(a_ref[...])

    col = out_ref.shape[3]
    res = jnp.dot(at_scr[...], g_ref[...], preferred_element_type=F32).astype(BF16)
    for j in range(out_ref.shape[1]):
        out_ref[0, j ^ meta_ref[1]] = res[:, j * col : (j + 1) * col]


def home_kernel(n_in, own_ref, cos_ref, sin_ref, *rest):
    ins, (dk_ref, dv_ref) = rest[:n_in], rest[n_in:]
    total = own_ref[...]
    for ref in ins:
        total = total + ref[...].astype(F32)
    dk = total[:, :HEAD] * SCALE
    dk = dk * cos_ref[...] - pltpu.roll(dk, HEAD // 2, 1) * sin_ref[...]
    dk_ref[...] = dk.astype(BF16)
    dv_ref[...] = total[:, HEAD:].astype(BF16)


SMEM_SPEC = pl.BlockSpec(memory_space=pltpu.SMEM)
VMEM_SPEC = pl.BlockSpec(memory_space=pltpu.VMEM)
ANY_SPEC = pl.BlockSpec(memory_space=pl.ANY)


def params():
    return pltpu.CompilerParams(
        dimension_semantics=("arbitrary",), vmem_limit_bytes=VMEM_LIMIT
    )


def on_device(queries, keys, values, doc_lengths, owner, out_weight, out_grad):
    n_ctx = lax.axis_size("ctx")
    n_dp = lax.axis_size("dp")
    dev = lax.axis_index("ctx").astype(jnp.int32)
    dp = lax.axis_index("dp").astype(jnp.int32)
    tok = queries.shape[1]
    width = queries.shape[2]
    heads = width // HEAD
    seq_len = tok * n_ctx
    block_len = tok // n_ctx
    d_model = out_grad.shape[2]
    reach = min(WIN, seq_len // 2)
    back = min(-(-reach // tok), n_ctx - 1)
    home_pos = dev * tok
    sds = jax.ShapeDtypeStruct

    half = HEAD // 2
    freq = (10000.0 ** (-2.0 * np.arange(half) / HEAD)).astype(np.float32)
    freq = jnp.asarray(np.concatenate([freq, freq])[None, :])

    def shift(x, pairs):
        return lax.ppermute(x, "ctx", pairs)

    paired = n_ctx == 8 and back == 4
    hop = [(i, i + 2) for i in range(n_ctx - 2)]
    hop_back = [(b, a) for a, b in hop]
    up = [(i, i + 1) for i in range(0, n_ctx, 2)]
    down = [(b, a) for a, b in up]
    swap = up + down
    odd = dev % 2

    def collect(x):
        if paired:
            a1 = shift(x, hop)
            e1 = shift(x, up)
            a2 = shift(a1, hop)
            s1 = shift(a1, swap)
            o3 = shift(a2, down)
            return [x, a1, e1, a2, s1, o3]
        return [x] + [
            shift(x, [(i, i + s) for i in range(n_ctx - s)]) for s in range(1, back + 1)
        ]

    if paired:
        skip = jnp.int32(-1)
        slots = [
            jnp.int32(4),
            jnp.int32(2),
            jnp.where(odd == 1, 3, skip),
            jnp.int32(0),
            jnp.where(odd == 1, 1, 3),
            jnp.where(odd == 1, skip, 1),
        ]
    else:
        slots = [jnp.int32(back - s) for s in range(back + 1)]
    meta = jnp.stack([home_pos, dev * n_ctx] + [jnp.asarray(s, jnp.int32) for s in slots])
    meta_wo = jnp.stack([dp, dev])

    v_blocks = collect(values[0])

    q_rot, k_rot, cos, sin = pl.pallas_call(
        prep_kernel,
        out_shape=(
            sds((tok, width), BF16),
            sds((tok, HEAD), BF16),
            sds((tok, HEAD), F32),
            sds((tok, HEAD), F32),
        ),
        in_specs=[SMEM_SPEC, SMEM_SPEC, VMEM_SPEC, VMEM_SPEC, VMEM_SPEC],
        out_specs=(VMEM_SPEC,) * 4,
        compiler_params=pltpu.CompilerParams(vmem_limit_bytes=VMEM_LIMIT),
        name="prep",
    )(meta, doc_lengths, freq, queries[0], keys[0])
    k_blocks = collect(k_rot)

    d_out = lax.dot_general(
        out_grad[0], out_weight, (((1,), (1,)), ((), ())), preferred_element_type=F32
    ).astype(BF16)

    n_refs = len(k_blocks)
    n_keys = (back + 1) * tok
    qb = 128
    kb = min(512, tok)
    tok_spec = pl.BlockSpec((qb, width), lambda i: (i, 0))
    lse_spec = pl.BlockSpec((heads, qb), lambda i: (0, i))
    table_spec = pl.BlockSpec((qb, HEAD), lambda i: (i, 0))
    kv_scratch = [pltpu.VMEM((n_keys, HEAD), BF16), pltpu.VMEM((n_keys, HEAD), BF16)]
    sems = [pltpu.SemaphoreType.DMA((n_refs,)), pltpu.SemaphoreType.DMA((n_refs,))]
    pair_flops = 2 * heads * tok * (tok + reach // 2) * HEAD
    attn, lse, lse_send = pl.pallas_call(
        functools.partial(fwd_kernel, n_refs),
        grid=(tok // qb,),
        out_shape=(
            sds((tok, width), BF16),
            sds((heads, tok), F32),
            sds((n_ctx, heads, block_len), F32),
        ),
        in_specs=[SMEM_SPEC, SMEM_SPEC, SMEM_SPEC, tok_spec] + [ANY_SPEC] * (2 * n_refs),
        out_specs=(tok_spec, lse_spec, pl.BlockSpec((n_ctx, heads, block_len), lambda i: (0, 0, 0))),
        scratch_shapes=[pltpu.VMEM((n_keys // kb, heads * qb, kb), F32)] + kv_scratch + sems,
        compiler_params=params(),
        cost_estimate=pl.CostEstimate(
            flops=4 * pair_flops, bytes_accessed=4 << 20, transcendentals=pair_flops // HEAD
        ),
        name="fwd",
    )(meta, doc_lengths, owner[0], q_rot, *k_blocks, *v_blocks)

    lse_recv = lax.all_to_all(lse_send, "ctx", split_axis=0, concat_axis=0, tiled=True)
    owner_lse = lse_recv.transpose(0, 2, 1).reshape(1, 1, tok, heads)

    col = d_model // (n_dp * n_ctx)
    bits_dp = n_dp.bit_length() - 1
    bits_ctx = n_ctx.bit_length() - 1

    def partial_wo(part, core, rows):
        return pl.pallas_call(
            wo_kernel,
            grid_spec=pltpu.PrefetchScalarGridSpec(
                num_scalar_prefetch=1,
                grid=(n_dp // 2,),
                in_specs=[
                    pl.BlockSpec((tok, rows), lambda i, m: (0, part)),
                    pl.BlockSpec((tok, n_ctx * col), lambda i, m: (0, (2 * i + core) ^ m[0])),
                ],
                out_specs=pl.BlockSpec((1, n_ctx, rows, col), lambda i, m: (i, 0, 0, 0)),
                scratch_shapes=[pltpu.VMEM((rows, tok), BF16)],
            ),
            out_shape=sds((n_dp // 2, n_ctx, rows, col), BF16),
            compiler_params=params(),
            cost_estimate=pl.CostEstimate(
                flops=tok * rows * d_model, bytes_accessed=6 << 20, transcendentals=0
            ),
            name="wo",
        )(meta_wo, attn, out_grad[0])

    def exchange(x, axis, bit, size):
        return lax.ppermute(x, axis, [(i, i ^ bit) for i in range(size)])

    n_parts = 2
    rows = width // n_parts
    reduced = []
    for part in range(n_parts):
        send = partial_wo(part, 1, rows)
        recv = exchange(send, "dp", 1, n_dp)
        keep = partial_wo(part, 0, rows)
        shape = (2,) * (bits_dp - 1 + bits_ctx) + (rows, col)
        pieces = (keep.reshape(shape), recv.reshape(shape))
        left = [("dp", b) for b in range(bits_dp - 1, 0, -1)]
        left += [("ctx", b) for b in range(bits_ctx - 1, -1, -1)]
        order = [("dp", b) for b in range(1, bits_dp)]
        if part == 0:
            order = order + [("ctx", b) for b in range(bits_ctx)]
        else:
            order = [("ctx", 0)] + order + [("ctx", b) for b in range(1, bits_ctx)]
        for axis, b in order:
            at = left.index((axis, b))
            left.pop(at)

            def pick(which):
                one, two = [lax.index_in_dim(x, which, at, keepdims=False) for x in pieces]
                return (one.astype(F32) + two.astype(F32)).astype(BF16)

            send = pick(1)
            recv = exchange(send, axis, 1 << b, n_dp if axis == "dp" else n_ctx)
            pieces = (pick(0), recv)
        reduced.append(pieces[0].astype(F32) + pieces[1].astype(F32))
    wgrad = jnp.concatenate(reduced, axis=0)

    q_grad, far, own = pl.pallas_call(
        functools.partial(bwd_kernel, n_refs, kb),
        grid=(tok // qb,),
        out_shape=(
            sds((tok, width), BF16),
            sds((back, tok, 2 * HEAD), BF16),
            sds((tok, 2 * HEAD), F32),
        ),
        in_specs=[SMEM_SPEC, SMEM_SPEC, tok_spec, tok_spec, tok_spec, lse_spec, table_spec, table_spec]
        + [ANY_SPEC] * (2 * n_refs),
        out_specs=(
            tok_spec,
            pl.BlockSpec((back, tok, 2 * HEAD), lambda i: (0, 0, 0)),
            pl.BlockSpec((tok, 2 * HEAD), lambda i: (0, 0)),
        ),
        scratch_shapes=kv_scratch
        + [pltpu.VMEM((n_keys, HEAD), F32), pltpu.VMEM((n_keys, HEAD), F32)]
        + sems,
        compiler_params=params(),
        cost_estimate=pl.CostEstimate(
            flops=8 * pair_flops, bytes_accessed=8 << 20, transcendentals=pair_flops // HEAD
        ),
        name="bwd",
    )(meta, doc_lengths, q_rot, d_out, attn, lse, cos, sin, *k_blocks, *v_blocks)

    def plus(*xs):
        return functools.reduce(jnp.add, [x.astype(F32) for x in xs]).astype(BF16)

    if paired:
        d4, d3, d2, d1 = far[0], far[1], far[2], far[3]
        sum4 = plus(d4, shift(d3, up))
        b2 = shift(sum4, hop_back)
        s1 = shift(jnp.where(odd == 1, d3, d1), swap)
        sum2 = plus(d2, b2, s1)
        arrived = [shift(sum2, hop_back), shift(d1, down)]
    else:
        arrived = [
            shift(far[back - s], [(i + s, i) for i in range(n_ctx - s)]) for s in range(1, back + 1)
        ]
    k_grad, v_grad = pl.pallas_call(
        functools.partial(home_kernel, len(arrived)),
        out_shape=(sds((tok, HEAD), BF16), sds((tok, HEAD), BF16)),
        in_specs=[VMEM_SPEC] * (3 + len(arrived)),
        out_specs=(VMEM_SPEC, VMEM_SPEC),
        compiler_params=pltpu.CompilerParams(vmem_limit_bytes=VMEM_LIMIT),
        name="home",
    )(own, cos, sin, *arrived)

    return (attn[None], q_grad[None], k_grad[None], v_grad[None], wgrad, owner_lse)


def solution(mesh):
    in_specs = (
        P("dp", "ctx", None),
        P("dp", "ctx", None),
        P("dp", "ctx", None),
        P("dp", None),
        P("dp", None),
        P(),
        P("dp", "ctx", None),
    )
    out_specs = (
        P("dp", "ctx", None),
        P("dp", "ctx", None),
        P("dp", "ctx", None),
        P("dp", "ctx", None),
        P(None, ("dp", "ctx")),
        P("dp", "ctx", None, None),
    )
    return jax.shard_map(
        on_device, mesh=mesh, in_specs=in_specs, out_specs=out_specs, check_vma=False
    )
```

time: 791 us -> 151 us (0.19)
  waiting for transfers between devices: 286 us -> 23.9 us
  other arithmetic: 247 us -> 5.48 us
  matrix products: 127 us -> 6.62 us
  local copies, waits for them, and re-layouts: 95.1 us -> 4.68 us
  Pallas kernels: 0 us -> 39.4 us
  starting transfers between devices: 18.1 us -> 49.1 us
  blocking collectives: 0 us -> 18.2 us
  between operations: 14 us -> 1.1 us
    scatter-add x4 -> x0, other arithmetic: 219 us -> none  [run_group(): grads.at[target].add(piece.reshape(group_size * span_len, 2 * width_k))]
    reduce_scatter x2 -> x0, waiting for transfers between devices: 203 us -> none  [the longest x1 183 us: on_device(): lax.psum_scatter(partial_value, ('dp', 'ctx'), scatter_dimension=1, tiled...]
    dot_general x25 -> x0, matrix products: 121 us -> none  [the longest x4 32.1 us: run_group(): jnp.einsum('gheqk,gheqd->gkhd', prob_r, grad_t, preferred_element_type=jn...]
    all_to_all x4 -> x0, waiting for transfers between devices: 83.1 us -> none  [the longest x1 27.1 us: on_device(): lax.all_to_all(send_q, 'ctx', split_axis=0, concat_axis=0, tiled=True)]
    ppermute x0 -> x25, starting transfers between devices: none -> 49.1 us  [the longest x15 38.7 us: shift(): return lax.ppermute(x, 'ctx', pairs)]
    gather x40 -> x0, local copies, waits for them, and re-layouts: 45.3 us -> none
    pallas_call x0 -> x8, Pallas kernels: none -> 39.4 us  [the longest x4 15.6 us: partial_wo(): pl.pallas_call(wo_kernel, grid_spec=pltpu.PrefetchScalarGridSpec(num_scal...]
    ppermute x0 -> x25, waiting for transfers between devices: none -> 23.9 us  [the longest x15 15.5 us: shift(): return lax.ppermute(x, 'ctx', pairs)]
  transfers between devices with their start and end apart: 7 -> 25, of which waited for: 6 -> 5; matrix products, arithmetic and copies ran while one was open for 3% -> 9% of each run, Pallas kernels for 0% -> 13%
where the time goes in v1:
time: 151 us; the launch traced here: 149 us
  starting transfers between devices  49.1 us (33%)
  Pallas kernels  39.4 us (26%)
  waiting for transfers between devices  23.9 us (16%)
  blocking collectives  18.2 us (12%)
  matrix products  6.62 us (4%)
  other arithmetic  5.48 us (4%)
  local copies, waits for them, and re-layouts  4.68 us (3%)
    ppermute x15, starting transfers between devices, shift(): return lax.ppermute(x, 'ctx', pairs)  38.7 us
    all_to_all x1, blocking collectives, on_device(): lax.all_to_all(lse_send, 'ctx', split_axis=0, concat_axis=0, tiled=True)  18.2 us
    pallas_call x4, Pallas kernels, partial_wo(): pl.pallas_call(wo_kernel, grid_spec=pltpu.PrefetchScalarGridSpec(num_scal...  15.6 us
    ppermute x15, waiting for transfers between devices, shift(): return lax.ppermute(x, 'ctx', pairs)  15.5 us
    ppermute x10, starting transfers between devices, exchange(): return lax.ppermute(x, axis, [(i, i ^ bit) for i in range(size)])  10.3 us
    pallas_call x1, Pallas kernels, on_device(): pl.pallas_call(functools.partial(bwd_kernel, n_refs, kb), grid=(tok // qb...  9.98 us
    pallas_call x1, Pallas kernels, on_device(): pl.pallas_call(functools.partial(fwd_kernel, n_refs), grid=(tok // qb,),...  8.95 us
    ppermute x10, waiting for transfers between devices, exchange(): return lax.ppermute(x, axis, [(i, i ^ bit) for i in range(size)])  8.39 us
  transfers between devices with their start and end apart: 25, of which 5 were waited for; matrix products, arithmetic and copies ran while one was open for 9% of the time, Pallas kernels for 13%

profile of v1, /device:TPU:0, one launch (start us, length us, event | category | flops | bytes accessed | tf_op | source)
XLA Modules:
  0.0 148.5 jit_solution(17023266212018895856)
XLA Ops:
  1.3 2.8 %prep.1 = (bf16[512,512]{1,0:T(8,128)(2,1)}, bf16[512,128]{1,0:T(8,128)(2,1)}, f32[512,128]{1,0:T(8,128)}, f32[512,128]{1,0:T(8,128)}) custom-call(s32[8]{0:T(128)} %stack.32.meta_ref, s32[1,8]{1,0:T(1,128)} %lens_ref.5, f32[1,128]{1,0:T(1,128)} %constant.38.clone.freq_ref, bf16[512,512]{1,0:T(8,128)(2,1)} %bitcast.133, bf16[512,128]{1,0:T(8,128)(2,1)} %bitcast.134), custom_call_target="tpu_custom_call" | custom-call | tf_op jit(solution)/shard_map/prep/pallas_call | solution.py:328
  4.0 5.0 %collective-permute-start = (bf16[512,128]{1,0:T(8,128)(2,1)}, bf16[512,128]{1,0:T(8,128)(2,1)S(1)}, u32[]{:S(2)}, u32[]{:S(2)}) collective-permute-start(bf16[512,128]{1,0:T(8,128)(2,1)} %get-tuple-element.19.rest_0_), channel_id=1, source_target_pairs={{0,2},{1,3},{2,4},{3,5},{4,6},{5,7},{8,10},{9,11},{10,12},{11,13},... | collective-permute-start | bytes 393224 | tf_op jit(solution)/shard_map/ppermute | solution.py:289
  9.0 3.5 %collective-permute-start.5 = (bf16[512,128]{1,0:T(8,128)(2,1)}, bf16[512,128]{1,0:T(8,128)(2,1)S(1)}, u32[]{:S(2)}, u32[]{:S(2)}) collective-permute-start(bf16[512,128]{1,0:T(8,128)(2,1)} %bitcast.136), channel_id=1, source_target_pairs={{0,2},{1,3},{2,4},{3,5},{4,6},{5,7},{8,10},{9,11},{10,12},{11,13},... | collective-permute-start | bytes 393224 | tf_op jit(solution)/shard_map/ppermute | solution.py:289
  12.5 3.4 %collective-permute-start.1 = (bf16[512,128]{1,0:T(8,128)(2,1)}, bf16[512,128]{1,0:T(8,128)(2,1)S(1)}, u32[]{:S(2)}, u32[]{:S(2)}) collective-permute-start(bf16[512,128]{1,0:T(8,128)(2,1)} %get-tuple-element.19.rest_0_), channel_id=1, source_target_pairs={{0,1},{2,3},{4,5},{6,7},{8,9},{10,11},{12,13},{14,15},{16,17},{18,... | collective-permute-start | bytes 393224 | tf_op jit(solution)/shard_map/ppermute | solution.py:289
  16.0 3.5 %collective-permute-start.2 = (bf16[512,128]{1,0:T(8,128)(2,1)S(1)}, bf16[512,128]{1,0:T(8,128)(2,1)S(1)}, u32[]{:S(2)}, u32[]{:S(2)}) collective-permute-start(bf16[512,128]{1,0:T(8,128)(2,1)S(1)} %collective-permute-done.rest_1_), channel_id=1, source_target_pairs={{0,2},{1,3},{2,4},{3,5},{4,6},{5,7},{8,10},{9,11},{10,12},{11,13},... | collective-permute-start | bytes 393224 | tf_op jit(solution)/shard_map/ppermute | solution.py:289
  19.5 1.9 %collective-permute-start.7 = (bf16[512,128]{1,0:T(8,128)(2,1)S(1)}, bf16[512,128]{1,0:T(8,128)(2,1)S(1)}, u32[]{:S(2)}, u32[]{:S(2)}) collective-permute-start(bf16[512,128]{1,0:T(8,128)(2,1)S(1)} %collective-permute-done.5.rest_7_), channel_id=1, source_target_pairs={{0,2},{1,3},{2,4},{3,5},{4,6},{5,7},{8,10},{9,11},{10,12},{11,13},... | collective-permute-start | bytes 393224 | tf_op jit(solution)/shard_map/ppermute | solution.py:289
  21.4 2.0 %collective-permute-start.6 = (bf16[512,128]{1,0:T(8,128)(2,1)}, bf16[512,128]{1,0:T(8,128)(2,1)S(1)}, u32[]{:S(2)}, u32[]{:S(2)}) collective-permute-start(bf16[512,128]{1,0:T(8,128)(2,1)} %bitcast.137), channel_id=1, source_target_pairs={{0,1},{2,3},{4,5},{6,7},{8,9},{10,11},{12,13},{14,15},{16,17},{18,... | collective-permute-start | bytes 393224 | tf_op jit(solution)/shard_map/ppermute | solution.py:289
  23.5 2.0 %collective-permute-start.8 = (bf16[512,128]{1,0:T(8,128)(2,1)S(1)}, bf16[512,128]{1,0:T(8,128)(2,1)S(1)}, u32[]{:S(2)}, u32[]{:S(2)}) collective-permute-start(bf16[512,128]{1,0:T(8,128)(2,1)S(1)} %collective-permute-done.5.rest_7_), channel_id=1, source_target_pairs={{0,1},{2,3},{4,5},{6,7},{1,0},{3,2},{5,4},{7,6},{8,9},{10,11},{12,... | collective-permute-start | bytes 393224 | tf_op jit(solution)/shard_map/ppermute | solution.py:289
  28.1 6.6 %convolution_convert_fusion.dy_ref = bf16[512,512]{1,0:T(8,128)(2,1)} fusion(bf16[512,4096]{1,0:T(8,128)(2,1)} %param.13, bf16[1,512,4096]{2,1,0:T(8,128)(2,1)} %param.14), kind=kOutput, calls=%fused_computation | convolution fusion | flops 2147745792 | bytes 8912896 | tf_op jit(solution)/shard_map/dot_general | solution.py:343
  36.2 9.0 %fwd.1 = (bf16[512,512]{1,0:T(8,128)(2,1)}, f32[4,512]{1,0:T(4,128)}, f32[8,4,64]{2,1,0:T(4,128)}) custom-call(s32[8]{0:T(128)} %stack.32.meta_ref, s32[1,8]{1,0:T(1,128)} %lens_ref.5, s32[64]{0:T(128)} %bitcast.142, bf16[512,512]{1,0:T(8,128)(2,1)} %get-tuple-element.18.q_ref, bf16[512,128]{1,0:T(8,128)(2,1)} %get-tuple-element.19.rest_0_, ...), custom_call_target="tpu_custom_call" | custom-call | flops 3221225472 | bytes 4194304 | tf_op jit(solution)/shard_map/fwd/pallas_call | solution.py:357
  45.1 3.8 %wo.7 = bf16[2,8,256,128]{3,2,1,0:T(8,128)(2,1)} custom-call(s32[2]{0:T(128)} %pad_add_fusion.meta_ref, bf16[512,512]{1,0:T(8,128)(2,1)} %get-tuple-element.20.o_ref.a_ref, bf16[512,4096]{1,0:T(8,128)(2,1)} %bitcast.122), custom_call_target="tpu_custom_call" | custom-call | flops 536870912 | bytes 6291456 | tf_op jit(solution)/shard_map/wo/pallas_call | solution.py:383
  49.0 4.0 %wo.5 = bf16[2,8,256,128]{3,2,1,0:T(8,128)(2,1)} custom-call(s32[2]{0:T(128)} %pad_add_fusion.meta_ref, bf16[512,512]{1,0:T(8,128)(2,1)} %get-tuple-element.20.o_ref.a_ref, bf16[512,4096]{1,0:T(8,128)(2,1)} %bitcast.123), custom_call_target="tpu_custom_call" | custom-call | flops 536870912 | bytes 6291456 | tf_op jit(solution)/shard_map/wo/pallas_call | solution.py:383
  53.5 10.0 %bwd.1 = (bf16[512,512]{1,0:T(8,128)(2,1)}, bf16[4,512,256]{2,1,0:T(8,128)(2,1)}, f32[512,256]{1,0:T(8,128)}) custom-call(s32[8]{0:T(128)} %stack.32.meta_ref, s32[1,8]{1,0:T(1,128)} %lens_ref.5, bf16[512,512]{1,0:T(8,128)(2,1)} %get-tuple-element.18.q_ref, bf16[512,512]{1,0:T(8,128)(2,1)} %convolution_convert_fusion.dy_ref, ...), custom_call_target="tpu_custom_call" | custom-call | flops 6442450944 | bytes 8388608 | tf_op jit(solution)/shard_map/bwd/pallas_call | solution.py:436
  64.5 10.9 %collective-permute-start.10 = (bf16[512,256]{1,0:T(8,128)(2,1)S(1)}, bf16[512,256]{1,0:T(8,128)(2,1)S(1)}, u32[]{:S(2)}, u32[]{:S(2)}) collective-permute-start(bf16[512,256]{1,0:T(8,128)(2,1)S(1)} %get-tuple-element.37), channel_id=1, source_target_pairs={{0,1},{2,3},{4,5},{6,7},{8,9},{10,11},{12,13},{14,15},{16,17},{18,... | collective-permute-start | bytes 786440 | tf_op jit(solution)/shard_map/ppermute | solution.py:289
  77.9 3.8 %wo.6 = bf16[2,8,256,128]{3,2,1,0:T(8,128)(2,1)} custom-call(s32[2]{0:T(128)} %pad_add_fusion.meta_ref, bf16[512,512]{1,0:T(8,128)(2,1)} %get-tuple-element.20.o_ref.a_ref, bf16[512,4096]{1,0:T(8,128)(2,1)} %bitcast.124), custom_call_target="tpu_custom_call" | custom-call | flops 536870912 | bytes 6291456 | tf_op jit(solution)/shard_map/wo/pallas_call | solution.py:383
  81.7 3.9 %wo.4 = bf16[2,8,256,128]{3,2,1,0:T(8,128)(2,1)} custom-call(s32[2]{0:T(128)} %pad_add_fusion.meta_ref, bf16[512,512]{1,0:T(8,128)(2,1)} %get-tuple-element.20.o_ref.a_ref, bf16[512,4096]{1,0:T(8,128)(2,1)} %bitcast.125), custom_call_target="tpu_custom_call" | custom-call | flops 536870912 | bytes 6291456 | tf_op jit(solution)/shard_map/wo/pallas_call | solution.py:383
  87.2 2.7 %collective-permute-start.21 = (bf16[2,2,2,256,128]{4,3,2,1,0:T(8,128)(2,1)S(1)}, bf16[2,2,2,256,128]{4,3,2,1,0:T(8,128)(2,1)S(1)}, u32[]{:S(2)}, u32[]{:S(2)}) collective-permute-start(bf16[2,2,2,256,128]{4,3,2,1,0:T(8,128)(2,1)S(1)} %fusion), channel_id=1, source_target_pairs={{0,1},{1,0},{2,3},{3,2},{4,5},{5,4},{6,7},{7,6},{8,9},{9,8},{10,11... | collective-permute-start | bytes 1572872 | tf_op jit(solution)/shard_map/ppermute | solution.py:404
  91.6 15.5 %collective-permute-done.11 = bf16[512,256]{1,0:T(8,128)(2,1)S(1)} collective-permute-done((bf16[512,256]{1,0:T(8,128)(2,1)S(1)}, bf16[512,256]{1,0:T(8,128)(2,1)S(1)}, u32[]{:S(2)}, u32[]{:S(2)}) %collective-permute-start.11) | collective-permute-done | bytes 262176 | tf_op jit(solution)/shard_map/ppermute | solution.py:289
  109.0 2.7 %collective-permute-start.17 = (bf16[2,2,256,128]{3,2,1,0:T(8,128)(2,1)S(1)}, bf16[2,2,256,128]{3,2,1,0:T(8,128)(2,1)S(1)}, u32[]{:S(2)}, u32[]{:S(2)}) collective-permute-start(bf16[2,2,256,128]{3,2,1,0:T(8,128)(2,1)S(1)} %get-tuple-element.33), channel_id=1, source_target_pairs={{0,1},{1,0},{2,3},{3,2},{4,5},{5,4},{6,7},{7,6},{8,9},{9,8},{10,11... | collective-permute-start | bytes 786440 | tf_op jit(solution)/shard_map/ppermute | solution.py:404
  111.8 18.2 %all_to_all.5 = f32[8,1,256]{2,1,0:T(1,128)S(1)} all-to-all(f32[8,1,256]{2,1,0:T(1,128)S(1)} %reshape.134), channel_id=1, replica_groups=mesh['dp'=4,'ctx'=8] {'ctx'}, dimensions={0} | all-to-all | bytes 16384 | tf_op jit(solution)/shard_map/all_to_all | solution.py:375
  132.8 2.2 %home.1 = (bf16[512,128]{1,0:T(8,128)(2,1)}, bf16[512,128]{1,0:T(8,128)(2,1)}) custom-call(f32[512,256]{1,0:T(8,128)} %get-tuple-element.25.own_ref, f32[512,128]{1,0:T(8,128)} %get-tuple-element.22.cos_ref, f32[512,128]{1,0:T(8,128)} %get-tuple-element.23.sin_ref, bf16[512,256]{1,0:T(8,128)(2,1)} %copy-done.4, bf16[512,256]{1,0:T(8,128)(2,1)} %copy-done.3), custom_call_target="tpu_custom_call" | custom-call | tf_op jit(solution)/shard_map/home/pallas_call | solution.py:475
  137.2 3.5 %collective-permute-done.23 = bf16[2,256,128]{2,1,0:T(8,128)(2,1)S(1)} collective-permute-done((bf16[2,256,128]{2,1,0:T(8,128)(2,1)S(1)}, bf16[2,256,128]{2,1,0:T(8,128)(2,1)S(1)}, u32[]{:S(2)}, u32[]{:S(2)}) %collective-permute-start.23) | collective-permute-done | bytes 131104 | tf_op jit(solution)/shard_map/ppermute | solution.py:404
  142.1 1.7 %collective-permute-start.19 = (bf16[256,128]{1,0:T(8,128)(2,1)S(1)}, bf16[256,128]{1,0:T(8,128)(2,1)S(1)}, u32[]{:S(2)}, u32[]{:S(2)}) collective-permute-start(bf16[256,128]{1,0:T(8,128)(2,1)S(1)} %fusion.17), channel_id=1, source_target_pairs={{0,4},{1,5},{2,6},{3,7},{4,0},{5,1},{6,2},{7,3},{8,12},{9,13},{10,... | collective-permute-start | bytes 196616 | tf_op jit(solution)/shard_map/ppermute | solution.py:404
  143.8 2.6 %collective-permute-done.24 = bf16[256,128]{1,0:T(8,128)(2,1)S(1)} collective-permute-done((bf16[256,128]{1,0:T(8,128)(2,1)S(1)}, bf16[256,128]{1,0:T(8,128)(2,1)S(1)}, u32[]{:S(2)}, u32[]{:S(2)}) %collective-permute-start.24) | collective-permute-done | bytes 65568 | tf_op jit(solution)/shard_map/ppermute | solution.py:404
  (93 shorter events, 22.4 us)
Async XLA Ops:
  4.0 11.9 %collective-permute-start = (bf16[512,128]{1,0:T(8,128)(2,1)}, bf16[512,128]{1,0:T(8,128)(2,1)S(1)}, u32[]{:S(2)}, u32[]{:S(2)}) collective-permute-start(bf16[512,128]{1,0:T(8,128)(2,1)} %get-tuple-element.19.rest_0_), channel_id=1, source_target_pairs={{0,2},{1,3},{2,4},{3,5},{4,6},{5,7},{8,10},{9,11},{10,12},{11,13},... | collective-permute-start | bytes 393224 | tf_op jit(solution)/shard_map/ppermute | solution.py:289
  9.0 10.5 %collective-permute-start.5 = (bf16[512,128]{1,0:T(8,128)(2,1)}, bf16[512,128]{1,0:T(8,128)(2,1)S(1)}, u32[]{:S(2)}, u32[]{:S(2)}) collective-permute-start(bf16[512,128]{1,0:T(8,128)(2,1)} %bitcast.136), channel_id=1, source_target_pairs={{0,2},{1,3},{2,4},{3,5},{4,6},{5,7},{8,10},{9,11},{10,12},{11,13},... | collective-permute-start | bytes 393224 | tf_op jit(solution)/shard_map/ppermute | solution.py:289
  12.5 11.0 %collective-permute-start.1 = (bf16[512,128]{1,0:T(8,128)(2,1)}, bf16[512,128]{1,0:T(8,128)(2,1)S(1)}, u32[]{:S(2)}, u32[]{:S(2)}) collective-permute-start(bf16[512,128]{1,0:T(8,128)(2,1)} %get-tuple-element.19.rest_0_), channel_id=1, source_target_pairs={{0,1},{2,3},{4,5},{6,7},{8,9},{10,11},{12,13},{14,15},{16,17},{18,... | collective-permute-start | bytes 393224 | tf_op jit(solution)/shard_map/ppermute | solution.py:289
  16.0 9.5 %collective-permute-start.2 = (bf16[512,128]{1,0:T(8,128)(2,1)S(1)}, bf16[512,128]{1,0:T(8,128)(2,1)S(1)}, u32[]{:S(2)}, u32[]{:S(2)}) collective-permute-start(bf16[512,128]{1,0:T(8,128)(2,1)S(1)} %collective-permute-done.rest_1_), channel_id=1, source_target_pairs={{0,2},{1,3},{2,4},{3,5},{4,6},{5,7},{8,10},{9,11},{10,12},{11,13},... | collective-permute-start | bytes 393224 | tf_op jit(solution)/shard_map/ppermute | solution.py:289
  19.5 7.3 %collective-permute-start.7 = (bf16[512,128]{1,0:T(8,128)(2,1)S(1)}, bf16[512,128]{1,0:T(8,128)(2,1)S(1)}, u32[]{:S(2)}, u32[]{:S(2)}) collective-permute-start(bf16[512,128]{1,0:T(8,128)(2,1)S(1)} %collective-permute-done.5.rest_7_), channel_id=1, source_target_pairs={{0,2},{1,3},{2,4},{3,5},{4,6},{5,7},{8,10},{9,11},{10,12},{11,13},... | collective-permute-start | bytes 393224 | tf_op jit(solution)/shard_map/ppermute | solution.py:289
  21.4 13.9 %collective-permute-start.6 = (bf16[512,128]{1,0:T(8,128)(2,1)}, bf16[512,128]{1,0:T(8,128)(2,1)S(1)}, u32[]{:S(2)}, u32[]{:S(2)}) collective-permute-start(bf16[512,128]{1,0:T(8,128)(2,1)} %bitcast.137), channel_id=1, source_target_pairs={{0,1},{2,3},{4,5},{6,7},{8,9},{10,11},{12,13},{14,15},{16,17},{18,... | collective-permute-start | bytes 393224 | tf_op jit(solution)/shard_map/ppermute | solution.py:289
  23.4 12.0 %collective-permute-start.3 = (bf16[512,128]{1,0:T(8,128)(2,1)S(1)}, bf16[512,128]{1,0:T(8,128)(2,1)S(1)}, u32[]{:S(2)}, u32[]{:S(2)}) collective-permute-start(bf16[512,128]{1,0:T(8,128)(2,1)S(1)} %collective-permute-done.rest_1_), channel_id=1, source_target_pairs={{0,1},{2,3},{4,5},{6,7},{1,0},{3,2},{5,4},{7,6},{8,9},{10,11},{12,... | collective-permute-start | bytes 393224 | tf_op jit(solution)/shard_map/ppermute | solution.py:289
  23.5 11.9 %collective-permute-start.8 = (bf16[512,128]{1,0:T(8,128)(2,1)S(1)}, bf16[512,128]{1,0:T(8,128)(2,1)S(1)}, u32[]{:S(2)}, u32[]{:S(2)}) collective-permute-start(bf16[512,128]{1,0:T(8,128)(2,1)S(1)} %collective-permute-done.5.rest_7_), channel_id=1, source_target_pairs={{0,1},{2,3},{4,5},{6,7},{1,0},{3,2},{5,4},{7,6},{8,9},{10,11},{12,... | collective-permute-start | bytes 393224 | tf_op jit(solution)/shard_map/ppermute | solution.py:289
  25.5 9.9 %collective-permute-start.4 = (bf16[512,128]{1,0:T(8,128)(2,1)S(1)}, bf16[512,128]{1,0:T(8,128)(2,1)S(1)}, u32[]{:S(2)}, u32[]{:S(2)}) collective-permute-start(bf16[512,128]{1,0:T(8,128)(2,1)S(1)} %collective-permute-done.2.rest_3_), channel_id=1, source_target_pairs={{1,0},{3,2},{5,4},{7,6},{9,8},{11,10},{13,12},{15,14},{17,16},{19,... | collective-permute-start | bytes 393224 | tf_op jit(solution)/shard_map/ppermute | solution.py:289
  26.8 8.6 %collective-permute-start.9 = (bf16[512,128]{1,0:T(8,128)(2,1)S(1)}, bf16[512,128]{1,0:T(8,128)(2,1)S(1)}, u32[]{:S(2)}, u32[]{:S(2)}) collective-permute-start(bf16[512,128]{1,0:T(8,128)(2,1)S(1)} %collective-permute-done.7.rest_9_), channel_id=1, source_target_pairs={{1,0},{3,2},{5,4},{7,6},{9,8},{11,10},{13,12},{15,14},{17,16},{19,... | collective-permute-start | bytes 393224 | tf_op jit(solution)/shard_map/ppermute | solution.py:289
  53.0 34.1 %collective-permute-start.20 = (bf16[2,8,256,128]{3,2,1,0:T(8,128)(2,1)S(1)}, bf16[2,8,256,128]{3,2,1,0:T(8,128)(2,1)S(1)}, u32[]{:S(2)}, u32[]{:S(2)}) collective-permute-start(bf16[2,8,256,128]{3,2,1,0:T(8,128)(2,1)S(1)} %copy-done.2), channel_id=1, source_target_pairs={{0,8},{8,0},{16,24},{24,16},{1,9},{9,1},{17,25},{25,17},{2,10},{10... | collective-permute-start | bytes 3145736 | tf_op jit(solution)/shard_map/ppermute | solution.py:404
  53.0 37.0 %collective-permute-start.15 = (bf16[2,8,256,128]{3,2,1,0:T(8,128)(2,1)}, bf16[2,8,256,128]{3,2,1,0:T(8,128)(2,1)S(1)}, u32[]{:S(2)}, u32[]{:S(2)}) collective-permute-start(bf16[2,8,256,128]{3,2,1,0:T(8,128)(2,1)} %wo.5), channel_id=1, source_target_pairs={{0,8},{8,0},{16,24},{24,16},{1,9},{9,1},{17,25},{25,17},{2,10},{10... | collective-permute-start | bytes 3145736 | tf_op jit(solution)/shard_map/ppermute | solution.py:404
  64.5 21.1 %collective-permute-start.10 = (bf16[512,256]{1,0:T(8,128)(2,1)S(1)}, bf16[512,256]{1,0:T(8,128)(2,1)S(1)}, u32[]{:S(2)}, u32[]{:S(2)}) collective-permute-start(bf16[512,256]{1,0:T(8,128)(2,1)S(1)} %get-tuple-element.37), channel_id=1, source_target_pairs={{0,1},{2,3},{4,5},{6,7},{8,9},{10,11},{12,13},{14,15},{16,17},{18,... | collective-permute-start | bytes 786440 | tf_op jit(solution)/shard_map/ppermute | solution.py:289
  76.5 15.0 %collective-permute-start.12 = (bf16[512,256]{1,0:T(8,128)(2,1)S(1)}, bf16[512,256]{1,0:T(8,128)(2,1)S(1)}, u32[]{:S(2)}, u32[]{:S(2)}) collective-permute-start(bf16[512,256]{1,0:T(8,128)(2,1)S(1)} %broadcast_select_fusion), channel_id=1, source_target_pairs={{0,1},{2,3},{4,5},{6,7},{1,0},{3,2},{5,4},{7,6},{8,9},{10,11},{12,... | collective-permute-start | bytes 786440 | tf_op jit(solution)/shard_map/ppermute | solution.py:289
  76.6 55.4 %collective-permute-start.14 = (bf16[512,256]{1,0:T(8,128)(2,1)S(1)}, bf16[512,256]{1,0:T(8,128)(2,1)S(1)}, u32[]{:S(2)}, u32[]{:S(2)}) collective-permute-start(bf16[512,256]{1,0:T(8,128)(2,1)S(1)} %get-tuple-element.36), channel_id=1, source_target_pairs={{1,0},{3,2},{5,4},{7,6},{9,8},{11,10},{13,12},{15,14},{17,16},{19,... | collective-permute-start | bytes 786440 | tf_op jit(solution)/shard_map/ppermute | solution.py:289
  85.7 21.3 %collective-permute-start.11 = (bf16[512,256]{1,0:T(8,128)(2,1)S(1)}, bf16[512,256]{1,0:T(8,128)(2,1)S(1)}, u32[]{:S(2)}, u32[]{:S(2)}) collective-permute-start(bf16[512,256]{1,0:T(8,128)(2,1)S(1)} %fusion.3), channel_id=1, source_target_pairs={{2,0},{3,1},{4,2},{5,3},{6,4},{7,5},{10,8},{11,9},{12,10},{13,11},... | collective-permute-start | bytes 786440 | tf_op jit(solution)/shard_map/ppermute | solution.py:289
  87.2 21.4 %collective-permute-start.21 = (bf16[2,2,2,256,128]{4,3,2,1,0:T(8,128)(2,1)S(1)}, bf16[2,2,2,256,128]{4,3,2,1,0:T(8,128)(2,1)S(1)}, u32[]{:S(2)}, u32[]{:S(2)}) collective-permute-start(bf16[2,2,2,256,128]{4,3,2,1,0:T(8,128)(2,1)S(1)} %fusion), channel_id=1, source_target_pairs={{0,1},{1,0},{2,3},{3,2},{4,5},{5,4},{6,7},{7,6},{8,9},{9,8},{10,11... | collective-permute-start | bytes 1572872 | tf_op jit(solution)/shard_map/ppermute | solution.py:404
  91.5 17.4 %collective-permute-start.16 = (bf16[2,2,2,256,128]{4,3,1,0,2:T(8,128)(2,1)S(1)}, bf16[2,2,2,256,128]{4,3,1,0,2:T(8,128)(2,1)S(1)}, u32[]{:S(2)}, u32[]{:S(2)}) collective-permute-start(bf16[2,2,2,256,128]{4,3,1,0,2:T(8,128)(2,1)S(1)} %copy.22), channel_id=1, source_target_pairs={{0,16},{8,24},{16,0},{24,8},{1,17},{9,25},{17,1},{25,9},{2,18},{10... | collective-permute-start | bytes 1572872 | tf_op jit(solution)/shard_map/ppermute | solution.py:404
  107.1 24.8 %collective-permute-start.13 = (bf16[512,256]{1,0:T(8,128)(2,1)S(1)}, bf16[512,256]{1,0:T(8,128)(2,1)S(1)}, u32[]{:S(2)}, u32[]{:S(2)}) collective-permute-start(bf16[512,256]{1,0:T(8,128)(2,1)S(1)} %fusion.5), channel_id=1, source_target_pairs={{2,0},{3,1},{4,2},{5,3},{6,4},{7,5},{10,8},{11,9},{12,10},{13,11},... | collective-permute-start | bytes 786440 | tf_op jit(solution)/shard_map/ppermute | solution.py:289
  108.8 26.2 %collective-permute-start.22 = (bf16[2,2,256,128]{3,2,1,0:T(8,128)(2,1)S(1)}, bf16[2,2,256,128]{3,2,1,0:T(8,128)(2,1)S(1)}, u32[]{:S(2)}, u32[]{:S(2)}) collective-permute-start(bf16[2,2,256,128]{3,2,1,0:T(8,128)(2,1)S(1)} %get-tuple-element.35), channel_id=1, source_target_pairs={{0,16},{8,24},{16,0},{24,8},{1,17},{9,25},{17,1},{25,9},{2,18},{10... | collective-permute-start | bytes 786440 | tf_op jit(solution)/shard_map/ppermute | solution.py:404
  109.0 26.6 %collective-permute-start.17 = (bf16[2,2,256,128]{3,2,1,0:T(8,128)(2,1)S(1)}, bf16[2,2,256,128]{3,2,1,0:T(8,128)(2,1)S(1)}, u32[]{:S(2)}, u32[]{:S(2)}) collective-permute-start(bf16[2,2,256,128]{3,2,1,0:T(8,128)(2,1)S(1)} %get-tuple-element.33), channel_id=1, source_target_pairs={{0,1},{1,0},{2,3},{3,2},{4,5},{5,4},{6,7},{7,6},{8,9},{9,8},{10,11... | collective-permute-start | bytes 786440 | tf_op jit(solution)/shard_map/ppermute | solution.py:404
  135.0 5.7 %collective-permute-start.23 = (bf16[2,256,128]{2,1,0:T(8,128)(2,1)S(1)}, bf16[2,256,128]{2,1,0:T(8,128)(2,1)S(1)}, u32[]{:S(2)}, u32[]{:S(2)}) collective-permute-start(bf16[2,256,128]{2,1,0:T(8,128)(2,1)S(1)} %get-tuple-element.41), channel_id=1, source_target_pairs={{0,2},{1,3},{2,0},{3,1},{4,6},{5,7},{6,4},{7,5},{8,10},{9,11},{10,... | collective-permute-start | bytes 393224 | tf_op jit(solution)/shard_map/ppermute | solution.py:404
  135.7 6.5 %collective-permute-start.18 = (bf16[2,256,128]{2,1,0:T(8,128)(2,1)S(1)}, bf16[2,256,128]{2,1,0:T(8,128)(2,1)S(1)}, u32[]{:S(2)}, u32[]{:S(2)}) collective-permute-start(bf16[2,256,128]{2,1,0:T(8,128)(2,1)S(1)} %get-tuple-element.39), channel_id=1, source_target_pairs={{0,2},{1,3},{2,0},{3,1},{4,6},{5,7},{6,4},{7,5},{8,10},{9,11},{10,... | collective-permute-start | bytes 393224 | tf_op jit(solution)/shard_map/ppermute | solution.py:404
  142.1 5.6 %collective-permute-start.19 = (bf16[256,128]{1,0:T(8,128)(2,1)S(1)}, bf16[256,128]{1,0:T(8,128)(2,1)S(1)}, u32[]{:S(2)}, u32[]{:S(2)}) collective-permute-start(bf16[256,128]{1,0:T(8,128)(2,1)S(1)} %fusion.17), channel_id=1, source_target_pairs={{0,4},{1,5},{2,6},{3,7},{4,0},{5,1},{6,2},{7,3},{8,12},{9,13},{10,... | collective-permute-start | bytes 196616 | tf_op jit(solution)/shard_map/ppermute | solution.py:404
  (17 other events, 106.8 us)

commit v2 on v1

v2 whole, which is shorter than its diff:
```python
import functools
import math

import numpy as np

import jax
import jax.numpy as jnp
from jax import lax
from jax.experimental import pallas as pl
from jax.experimental.pallas import tpu as pltpu
from jax.sharding import PartitionSpec as P

HEAD = 128
WIN = 4096
NEG = -1e30
LOG2E = math.log2(math.e)
LN2 = math.log(2.0)
SCALE = 1.0 / math.sqrt(HEAD)
F32 = jnp.float32
BF16 = jnp.bfloat16


def doc_starts(lens_ref, pos):
    begin = jnp.int32(0)
    found = jnp.zeros_like(pos)
    for d in range(lens_ref.shape[1]):
        found = jnp.where(pos >= begin, begin, found)
        begin = begin + lens_ref[0, d]
    return found


def sincos(angle):
    turns = jnp.floor(angle * (2.0 / math.pi) + 0.5)
    rest = angle - turns * 1.5703125
    rest = rest - turns * 4.83751296997070312e-4
    rest = rest - turns * 7.54978995489188216e-8
    square = rest * rest
    sine = rest + rest * square * (
        -1.6666654611e-1 + square * (8.3321608736e-3 + square * -1.9515295891e-4)
    )
    cosine = (
        1.0
        - 0.5 * square
        + square
        * square
        * (4.166664568298827e-2 + square * (-1.388731625493765e-3 + square * 2.443315711809948e-5))
    )
    quarter = turns.astype(jnp.int32) & 3
    odd = (quarter & 1) == 1
    out_sin = jnp.where(odd, cosine, sine)
    out_cos = jnp.where(odd, sine, cosine)
    out_sin = jnp.where(quarter >= 2, -out_sin, out_sin)
    out_cos = jnp.where((quarter == 1) | (quarter == 2), -out_cos, out_cos)
    return out_sin, out_cos


def place():
    return lax.axis_index("ctx").astype(jnp.int32), lax.axis_size("ctx")


def rotate(x, cosine, sine):
    return x * cosine + pltpu.roll(x, HEAD // 2, 1) * sine


def prep_kernel(lens_ref, freq_ref, k_ref, v_ref, kv_ref, cos_ref, sin_ref):
    rows = k_ref.shape[0]
    dev, _ = place()
    pos = dev * rows + lax.broadcasted_iota(jnp.int32, (rows, HEAD), 0)
    rel = pos - doc_starts(lens_ref, pos)
    sine, cosine = sincos(rel.astype(F32) * freq_ref[...])
    lane = lax.broadcasted_iota(jnp.int32, (rows, HEAD), 1)
    sine = jnp.where(lane < HEAD // 2, -sine, sine)
    cos_ref[...] = cosine
    sin_ref[...] = sine
    kv_ref[:, :HEAD] = rotate(k_ref[...].astype(F32), cosine, sine).astype(BF16)
    kv_ref[:, HEAD:] = v_ref[...]


def rotq_kernel(q_ref, cos_ref, sin_ref, out_ref):
    for h in range(q_ref.shape[1] // HEAD):
        q = q_ref[:, h * HEAD : (h + 1) * HEAD].astype(F32)
        out_ref[:, h * HEAD : (h + 1) * HEAD] = rotate(q, cos_ref[...], sin_ref[...]).astype(BF16)


def is_paired(n_ctx, back):
    return n_ctx == 8 and back == 4


def slot_list(dev, n_ctx, back):
    if is_paired(n_ctx, back):
        odd = dev % 2 == 1
        skip = jnp.int32(-1)
        return [4, 2, jnp.where(odd, 3, skip), 0, jnp.where(odd, 1, 3), jnp.where(odd, skip, 1)]
    return [back - s for s in range(back + 1)]


def load_slots(slots, refs, scratch, sem, rows, lo=0):
    hi = lo + scratch.shape[0] // rows
    for start in (True, False):
        for i, (slot, ref) in enumerate(zip(slots, refs)):
            if isinstance(slot, int) and not lo <= slot < hi:
                continue

            def move(slot=slot, ref=ref, i=i):
                at = (slot - lo) * rows
                if not isinstance(at, int):
                    at = pl.multiple_of(at, rows)
                copy = pltpu.make_async_copy(ref, scratch.at[pl.ds(at, rows)], sem.at[i])
                if start:
                    copy.start()
                else:
                    copy.wait()

            if isinstance(slot, int):
                move()
            else:
                pl.when((slot >= lo) & (slot < hi))(move)


def tile_ranges(lens_ref, first, qb, kb, base, n_tiles):
    last = first + qb - 1
    low_first = jnp.maximum(doc_starts(lens_ref, first), first - WIN + 1)
    low_last = jnp.maximum(doc_starts(lens_ref, last), last - WIN + 1)
    hi = jnp.minimum((last - base) // kb + 1, n_tiles)
    lo = jnp.minimum(jnp.maximum(low_first - base, 0) // kb, hi)
    full_lo = jnp.clip((jnp.maximum(low_last - base, 0) + kb - 1) // kb, lo, hi)
    full_hi = jnp.clip((first - base + 1) // kb, full_lo, hi)
    return lo, full_lo, full_hi, hi


def over_tiles(ranges, visit, carry):
    lo, full_lo, full_hi, hi = ranges
    carry = lax.fori_loop(full_lo, full_hi, functools.partial(visit, False), carry)

    def edge(i, c):
        return visit(True, jnp.where(lo + i < full_lo, lo + i, full_hi + i - (full_lo - lo)), c)

    return lax.fori_loop(0, (full_lo - lo) + (hi - full_hi), edge, carry)


def fold(x, op):
    return op(x.reshape(x.shape[0] // 8, 8, x.shape[1]), axis=0)


def stack_heads(ref):
    heads = ref.shape[1] // HEAD
    return jnp.concatenate([ref[:, h * HEAD : (h + 1) * HEAD] for h in range(heads)], axis=0)


def query_bounds(lens_ref, first, qb, heads):
    pos = first + lax.broadcasted_iota(jnp.int32, (1, qb), 1)
    low = jnp.maximum(doc_starts(lens_ref, pos), pos - WIN + 1)
    return jnp.concatenate([low] * heads, axis=1), jnp.concatenate([pos] * heads, axis=1)


def masked_scores(s, base, at, low, high):
    key = base + at + lax.broadcasted_iota(jnp.int32, (s.shape[0], 1), 0)
    return jnp.where((key >= low) & (key <= high), s, NEG)


NT = (((1,), (1,)), ((), ()))
NN = (((1,), (0,)), ((), ()))
TN = (((0,), (0,)), ((), ()))


def dot(a, b, dims):
    return lax.dot_general(a, b, dims, preferred_element_type=F32)


def fwd_kernel(n_refs, back, kb, lens_ref, q_ref, *rest):
    kv_refs = rest[:n_refs]
    o_ref, lse_ref, pack_ref, kv_scr, sem = rest[n_refs:]
    step = pl.program_id(0)
    qb, width = q_ref.shape
    heads = width // HEAD
    rows = heads * qb
    tok = kv_refs[0].shape[0]
    dev, n_ctx = place()

    @pl.when(step == 0)
    def _():
        load_slots(slot_list(dev, n_ctx, back), kv_refs, kv_scr, sem, tok)

    base = (dev - back) * tok
    first = dev * tok + step * qb
    q = stack_heads(q_ref)
    low, high = query_bounds(lens_ref, first, qb, heads)
    factor = SCALE * LOG2E

    def visit(masked, j, carry):
        top, total, acc = carry
        at = pl.multiple_of(j * kb, kb)
        s = dot(kv_scr[pl.ds(at, kb), :HEAD], q, NT)
        if masked:
            s = masked_scores(s, base, at, low, high)
        new = jnp.maximum(top, jnp.max(fold(s, jnp.max), axis=0, keepdims=True) * factor)
        alpha = jnp.exp2(top - new)
        p = jnp.exp2(s * factor - new)
        total = total * alpha + fold(p, jnp.sum)
        acc = acc * alpha + dot(kv_scr[pl.ds(at, kb), HEAD:], p.astype(BF16), TN)
        return new, total, acc

    carry = (jnp.full((1, rows), NEG, F32), jnp.zeros((8, rows), F32), jnp.zeros((HEAD, rows), F32))
    ranges = tile_ranges(lens_ref, first, qb, kb, base, kv_scr.shape[0] // kb)
    top, total, acc = over_tiles(ranges, visit, carry)
    total = jnp.sum(total, axis=0, keepdims=True)
    lse = (top + jnp.log2(total)) * LN2
    out = acc / total
    for h in range(heads):
        lse_ref[h : h + 1, :] = lse[:, h * qb : (h + 1) * qb]
        o_ref[:, h * HEAD : (h + 1) * HEAD] = jnp.transpose(out[:, h * qb : (h + 1) * qb]).astype(BF16)
    lines = jnp.concatenate(
        [lse[:, c * HEAD : (c + 1) * HEAD] for c in range(rows // HEAD)], axis=0
    )
    coarse = lines.astype(BF16)
    fine = (lines - coarse.astype(F32)).astype(BF16)
    pack_ref[0] = jnp.concatenate([coarse, fine], axis=0)


def bwd_core(lens_ref, q_ref, dy_ref, o_ref, lse_ref, kv, base, kb, dk_scr, dv_scr, dq):
    qb, width = q_ref.shape
    heads = width // HEAD
    tok = qb * pl.num_programs(0)
    dev, _ = place()
    first = dev * tok + pl.program_id(0) * qb
    q, dy = stack_heads(q_ref), stack_heads(dy_ref)
    prod = dy.astype(F32) * stack_heads(o_ref).astype(F32)
    delta = jnp.concatenate(
        [
            jnp.sum(jnp.transpose(prod[h * qb : (h + 1) * qb, :]), axis=0, keepdims=True)
            for h in range(heads)
        ],
        axis=1,
    )
    lse = jnp.concatenate([lse_ref[h : h + 1, :] for h in range(heads)], axis=1) * LOG2E
    low, high = query_bounds(lens_ref, first, qb, heads)
    factor = SCALE * LOG2E

    def visit(masked, j, dq):
        at = pl.multiple_of(j * kb, kb)
        k, v = kv[pl.ds(at, kb), :HEAD], kv[pl.ds(at, kb), HEAD:]
        s = dot(k, q, NT)
        if masked:
            s = masked_scores(s, base, at, low, high)
        p = jnp.exp2(s * factor - lse)
        ds = (p * (dot(v, dy, NT) - delta)).astype(BF16)
        dv_scr[pl.ds(at, kb), :] += dot(p.astype(BF16), dy, NN)
        dk_scr[pl.ds(at, kb), :] += dot(ds, q, NN)
        return dq + dot(k, ds, TN)

    return over_tiles(tile_ranges(lens_ref, first, qb, kb, base, kv.shape[0] // kb), visit, dq)


def far_kernel(n_refs, back, lo, has_dq, kb, lens_ref, q_ref, dy_ref, o_ref, lse_ref, *rest):
    kv_refs = rest[:n_refs]
    dqin_ref = rest[n_refs] if has_dq else None
    dq_ref, far_ref, kv_scr, dk_scr, dv_scr, sem = rest[n_refs + has_dq :]
    tok = kv_refs[0].shape[0]
    dev, n_ctx = place()
    step = pl.program_id(0)

    @pl.when(step == 0)
    def _():
        load_slots(slot_list(dev, n_ctx, back)[1:], kv_refs, kv_scr, sem, tok, lo)
        dk_scr[...] = jnp.zeros_like(dk_scr)
        dv_scr[...] = jnp.zeros_like(dv_scr)

    base = (dev - back + lo) * tok
    dq = dqin_ref[0] if has_dq else jnp.zeros(dq_ref.shape[1:], F32)
    dq_ref[0] = bwd_core(
        lens_ref, q_ref, dy_ref, o_ref, lse_ref, kv_scr, base, kb, dk_scr, dv_scr, dq
    )

    @pl.when(step == pl.num_programs(0) - 1)
    def _():
        for r in range(far_ref.shape[0]):
            far_ref[r, :, :HEAD] = dk_scr[r * tok : (r + 1) * tok, :].astype(BF16)
            far_ref[r, :, HEAD:] = dv_scr[r * tok : (r + 1) * tok, :].astype(BF16)


def near_kernel(kb, lens_ref, q_ref, dy_ref, o_ref, lse_ref, dqin_ref, kv_ref, cos_ref, sin_ref,
                dq_ref, own_ref, dk_scr, dv_scr):
    tok = kv_ref.shape[0]
    dev, _ = place()
    step = pl.program_id(0)
    qb = q_ref.shape[0]

    @pl.when(step == 0)
    def _():
        dk_scr[...] = jnp.zeros_like(dk_scr)
        dv_scr[...] = jnp.zeros_like(dv_scr)

    dq = bwd_core(
        lens_ref, q_ref, dy_ref, o_ref, lse_ref, kv_ref, dev * tok, kb, dk_scr, dv_scr, dqin_ref[0]
    )
    for h in range(q_ref.shape[1] // HEAD):
        part = jnp.transpose(dq[:, h * qb : (h + 1) * qb]) * SCALE
        dq_ref[:, h * HEAD : (h + 1) * HEAD] = rotate(part, cos_ref[...], -sin_ref[...]).astype(BF16)

    @pl.when(step == pl.num_programs(0) - 1)
    def _():
        own_ref[:, :HEAD] = dk_scr[...]
        own_ref[:, HEAD:] = dv_scr[...]


def wo_kernel(core, group, a_ref, g_ref, *rest):
    outs, (g_scr, sem) = rest[:-2], rest[-2:]
    dev, _ = place()
    dp = lax.axis_index("dp").astype(jnp.int32)
    n_half, n_ctx, rows, col = outs[0].shape
    wide = group * col
    groups = n_ctx // group
    at = jnp.transpose(a_ref[...])

    def fetch(n):
        i, p = divmod(n, groups)
        block = ((2 * i + core) ^ dp) * groups + (p ^ (dev // group))
        start = pl.multiple_of(block * wide, wide)
        return pltpu.make_async_copy(g_ref.at[:, pl.ds(start, wide)], g_scr.at[n], sem.at[n])

    for n in range(n_half * groups):
        fetch(n).start()
    for n in range(n_half * groups):
        i, p = divmod(n, groups)
        fetch(n).wait()
        res = jnp.dot(at, g_scr[n], preferred_element_type=F32).astype(BF16)
        for j in range(group):
            to = p * group + (j ^ (dev & (group - 1)))
            for c, out_ref in enumerate(outs):
                out_ref[i, to] = res[c * rows : (c + 1) * rows, j * col : (j + 1) * col]


def home_kernel(n_in, own_ref, cos_ref, sin_ref, *rest):
    ins, (dk_ref, dv_ref) = rest[:n_in], rest[n_in:]
    total = own_ref[...]
    for ref in ins:
        total = total + ref[...].astype(F32)
    dk_ref[...] = rotate(total[:, :HEAD] * SCALE, cos_ref[...], -sin_ref[...]).astype(BF16)
    dv_ref[...] = total[:, HEAD:].astype(BF16)


def owner_kernel(owner_ref, lse_ref, out_ref):
    dev, n_ctx = place()
    heads = out_ref.shape[1]
    tok = out_ref.shape[0]
    block_len = tok // n_ctx
    halves = lse_ref.shape[1]
    chunks = tok // halves // HEAD
    for i in range(n_ctx):
        c = dev ^ i
        mine = jnp.zeros((heads, block_len), F32)
        lines = lse_ref[i].astype(F32)
        lines = lines[:, : heads * chunks] + lines[:, heads * chunks :]
        for s in range(n_ctx):
            half, rest = divmod(s * block_len, tok // halves)
            chunk, lane = divmod(rest, HEAD)
            part = jnp.concatenate(
                [
                    lines[half, h * chunks + chunk : h * chunks + chunk + 1, lane : lane + block_len]
                    for h in range(heads)
                ],
                axis=0,
            )
            mine = jnp.where(owner_ref[c * n_ctx + s] == dev, part, mine)
        out_ref[pl.ds(pl.multiple_of(c * block_len, block_len), block_len), :] = jnp.transpose(mine)


SMEM_SPEC = pl.BlockSpec(memory_space=pltpu.SMEM)
VMEM_SPEC = pl.BlockSpec(memory_space=pltpu.VMEM)
ANY_SPEC = pl.BlockSpec(memory_space=pl.ANY)


def params(mib, *semantics):
    return pltpu.CompilerParams(dimension_semantics=semantics or None, vmem_limit_bytes=mib << 20)


def cost(flops, size, exps=0):
    return pl.CostEstimate(flops=int(flops), bytes_accessed=int(size), transcendentals=int(exps))


def after(x, *others):
    return lax.optimization_barrier((x, *others))[0]


def on_device(queries, keys, values, doc_lengths, owner, out_weight, out_grad):
    n_ctx = lax.axis_size("ctx")
    n_dp = lax.axis_size("dp")
    dev = lax.axis_index("ctx").astype(jnp.int32)
    dp = lax.axis_index("dp").astype(jnp.int32)
    tok = queries.shape[1]
    width = queries.shape[2]
    heads = width // HEAD
    seq_len = tok * n_ctx
    d_model = out_grad.shape[2]
    reach = min(WIN, seq_len // 2)
    back = min(-(-reach // tok), n_ctx - 1)
    sds = jax.ShapeDtypeStruct

    half = HEAD // 2
    freq = (10000.0 ** (-2.0 * np.arange(half) / HEAD)).astype(np.float32)
    freq = jnp.asarray(np.concatenate([freq, freq])[None, :])

    def shift(x, pairs):
        return lax.ppermute(x, "ctx", pairs)

    hop = [(i, i + 2) for i in range(n_ctx - 2)]
    hop_back = [(b, a) for a, b in hop]
    up = [(i, i + 1) for i in range(0, n_ctx, 2)]
    down = [(b, a) for a, b in up]
    swap = up + down
    odd = dev % 2 == 1
    paired = is_paired(n_ctx, back)

    kv_home, cos, sin = pl.pallas_call(
        prep_kernel,
        out_shape=(sds((tok, 2 * HEAD), BF16), sds((tok, HEAD), F32), sds((tok, HEAD), F32)),
        in_specs=[SMEM_SPEC] + [VMEM_SPEC] * 3,
        out_specs=(VMEM_SPEC,) * 3,
        compiler_params=params(58),
        cost_estimate=cost(1 << 22, 1 << 20),
        name="prep",
    )(doc_lengths, freq, keys[0], values[0])

    def d_out_of(grad):
        return lax.dot_general(
            grad, out_weight, (((1,), (1,)), ((), ())), preferred_element_type=F32
        ).astype(BF16)

    def rotated_queries(x):
        return pl.pallas_call(
            rotq_kernel,
            out_shape=sds((tok, width), BF16),
            in_specs=[VMEM_SPEC] * 3,
            out_specs=VMEM_SPEC,
            compiler_params=params(4),
            cost_estimate=cost(1 << 22, 2 << 20),
            name="rotq",
        )(x, cos, sin)

    if paired:
        a1 = shift(kv_home, hop)
        e1 = shift(kv_home, up)
        d_out = d_out_of(out_grad[0])
        a1 = after(a1, d_out)
        s1 = shift(a1, swap)
        a2 = shift(a1, hop)
        q_rot = rotated_queries(queries[0])
        o3 = shift(a2, down)
        blocks = [kv_home, a1, e1, a2, s1, o3]
    else:
        blocks = [kv_home] + [
            shift(kv_home, [(i, i + s) for i in range(n_ctx - s)]) for s in range(1, back + 1)
        ]
        q_rot = rotated_queries(queries[0])
        d_out = d_out_of(out_grad[0])

    n_keys = (back + 1) * tok
    qb = tok // 2
    kb = tok
    tok_spec = pl.BlockSpec((qb, width), lambda i: (i, 0))
    lse_spec = pl.BlockSpec((heads, qb), lambda i: (0, i))
    table_spec = pl.BlockSpec((qb, HEAD), lambda i: (i, 0))
    dq_spec = pl.BlockSpec((1, HEAD, heads * qb), lambda i: (i, 0, 0))
    pairs = heads * tok * (tok + reach) // 2
    pack_rows = 2 * heads * qb // HEAD
    attn, lse, pack = pl.pallas_call(
        functools.partial(fwd_kernel, len(blocks), back, kb),
        grid=(tok // qb,),
        out_shape=(
            sds((tok, width), BF16),
            sds((heads, tok), F32),
            sds((tok // qb, pack_rows, HEAD), BF16),
        ),
        in_specs=[SMEM_SPEC, tok_spec] + [ANY_SPEC] * len(blocks),
        out_specs=(tok_spec, lse_spec, pl.BlockSpec((1, pack_rows, HEAD), lambda i: (i, 0, 0))),
        scratch_shapes=[
            pltpu.VMEM((n_keys, 2 * HEAD), BF16),
            pltpu.SemaphoreType.DMA((len(blocks),)),
        ],
        compiler_params=params(20, "arbitrary"),
        cost_estimate=cost(4 * pairs * HEAD, 4 << 20, pairs),
        name="fwd",
    )(doc_lengths, q_rot, *blocks)

    col = d_model // (n_dp * n_ctx)
    bits_dp = n_dp.bit_length() - 1
    bits_ctx = n_ctx.bit_length() - 1
    group = min(n_ctx, max(1, 256 // col))
    colors = 2
    rows = width // colors
    steps = n_dp // 2 * (n_ctx // group)

    def partial_wo(core):
        return pl.pallas_call(
            functools.partial(wo_kernel, core, group),
            out_shape=(sds((n_dp // 2, n_ctx, rows, col), BF16),) * colors,
            in_specs=[VMEM_SPEC, ANY_SPEC],
            out_specs=(VMEM_SPEC,) * colors,
            scratch_shapes=[
                pltpu.VMEM((steps, tok, group * col), BF16),
                pltpu.SemaphoreType.DMA((steps,)),
            ],
            compiler_params=params(16),
            cost_estimate=cost(tok * width * d_model, 6 << 20),
            name="wo",
        )(attn, out_grad[0])

    def exchange(x, axis, bit, size):
        return lax.ppermute(x, axis, [(i, i ^ bit) for i in range(size)])

    size_of = {"dp": n_dp, "ctx": n_ctx}
    lead = [("dp", b) for b in range(bits_dp - 1, 0, -1)]
    lead += [("ctx", b) for b in range(bits_ctx - 1, -1, -1)]

    class Parts:
        def __init__(self, one, two, left):
            self.one, self.two, self.left = one, two, left

        def pick(self, axis, which):
            at = self.left.index(axis)
            one, two = [lax.index_in_dim(x, which, at, keepdims=False) for x in (self.one, self.two)]
            return (one.astype(F32) + two.astype(F32)).astype(BF16)

        def step(self, axis, recv):
            left = [a for a in self.left if a != axis]
            return Parts(self.pick(axis, 0), recv, left)

    def move(x, axis):
        return exchange(x, axis[0], 1 << axis[1], size_of[axis[0]])

    wo_send = partial_wo(1)
    wo_recv = [exchange(x, "dp", 1, n_dp) for x in wo_send]
    wo_keep = partial_wo(0)
    shape = (2,) * len(lead) + (rows, col)
    color = [Parts(k.reshape(shape), r.reshape(shape), lead) for k, r in zip(wo_keep, wo_recv)]
    first_dp = [("dp", b) for b in range(1, bits_dp)]
    ctx_axes = [("ctx", b) for b in range(bits_ctx)]
    orders = [first_dp + ctx_axes[:1], ctx_axes[:1] + first_dp]

    lines = pack.reshape(-1, col)

    def move_with_lse(x, axis, lse_of):
        size = x.size // col
        out = move(jnp.concatenate([x.reshape(size, col), lse_of], axis=0), axis)
        return out[:size].reshape(x.shape), jnp.concatenate([lse_of, out[size:]], axis=0)

    sends = [color[c].pick(orders[c][0], 1) for c in range(colors)]
    recvs = [move(sends[0], orders[0][0])]
    recv, lines = move_with_lse(sends[1], orders[1][0], lines)
    recvs.append(recv)
    color = [color[c].step(orders[c][0], recvs[c]) for c in range(colors)]

    def backward_far(lo, hi, lse_in, dq_in):
        count = hi - lo
        return pl.pallas_call(
            functools.partial(far_kernel, len(blocks) - 1, back, lo, len(dq_in), kb),
            grid=(tok // qb,),
            out_shape=(sds((tok // qb, HEAD, heads * qb), F32), sds((count, tok, 2 * HEAD), BF16)),
            in_specs=[SMEM_SPEC, tok_spec, tok_spec, tok_spec, lse_spec]
            + [ANY_SPEC] * (len(blocks) - 1)
            + [dq_spec] * len(dq_in),
            out_specs=(dq_spec, pl.BlockSpec((count, tok, 2 * HEAD), lambda i: (0, 0, 0))),
            scratch_shapes=[
                pltpu.VMEM((count * tok, 2 * HEAD), BF16),
                pltpu.VMEM((count * tok, HEAD), F32),
                pltpu.VMEM((count * tok, HEAD), F32),
                pltpu.SemaphoreType.DMA((len(blocks) - 1,)),
            ],
            compiler_params=params(28, "arbitrary"),
            cost_estimate=cost(8 * pairs * HEAD, 8 << 20, pairs),
            name="far",
        )(doc_lengths, q_rot, d_out, attn, lse_in, *blocks[1:], *dq_in)

    def plus(*xs):
        return functools.reduce(jnp.add, [x.astype(F32) for x in xs]).astype(BF16)

    lse_b = after(lse, *sends)
    if paired:
        dq_far, (d4, d3) = backward_far(0, 2, lse_b, [])
        r3 = shift(d3, swap)
        dq_far, (d2, d1) = backward_far(2, 4, lse_b, [dq_far])
        none = jnp.zeros_like(r3)
        sum4 = plus(d4, jnp.where(odd, r3, none))
        b2 = shift(sum4, hop_back)
        r1 = shift(d1, swap)
    else:
        dq_far, far = backward_far(0, back, lse_b, [])

    for c in range(colors):
        color[c].two = after(color[c].two, dq_far)
    sends = []
    for c in range(colors):
        for axis in orders[c][1:]:
            sends.append(color[c].pick(axis, 1))
            color[c] = color[c].step(axis, move(sends[-1], axis))

    dq_near = after(dq_far, *sends)
    near_kb = max(kb // 2, 8)
    q_grad, own = pl.pallas_call(
        functools.partial(near_kernel, near_kb),
        grid=(tok // qb,),
        out_shape=(sds((tok, width), BF16), sds((tok, 2 * HEAD), F32)),
        in_specs=[SMEM_SPEC, tok_spec, tok_spec, tok_spec, lse_spec, dq_spec, VMEM_SPEC, table_spec, table_spec],
        out_specs=(tok_spec, pl.BlockSpec((tok, 2 * HEAD), lambda i: (0, 0))),
        scratch_shapes=[pltpu.VMEM((tok, HEAD), F32), pltpu.VMEM((tok, HEAD), F32)],
        compiler_params=params(20, "arbitrary"),
        cost_estimate=cost(8 * heads * tok * tok * HEAD, 4 << 20, heads * tok * tok),
        name="near",
    )(doc_lengths, q_rot, d_out, attn, lse, dq_near, kv_home, cos, sin)

    left = color[0].left
    join = len(left)
    one = jnp.concatenate([color[c].one for c in range(colors)], axis=join)
    two = jnp.concatenate([color[c].two for c in range(colors)], axis=join)
    both = Parts(one, two, left)
    for axis in ctx_axes[1:]:
        send = after(both.pick(axis, 1), own)
        recv, lines = move_with_lse(send, axis, lines)
        both = both.step(axis, recv)
    wgrad = both.one.astype(F32) + both.two.astype(F32)

    if paired:
        sum2 = plus(d2, b2, jnp.where(odd, r1, r3))
        arrived = [shift(after(sum2, own), hop_back), jnp.where(odd, none, r1)]
    else:
        arrived = [
            shift(far[back - s], [(i + s, i) for i in range(n_ctx - s)]) for s in range(1, back + 1)
        ]
    k_grad, v_grad = pl.pallas_call(
        functools.partial(home_kernel, len(arrived)),
        out_shape=(sds((tok, HEAD), BF16), sds((tok, HEAD), BF16)),
        in_specs=[VMEM_SPEC] * (3 + len(arrived)),
        out_specs=(VMEM_SPEC, VMEM_SPEC),
        compiler_params=params(4),
        cost_estimate=cost(1 << 20, 2 << 20),
        name="home",
    )(own, cos, sin, *arrived)

    owner_lse = pl.pallas_call(
        owner_kernel,
        out_shape=sds((tok, heads), F32),
        in_specs=[SMEM_SPEC, VMEM_SPEC],
        out_specs=VMEM_SPEC,
        compiler_params=params(4),
        cost_estimate=cost(1 << 18, 1 << 18),
        name="owned",
    )(owner[0], lines.reshape(n_ctx, tok // qb, pack_rows, HEAD))

    return (attn[None], q_grad[None], k_grad[None], v_grad[None], wgrad, owner_lse[None, None])


def solution(mesh):
    in_specs = (
        P("dp", "ctx", None),
        P("dp", "ctx", None),
        P("dp", "ctx", None),
        P("dp", None),
        P("dp", None),
        P(),
        P("dp", "ctx", None),
    )
    out_specs = (
        P("dp", "ctx", None),
        P("dp", "ctx", None),
        P("dp", "ctx", None),
        P("dp", "ctx", None),
        P(None, ("dp", "ctx")),
        P("dp", "ctx", None, None),
    )
    return jax.shard_map(
        on_device, mesh=mesh, in_specs=in_specs, out_specs=out_specs, check_vma=False
    )
```

time: 151 us -> 116 us (0.77); the launches traced: 149 us -> 117 us
  blocking collectives: 18.2 us -> 0 us
  Pallas kernels: 39.4 us -> 27 us
  starting transfers between devices: 49.1 us -> 39.4 us
  waiting for transfers between devices: 23.9 us -> 32.7 us
    ppermute x15 -> x9, starting transfers between devices: 38.7 us -> 20.5 us  [shift(): return lax.ppermute(x, 'ctx', pairs)]
    all_to_all x1 -> x0, blocking collectives: 18.2 us -> none  [on_device(): lax.all_to_all(lse_send, 'ctx', split_axis=0, concat_axis=0, tiled=True)]
    pallas_call x7 -> x9, Pallas kernels: 37.3 us -> 26.2 us  [the longest x2 8.84 us: partial_wo(): pl.pallas_call(functools.partial(wo_kernel, core, group), out_shape=(sds(...]
    ppermute x10 -> x8, waiting for transfers between devices: 8.39 us -> 17.4 us  [exchange(): return lax.ppermute(x, axis, [(i, i ^ bit) for i in range(size)])]
    ppermute x10 -> x8, starting transfers between devices: 10.3 us -> 18.9 us  [exchange(): return lax.ppermute(x, axis, [(i, i ^ bit) for i in range(size)])]
    convert_element_type x9 -> x7, other arithmetic: 2.23 us -> 4.58 us  [pick(): return (one.astype(F32) + two.astype(F32)).astype(BF16)]
    unnamed x34 -> x36, local copies, waits for them, and re-layouts: 1.76 us -> 4.02 us
    ppermute x15 -> x9, waiting for transfers between devices: 15.5 us -> 15.3 us  [shift(): return lax.ppermute(x, 'ctx', pairs)]
  transfers between devices with their start and end apart: 25 -> 17, of which waited for: 5 -> 10; matrix products, arithmetic and copies ran while one was open for 9% -> 10% of each run, Pallas kernels for 13% -> 12%
where the time goes in v2:
time: 116 us; the launch traced here: 117 us
  starting transfers between devices  39.4 us (34%)
  waiting for transfers between devices  32.7 us (28%)
  Pallas kernels  27 us (23%)
  matrix products  6.62 us (6%)
  other arithmetic  5.65 us (5%)
  local copies, waits for them, and re-layouts  4.18 us (4%)
    ppermute x9, starting transfers between devices, shift(): return lax.ppermute(x, 'ctx', pairs)  20.5 us
    ppermute x8, starting transfers between devices, exchange(): return lax.ppermute(x, axis, [(i, i ^ bit) for i in range(size)])  18.9 us
    ppermute x8, waiting for transfers between devices, exchange(): return lax.ppermute(x, axis, [(i, i ^ bit) for i in range(size)])  17.4 us
    ppermute x9, waiting for transfers between devices, shift(): return lax.ppermute(x, 'ctx', pairs)  15.3 us
    pallas_call x2, Pallas kernels, partial_wo(): pl.pallas_call(functools.partial(wo_kernel, core, group), out_shape=(sds(...  8.84 us
    dot_general x1, matrix products, d_out_of(): lax.dot_general(grad, out_weight, (((1,), (1,)), ((), ())), preferred_ele...  6.62 us
    pallas_call x1, Pallas kernels, on_device(): pl.pallas_call(functools.partial(near_kernel, near_kb), grid=(tok // qb,)...  5.52 us
    convert_element_type x7, other arithmetic, pick(): return (one.astype(F32) + two.astype(F32)).astype(BF16)  4.58 us
  transfers between devices with their start and end apart: 17, of which 10 were waited for; matrix products, arithmetic and copies ran while one was open for 10% of the time, Pallas kernels for 12%

profile of v2, /device:TPU:0, one launch (start us, length us, event | category | flops | bytes accessed | tf_op | source)
XLA Modules:
  0.0 116.6 jit_solution(6533351602073250876)
XLA Ops:
  0.6 2.6 %prep.1 = (bf16[512,256]{1,0:T(8,128)(2,1)}, f32[512,128]{1,0:T(8,128)}, f32[512,128]{1,0:T(8,128)}) custom-call(s32[1,8]{1,0:T(1,128)} %lens_ref.9, f32[1,128]{1,0:T(1,128)} %constant.22.clone.freq_ref, bf16[512,128]{1,0:T(8,128)(2,1)} %bitcast.96, bf16[512,128]{1,0:T(8,128)(2,1)} %bitcast.97), custom_call_target="tpu_custom_call" | custom-call | flops 4194304 | bytes 1048576 | tf_op jit(solution)/shard_map/prep/pallas_call | solution.py:414
  3.3 5.1 %collective-permute-start = (bf16[512,256]{1,0:T(8,128)(2,1)}, bf16[512,256]{1,0:T(8,128)(2,1)S(1)}, u32[]{:S(2)}, u32[]{:S(2)}) collective-permute-start(bf16[512,256]{1,0:T(8,128)(2,1)} %get-tuple-element.34.rest_0_.kv_ref), channel_id=1, source_target_pairs={{0,2},{1,3},{2,4},{3,5},{4,6},{5,7},{8,10},{9,11},{10,12},{11,13},... | collective-permute-start | bytes 786440 | tf_op jit(solution)/shard_map/ppermute | solution.py:404
  8.4 6.6 %convolution_convert_fusion.dy_ref = bf16[512,512]{1,0:T(8,128)(2,1)} fusion(bf16[512,4096]{1,0:T(8,128)(2,1)} %param.13, bf16[1,512,4096]{2,1,0:T(8,128)(2,1)} %param.14), kind=kOutput, calls=%fused_computation | convolution fusion | flops 2147745792 | bytes 8912896 | tf_op jit(solution)/shard_map/dot_general | solution.py:425
  15.1 3.8 %collective-permute-start.2 = (bf16[512,256]{1,0:T(8,128)(2,1)S(1)}, bf16[512,256]{1,0:T(8,128)(2,1)S(1)}, u32[]{:S(2)}, u32[]{:S(2)}) collective-permute-start(bf16[512,256]{1,0:T(8,128)(2,1)S(1)} %collective-permute-done.rest_1_.rest_0_), channel_id=1, source_target_pairs={{0,2},{1,3},{2,4},{3,5},{4,6},{5,7},{8,10},{9,11},{10,12},{11,13},... | collective-permute-start | bytes 786440 | tf_op jit(solution)/shard_map/ppermute | solution.py:404
  18.8 3.4 %collective-permute-start.1 = (bf16[512,256]{1,0:T(8,128)(2,1)S(1)}, bf16[512,256]{1,0:T(8,128)(2,1)S(1)}, u32[]{:S(2)}, u32[]{:S(2)}) collective-permute-start(bf16[512,256]{1,0:T(8,128)(2,1)S(1)} %copy-done.9), channel_id=1, source_target_pairs={{0,1},{2,3},{4,5},{6,7},{8,9},{10,11},{12,13},{14,15},{16,17},{18,... | collective-permute-start | bytes 786440 | tf_op jit(solution)/shard_map/ppermute | solution.py:404
  22.4 1.7 %collective-permute-done.2.rest_3_.rest_2_ = bf16[512,256]{1,0:T(8,128)(2,1)S(1)} collective-permute-done((bf16[512,256]{1,0:T(8,128)(2,1)S(1)}, bf16[512,256]{1,0:T(8,128)(2,1)S(1)}, u32[]{:S(2)}, u32[]{:S(2)}) %collective-permute-start.2) | collective-permute-done | bytes 262176 | tf_op jit(solution)/shard_map/ppermute | solution.py:404
  25.8 3.1 %collective-permute-done.1.rest_2_.rest_1_ = bf16[512,256]{1,0:T(8,128)(2,1)S(1)} collective-permute-done((bf16[512,256]{1,0:T(8,128)(2,1)S(1)}, bf16[512,256]{1,0:T(8,128)(2,1)S(1)}, u32[]{:S(2)}, u32[]{:S(2)}) %collective-permute-start.1) | collective-permute-done | bytes 262176 | tf_op jit(solution)/shard_map/ppermute | solution.py:404
  29.0 3.9 %collective-permute-done.3.rest_4_.rest_3_ = bf16[512,256]{1,0:T(8,128)(2,1)S(1)} collective-permute-done((bf16[512,256]{1,0:T(8,128)(2,1)S(1)}, bf16[512,256]{1,0:T(8,128)(2,1)S(1)}, u32[]{:S(2)}, u32[]{:S(2)}) %collective-permute-start.3) | collective-permute-done | bytes 262176 | tf_op jit(solution)/shard_map/ppermute | solution.py:404
  32.8 2.3 %collective-permute-done.4.rest_5_.rest_4_ = bf16[512,256]{1,0:T(8,128)(2,1)S(1)} collective-permute-done((bf16[512,256]{1,0:T(8,128)(2,1)S(1)}, bf16[512,256]{1,0:T(8,128)(2,1)S(1)}, u32[]{:S(2)}, u32[]{:S(2)}) %collective-permute-start.4) | collective-permute-done | bytes 262176 | tf_op jit(solution)/shard_map/ppermute | solution.py:404
  35.2 4.5 %fwd.1 = (bf16[512,512]{1,0:T(8,128)(2,1)}, f32[4,512]{1,0:T(4,128)S(1)}, bf16[2,16,128]{2,1,0:T(8,128)(2,1)S(1)}) custom-call(s32[1,8]{1,0:T(1,128)S(1)} %copy-done.7, bf16[512,512]{1,0:T(8,128)(2,1)S(1)} %rotq.1.q_ref, bf16[512,256]{1,0:T(8,128)(2,1)S(1)} %copy-done.9, bf16[512,256]{1,0:T(8,128)(2,1)S(1)} %collective-permute-done.rest_1_.rest_0_, ...), custom_call_target="tpu_custom_call" | custom-call | flops 1342177280 | bytes 4194304 | tf_op jit(solution)/shard_map/fwd/pallas_call | solution.py:466
  40.7 4.9 %wo.3 = (bf16[2,8,256,128]{3,2,1,0:T(8,128)(2,1)}, bf16[2,8,256,128]{3,2,1,0:T(8,128)(2,1)S(1)}) custom-call(bf16[512,512]{1,0:T(8,128)(2,1)S(1)} %copy-done.2, bf16[512,4096]{1,0:T(8,128)(2,1)S(1)} %bitcast.78), custom_call_target="tpu_custom_call" | custom-call | flops 1073741824 | bytes 6291456 | tf_op jit(solution)/shard_map/wo/pallas_call | solution.py:494
  46.2 2.2 %copy-done.1 = bf16[1,512,4096]{2,1,0:T(8,128)(2,1)S(1)} copy-done((bf16[1,512,4096]{2,1,0:T(8,128)(2,1)S(1)}, bf16[1,512,4096]{2,1,0:T(8,128)(2,1)}, u32[]{:S(2)}) %copy-start.1) | copy-done | bytes 4194328
  48.4 4.0 %wo.2 = (bf16[2,8,256,128]{3,2,1,0:T(8,128)(2,1)S(1)}, bf16[2,8,256,128]{3,2,1,0:T(8,128)(2,1)S(1)}) custom-call(bf16[512,512]{1,0:T(8,128)(2,1)S(1)} %copy-done.3, bf16[512,4096]{1,0:T(8,128)(2,1)S(1)} %bitcast.79), custom_call_target="tpu_custom_call" | custom-call | flops 1073741824 | bytes 6291456 | tf_op jit(solution)/shard_map/wo/pallas_call | solution.py:494
  52.4 1.7 %add_convert_fusion.2 = (bf16[1,8,256,128]{3,2,1,0:T(8,128)(2,1)S(1)}, bf16[1,8,256,128]{3,2,1,0:T(8,128)(2,1)S(1)}) fusion(bf16[2,8,256,128]{3,2,1,0:T(8,128)(2,1)} %collective-permute-done.5, bf16[2,8,256,128]{3,2,1,0:T(8,128)(2,1)S(1)} %get-tuple-element.38), kind=kLoop, calls=%fused_computation.3 | loop fusion | flops 2097152 | bytes 3145728 | tf_op jit(solution)/shard_map/convert_element_type | solution.py:522
  60.0 1.7 %far.3 = (f32[2,128,1024]{2,1,0:T(8,128)S(1)}, bf16[2,512,256]{2,1,0:T(8,128)(2,1)S(1)}) custom-call(s32[1,8]{1,0:T(1,128)S(1)} %copy-done.7, bf16[512,512]{1,0:T(8,128)(2,1)S(1)} %rotq.1.q_ref, bf16[512,512]{1,0:T(8,128)(2,1)S(1)} %copy-done.16, bf16[512,512]{1,0:T(8,128)(2,1)S(1)} %copy-done.3, f32[4,512]{1,0:T(4,128)S(1)} %get-tuple-element.40.lse_ref, ...), custom_call_target="tpu_custom_call" | custom-call | flops 2684354560 | bytes 8388608 | tf_op jit(solution)/shard_map/far/pallas_call | solution.py:555
  61.7 3.9 %collective-permute-start.9 = (bf16[512,256]{1,0:T(8,128)(2,1)S(1)}, bf16[512,256]{1,0:T(8,128)(2,1)S(1)}, u32[]{:S(2)}, u32[]{:S(2)}) collective-permute-start(bf16[512,256]{1,0:T(8,128)(2,1)S(1)} %slice_bitcast_fusion.7), channel_id=1, source_target_pairs={{0,1},{2,3},{4,5},{6,7},{1,0},{3,2},{5,4},{7,6},{8,9},{10,11},{12,... | collective-permute-start | bytes 786440 | tf_op jit(solution)/shard_map/ppermute | solution.py:404
  68.3 2.6 %collective-permute-start.13 = (bf16[2,2,256,128]{3,2,1,0:T(8,128)(2,1)S(1)}, bf16[2,2,256,128]{3,2,1,0:T(8,128)(2,1)S(1)}, u32[]{:S(2)}, u32[]{:S(2)}) collective-permute-start(bf16[2,2,256,128]{3,2,1,0:T(8,128)(2,1)S(1)} %get-tuple-element.69), channel_id=1, source_target_pairs={{0,1},{1,0},{2,3},{3,2},{4,5},{5,4},{6,7},{7,6},{8,9},{9,8},{10,11... | collective-permute-start | bytes 786440 | tf_op jit(solution)/shard_map/ppermute | solution.py:509
  73.3 4.3 %collective-permute-done.9 = bf16[512,256]{1,0:T(8,128)(2,1)S(1)} collective-permute-done((bf16[512,256]{1,0:T(8,128)(2,1)S(1)}, bf16[512,256]{1,0:T(8,128)(2,1)S(1)}, u32[]{:S(2)}, u32[]{:S(2)}) %collective-permute-start.9) | collective-permute-done | bytes 262176 | tf_op jit(solution)/shard_map/ppermute | solution.py:404
  79.0 5.5 %near.1 = (bf16[512,512]{1,0:T(8,128)(2,1)}, f32[512,256]{1,0:T(8,128)S(1)}) custom-call(s32[1,8]{1,0:T(1,128)S(1)} %copy-done.7, bf16[512,512]{1,0:T(8,128)(2,1)S(1)} %rotq.1.q_ref, bf16[512,512]{1,0:T(8,128)(2,1)S(1)} %copy-done.16, bf16[512,512]{1,0:T(8,128)(2,1)S(1)} %copy-done.3, f32[4,512]{1,0:T(4,128)S(1)} %get-tuple-element.40.lse_ref, ...), custom_call_target="tpu_custom_call" | custom-call | flops 1073741824 | bytes 4194304 | tf_op jit(solution)/shard_map/near/pallas_call | solution.py:599
  84.6 3.1 %collective-permute-done.13 = bf16[2,2,256,128]{3,2,1,0:T(8,128)(2,1)S(1)} collective-permute-done((bf16[2,2,256,128]{3,2,1,0:T(8,128)(2,1)S(1)}, bf16[2,2,256,128]{3,2,1,0:T(8,128)(2,1)S(1)}, u32[]{:S(2)}, u32[]{:S(2)}) %collective-permute-start.13) | collective-permute-done | bytes 262176 | tf_op jit(solution)/shard_map/ppermute | solution.py:509
  88.0 5.8 %collective-permute-start.15 = (bf16[1088,128]{1,0:T(8,128)(2,1)S(1)}, bf16[1088,128]{1,0:T(8,128)(2,1)S(1)}, u32[]{:S(2)}, u32[]{:S(2)}) collective-permute-start(bf16[1088,128]{1,0:T(8,128)(2,1)S(1)} %pad_maximum_fusion.1), channel_id=1, source_target_pairs={{0,2},{1,3},{2,0},{3,1},{4,6},{5,7},{6,4},{7,5},{8,10},{9,11},{10,... | collective-permute-start | bytes 835592 | tf_op jit(solution)/shard_map/ppermute | solution.py:509
  95.2 7.8 %collective-permute-done.15 = bf16[1088,128]{1,0:T(8,128)(2,1)S(1)} collective-permute-done((bf16[1088,128]{1,0:T(8,128)(2,1)S(1)}, bf16[1088,128]{1,0:T(8,128)(2,1)S(1)}, u32[]{:S(2)}, u32[]{:S(2)}) %collective-permute-start.15) | collective-permute-done | bytes 278560 | tf_op jit(solution)/shard_map/ppermute | solution.py:509
  103.0 5.8 %collective-permute-start.16 = (bf16[640,128]{1,0:T(8,128)(2,1)S(1)}, bf16[640,128]{1,0:T(8,128)(2,1)S(1)}, u32[]{:S(2)}, u32[]{:S(2)}) collective-permute-start(bf16[640,128]{1,0:T(8,128)(2,1)S(1)} %pad_maximum_fusion.3), channel_id=1, source_target_pairs={{0,4},{1,5},{2,6},{3,7},{4,0},{5,1},{6,2},{7,3},{8,12},{9,13},{10,... | collective-permute-start | bytes 491528 | tf_op jit(solution)/shard_map/ppermute | solution.py:509
  109.7 4.2 %collective-permute-done.16 = bf16[640,128]{1,0:T(8,128)(2,1)S(1)} collective-permute-done((bf16[640,128]{1,0:T(8,128)(2,1)S(1)}, bf16[640,128]{1,0:T(8,128)(2,1)S(1)}, u32[]{:S(2)}, u32[]{:S(2)}) %collective-permute-start.16) | collective-permute-done | bytes 163872 | tf_op jit(solution)/shard_map/ppermute | solution.py:509
  (80 shorter events, 21.0 us)
Async XLA Ops:
  3.3 15.5 %copy-start.9 = (bf16[512,256]{1,0:T(8,128)(2,1)S(1)}, bf16[512,256]{1,0:T(8,128)(2,1)}, u32[]{:S(2)}) copy-start(bf16[512,256]{1,0:T(8,128)(2,1)} %get-tuple-element.34.rest_0_.kv_ref) | copy-start | bytes 786436
  3.3 22.2 %copy-start.4 = (f32[512,128]{1,0:T(8,128)S(1)}, f32[512,128]{1,0:T(8,128)}, u32[]{:S(2)}) copy-start(f32[512,128]{1,0:T(8,128)} %get-tuple-element.32.cos_ref) | copy-start | bytes 786436
  3.3 22.2 %copy-start.5 = (f32[512,128]{1,0:T(8,128)S(1)}, f32[512,128]{1,0:T(8,128)}, u32[]{:S(2)}) copy-start(f32[512,128]{1,0:T(8,128)} %get-tuple-element.33.sin_ref) | copy-start | bytes 786436
  3.3 22.2 %copy-start.6 = (bf16[1,512,512]{2,1,0:T(8,128)(2,1)S(1)}, bf16[1,512,512]{2,1,0:T(8,128)(2,1)}, u32[]{:S(2)}) copy-start(bf16[1,512,512]{2,1,0:T(8,128)(2,1)} %param.8) | copy-start | bytes 1572868
  3.3 31.8 %copy-start.7 = (s32[1,8]{1,0:T(1,128)S(1)}, s32[1,8]{1,0:T(1,128)}, u32[]{:S(2)}) copy-start(s32[1,8]{1,0:T(1,128)} %lens_ref.9) | copy-start | bytes 100
  3.3 11.7 %collective-permute-start = (bf16[512,256]{1,0:T(8,128)(2,1)}, bf16[512,256]{1,0:T(8,128)(2,1)S(1)}, u32[]{:S(2)}, u32[]{:S(2)}) collective-permute-start(bf16[512,256]{1,0:T(8,128)(2,1)} %get-tuple-element.34.rest_0_.kv_ref), channel_id=1, source_target_pairs={{0,2},{1,3},{2,4},{3,5},{4,6},{5,7},{8,10},{9,11},{10,12},{11,13},... | collective-permute-start | bytes 786440 | tf_op jit(solution)/shard_map/ppermute | solution.py:404
  15.0 24.6 %copy-start = (bf16[1,512,4096]{2,1,0:T(8,128)(2,1)S(1)}, bf16[1,512,4096]{2,1,0:T(8,128)(2,1)}, u32[]{:S(2)}) copy-start(bf16[1,512,4096]{2,1,0:T(8,128)(2,1)} %param.14) | copy-start | bytes 12582916
  15.1 9.0 %collective-permute-start.2 = (bf16[512,256]{1,0:T(8,128)(2,1)S(1)}, bf16[512,256]{1,0:T(8,128)(2,1)S(1)}, u32[]{:S(2)}, u32[]{:S(2)}) collective-permute-start(bf16[512,256]{1,0:T(8,128)(2,1)S(1)} %collective-permute-done.rest_1_.rest_0_), channel_id=1, source_target_pairs={{0,2},{1,3},{2,4},{3,5},{4,6},{5,7},{8,10},{9,11},{10,12},{11,13},... | collective-permute-start | bytes 786440 | tf_op jit(solution)/shard_map/ppermute | solution.py:404
  18.8 10.1 %collective-permute-start.1 = (bf16[512,256]{1,0:T(8,128)(2,1)S(1)}, bf16[512,256]{1,0:T(8,128)(2,1)S(1)}, u32[]{:S(2)}, u32[]{:S(2)}) collective-permute-start(bf16[512,256]{1,0:T(8,128)(2,1)S(1)} %copy-done.9), channel_id=1, source_target_pairs={{0,1},{2,3},{4,5},{6,7},{8,9},{10,11},{12,13},{14,15},{16,17},{18,... | collective-permute-start | bytes 786440 | tf_op jit(solution)/shard_map/ppermute | solution.py:404
  22.3 10.6 %collective-permute-start.3 = (bf16[512,256]{1,0:T(8,128)(2,1)S(1)}, bf16[512,256]{1,0:T(8,128)(2,1)S(1)}, u32[]{:S(2)}, u32[]{:S(2)}) collective-permute-start(bf16[512,256]{1,0:T(8,128)(2,1)S(1)} %collective-permute-done.rest_1_.rest_0_), channel_id=1, source_target_pairs={{0,1},{2,3},{4,5},{6,7},{1,0},{3,2},{5,4},{7,6},{8,9},{10,11},{12,... | collective-permute-start | bytes 786440 | tf_op jit(solution)/shard_map/ppermute | solution.py:404
  24.0 11.1 %collective-permute-start.4 = (bf16[512,256]{1,0:T(8,128)(2,1)S(1)}, bf16[512,256]{1,0:T(8,128)(2,1)S(1)}, u32[]{:S(2)}, u32[]{:S(2)}) collective-permute-start(bf16[512,256]{1,0:T(8,128)(2,1)S(1)} %collective-permute-done.2.rest_3_.rest_2_), channel_id=1, source_target_pairs={{1,0},{3,2},{5,4},{7,6},{9,8},{11,10},{13,12},{15,14},{17,16},{19,... | collective-permute-start | bytes 786440 | tf_op jit(solution)/shard_map/ppermute | solution.py:404
  45.6 6.8 %collective-permute-start.5 = (bf16[2,8,256,128]{3,2,1,0:T(8,128)(2,1)}, bf16[2,8,256,128]{3,2,1,0:T(8,128)(2,1)}, u32[]{:S(2)}, u32[]{:S(2)}) collective-permute-start(bf16[2,8,256,128]{3,2,1,0:T(8,128)(2,1)} %get-tuple-element.39), channel_id=1, source_target_pairs={{0,8},{8,0},{16,24},{24,16},{1,9},{9,1},{17,25},{25,17},{2,10},{10... | collective-permute-start | bytes 3145736 | tf_op jit(solution)/shard_map/ppermute | solution.py:509
  45.7 10.0 %collective-permute-start.7 = (bf16[2,8,256,128]{3,2,1,0:T(8,128)(2,1)S(1)}, bf16[2,8,256,128]{3,2,1,0:T(8,128)(2,1)}, u32[]{:S(2)}, u32[]{:S(2)}) collective-permute-start(bf16[2,8,256,128]{3,2,1,0:T(8,128)(2,1)S(1)} %get-tuple-element.45), channel_id=1, source_target_pairs={{0,8},{8,0},{16,24},{24,16},{1,9},{9,1},{17,25},{25,17},{2,10},{10... | collective-permute-start | bytes 3145736 | tf_op jit(solution)/shard_map/ppermute | solution.py:509
  54.1 14.0 %collective-permute-start.6 = (bf16[2,2,2,256,128]{4,3,1,0,2:T(8,128)(2,1)S(1)}, bf16[2,2,2,256,128]{4,3,1,0,2:T(8,128)(2,1)S(1)}, u32[]{:S(2)}, u32[]{:S(2)}) collective-permute-start(bf16[2,2,2,256,128]{4,3,1,0,2:T(8,128)(2,1)S(1)} %copy.15), channel_id=1, source_target_pairs={{0,16},{8,24},{16,0},{24,8},{1,17},{9,25},{17,1},{25,9},{2,18},{10... | collective-permute-start | bytes 1572872 | tf_op jit(solution)/shard_map/ppermute | solution.py:509
  57.0 15.0 %collective-permute-start.8 = (bf16[2080,128]{1,0:T(8,128)(2,1)S(1)}, bf16[2080,128]{1,0:T(8,128)(2,1)S(1)}, u32[]{:S(2)}, u32[]{:S(2)}) collective-permute-start(bf16[2080,128]{1,0:T(8,128)(2,1)S(1)} %pad_maximum_fusion), channel_id=1, source_target_pairs={{0,1},{1,0},{2,3},{3,2},{4,5},{5,4},{6,7},{7,6},{8,9},{9,8},{10,11... | collective-permute-start | bytes 1597448 | tf_op jit(solution)/shard_map/ppermute | solution.py:509
  61.7 15.9 %collective-permute-start.9 = (bf16[512,256]{1,0:T(8,128)(2,1)S(1)}, bf16[512,256]{1,0:T(8,128)(2,1)S(1)}, u32[]{:S(2)}, u32[]{:S(2)}) collective-permute-start(bf16[512,256]{1,0:T(8,128)(2,1)S(1)} %slice_bitcast_fusion.7), channel_id=1, source_target_pairs={{0,1},{2,3},{4,5},{6,7},{1,0},{3,2},{5,4},{7,6},{8,9},{10,11},{12,... | collective-permute-start | bytes 786440 | tf_op jit(solution)/shard_map/ppermute | solution.py:404
  65.7 28.1 %collective-permute-start.11 = (bf16[512,256]{1,0:T(8,128)(2,1)S(1)}, bf16[512,256]{1,0:T(8,128)(2,1)S(1)}, u32[]{:S(2)}, u32[]{:S(2)}) collective-permute-start(bf16[512,256]{1,0:T(8,128)(2,1)S(1)} %slice_bitcast_fusion.6), channel_id=1, source_target_pairs={{0,1},{2,3},{4,5},{6,7},{1,0},{3,2},{5,4},{7,6},{8,9},{10,11},{12,... | collective-permute-start | bytes 786440 | tf_op jit(solution)/shard_map/ppermute | solution.py:404
  68.3 19.4 %collective-permute-start.13 = (bf16[2,2,256,128]{3,2,1,0:T(8,128)(2,1)S(1)}, bf16[2,2,256,128]{3,2,1,0:T(8,128)(2,1)S(1)}, u32[]{:S(2)}, u32[]{:S(2)}) collective-permute-start(bf16[2,2,256,128]{3,2,1,0:T(8,128)(2,1)S(1)} %get-tuple-element.69), channel_id=1, source_target_pairs={{0,1},{1,0},{2,3},{3,2},{4,5},{5,4},{6,7},{7,6},{8,9},{9,8},{10,11... | collective-permute-start | bytes 786440 | tf_op jit(solution)/shard_map/ppermute | solution.py:509
  72.2 15.5 %collective-permute-start.14 = (bf16[2,2,256,128]{3,2,1,0:T(8,128)(2,1)S(1)}, bf16[2,2,256,128]{3,2,1,0:T(8,128)(2,1)S(1)}, u32[]{:S(2)}, u32[]{:S(2)}) collective-permute-start(bf16[2,2,256,128]{3,2,1,0:T(8,128)(2,1)S(1)} %get-tuple-element.71), channel_id=1, source_target_pairs={{0,16},{8,24},{16,0},{24,8},{1,17},{9,25},{17,1},{25,9},{2,18},{10... | collective-permute-start | bytes 786440 | tf_op jit(solution)/shard_map/ppermute | solution.py:509
  77.7 16.0 %collective-permute-start.10 = (bf16[512,256]{1,0:T(8,128)(2,1)S(1)}, bf16[512,256]{1,0:T(8,128)(2,1)S(1)}, u32[]{:S(2)}, u32[]{:S(2)}) collective-permute-start(bf16[512,256]{1,0:T(8,128)(2,1)S(1)} %fusion.1), channel_id=1, source_target_pairs={{2,0},{3,1},{4,2},{5,3},{6,4},{7,5},{10,8},{11,9},{12,10},{13,11},... | collective-permute-start | bytes 786440 | tf_op jit(solution)/shard_map/ppermute | solution.py:404
  84.6 29.3 %copy-start.8 = (s32[1,64]{1,0:T(1,128)S(1)}, s32[1,64]{1,0:T(1,128)}, u32[]{:S(2)}) copy-start(s32[1,64]{1,0:T(1,128)} %param.12) | copy-start | bytes 772
  88.0 15.0 %collective-permute-start.15 = (bf16[1088,128]{1,0:T(8,128)(2,1)S(1)}, bf16[1088,128]{1,0:T(8,128)(2,1)S(1)}, u32[]{:S(2)}, u32[]{:S(2)}) collective-permute-start(bf16[1088,128]{1,0:T(8,128)(2,1)S(1)} %pad_maximum_fusion.1), channel_id=1, source_target_pairs={{0,2},{1,3},{2,0},{3,1},{4,6},{5,7},{6,4},{7,5},{8,10},{9,11},{10,... | collective-permute-start | bytes 835592 | tf_op jit(solution)/shard_map/ppermute | solution.py:509
  93.9 15.0 %collective-permute-start.12 = (bf16[512,256]{1,0:T(8,128)(2,1)S(1)}, bf16[512,256]{1,0:T(8,128)(2,1)S(1)}, u32[]{:S(2)}, u32[]{:S(2)}) collective-permute-start(bf16[512,256]{1,0:T(8,128)(2,1)S(1)} %fusion.3), channel_id=1, source_target_pairs={{2,0},{3,1},{4,2},{5,3},{6,4},{7,5},{10,8},{11,9},{12,10},{13,11},... | collective-permute-start | bytes 786440 | tf_op jit(solution)/shard_map/ppermute | solution.py:404
  103.0 10.8 %collective-permute-start.16 = (bf16[640,128]{1,0:T(8,128)(2,1)S(1)}, bf16[640,128]{1,0:T(8,128)(2,1)S(1)}, u32[]{:S(2)}, u32[]{:S(2)}) collective-permute-start(bf16[640,128]{1,0:T(8,128)(2,1)S(1)} %pad_maximum_fusion.3), channel_id=1, source_target_pairs={{0,4},{1,5},{2,6},{3,7},{4,0},{5,1},{6,2},{7,3},{8,12},{9,13},{10,... | collective-permute-start | bytes 491528 | tf_op jit(solution)/shard_map/ppermute | solution.py:509
  (10 other events, 66.9 us)

commit v3 on v2

--- a/solution.py
+++ b/solution.py
@@ -10,12 +10,14 @@
 from jax.experimental.pallas import tpu as pltpu
 from jax.sharding import PartitionSpec as P
 
+
 HEAD = 128
 WIN = 4096
 NEG = -1e30
 LOG2E = math.log2(math.e)
 LN2 = math.log(2.0)
 SCALE = 1.0 / math.sqrt(HEAD)
+FWD_MIB, WO_MIB, FAR_MIB, NEAR_MIB = 16, 14, 20, 14
 F32 = jnp.float32
 BF16 = jnp.bfloat16
 
@@ -169,7 +171,7 @@
 
 def fwd_kernel(n_refs, back, kb, lens_ref, q_ref, *rest):
     kv_refs = rest[:n_refs]
-    o_ref, lse_ref, pack_ref, kv_scr, sem = rest[n_refs:]
+    o_ref, keep_ref, lse_ref, pack_ref, kv_scr, sem = rest[n_refs:]
     step = pl.program_id(0)
     qb, width = q_ref.shape
     heads = width // HEAD
@@ -208,7 +210,9 @@
     out = acc / total
     for h in range(heads):
         lse_ref[h : h + 1, :] = lse[:, h * qb : (h + 1) * qb]
-        o_ref[:, h * HEAD : (h + 1) * HEAD] = jnp.transpose(out[:, h * qb : (h + 1) * qb]).astype(BF16)
+        part = jnp.transpose(out[:, h * qb : (h + 1) * qb]).astype(BF16)
+        o_ref[:, h * HEAD : (h + 1) * HEAD] = part
+        keep_ref[:, h * HEAD : (h + 1) * HEAD] = part
     lines = jnp.concatenate(
         [lse[:, c * HEAD : (c + 1) * HEAD] for c in range(rows // HEAD)], axis=0
     )
@@ -217,22 +221,24 @@
     pack_ref[0] = jnp.concatenate([coarse, fine], axis=0)
 
 
-def bwd_core(lens_ref, q_ref, dy_ref, o_ref, lse_ref, kv, base, kb, dk_scr, dv_scr, dq):
+def delta_of(dy_ref, o_ref):
+    prod = stack_heads(dy_ref).astype(F32) * stack_heads(o_ref).astype(F32)
+    qb = dy_ref.shape[0]
+    return [
+        jnp.sum(jnp.transpose(prod[i : i + qb]), axis=0, keepdims=True)
+        for i in range(0, prod.shape[0], qb)
+    ]
+
+
+def bwd_core(lens_ref, q_ref, dy_ref, delta_ref, lse_ref, kv, base, kb, dk_scr, dv_scr, dq):
     qb, width = q_ref.shape
     heads = width // HEAD
     tok = qb * pl.num_programs(0)
     dev, _ = place()
     first = dev * tok + pl.program_id(0) * qb
     q, dy = stack_heads(q_ref), stack_heads(dy_ref)
-    prod = dy.astype(F32) * stack_heads(o_ref).astype(F32)
-    delta = jnp.concatenate(
-        [
-            jnp.sum(jnp.transpose(prod[h * qb : (h + 1) * qb, :]), axis=0, keepdims=True)
-            for h in range(heads)
-        ],
-        axis=1,
-    )
     lse = jnp.concatenate([lse_ref[h : h + 1, :] for h in range(heads)], axis=1) * LOG2E
+    delta = jnp.concatenate([delta_ref[h : h + 1, :] for h in range(heads)], axis=1)
     low, high = query_bounds(lens_ref, first, qb, heads)
     factor = SCALE * LOG2E
 
@@ -254,7 +260,14 @@
 def far_kernel(n_refs, back, lo, has_dq, kb, lens_ref, q_ref, dy_ref, o_ref, lse_ref, *rest):
     kv_refs = rest[:n_refs]
     dqin_ref = rest[n_refs] if has_dq else None
-    dq_ref, far_ref, kv_scr, dk_scr, dv_scr, sem = rest[n_refs + has_dq :]
+    dq_ref, far_ref, *rest = rest[n_refs + has_dq :]
+    if has_dq:
+        delta_ref = o_ref
+    else:
+        delta_ref, *rest = rest
+        for h, line in enumerate(delta_of(dy_ref, o_ref)):
+            delta_ref[h : h + 1, :] = line
+    kv_scr, dk_scr, dv_scr, sem = rest
     tok = kv_refs[0].shape[0]
     dev, n_ctx = place()
     step = pl.program_id(0)
@@ -268,7 +281,7 @@
     base = (dev - back + lo) * tok
     dq = dqin_ref[0] if has_dq else jnp.zeros(dq_ref.shape[1:], F32)
     dq_ref[0] = bwd_core(
-        lens_ref, q_ref, dy_ref, o_ref, lse_ref, kv_scr, base, kb, dk_scr, dv_scr, dq
+        lens_ref, q_ref, dy_ref, delta_ref, lse_ref, kv_scr, base, kb, dk_scr, dv_scr, dq
     )
 
     @pl.when(step == pl.num_programs(0) - 1)
@@ -278,7 +291,7 @@
             far_ref[r, :, HEAD:] = dv_scr[r * tok : (r + 1) * tok, :].astype(BF16)
 
 
-def near_kernel(kb, lens_ref, q_ref, dy_ref, o_ref, lse_ref, dqin_ref, kv_ref, cos_ref, sin_ref,
+def near_kernel(kb, lens_ref, q_ref, dy_ref, delta_ref, lse_ref, dqin_ref, kv_ref, cos_ref, sin_ref,
                 dq_ref, own_ref, dk_scr, dv_scr):
     tok = kv_ref.shape[0]
     dev, _ = place()
@@ -291,7 +304,7 @@
         dv_scr[...] = jnp.zeros_like(dv_scr)
 
     dq = bwd_core(
-        lens_ref, q_ref, dy_ref, o_ref, lse_ref, kv_ref, dev * tok, kb, dk_scr, dv_scr, dqin_ref[0]
+        lens_ref, q_ref, dy_ref, delta_ref, lse_ref, kv_ref, dev * tok, kb, dk_scr, dv_scr, dqin_ref[0]
     )
     for h in range(q_ref.shape[1] // HEAD):
         part = jnp.transpose(dq[:, h * qb : (h + 1) * qb]) * SCALE
@@ -303,31 +316,42 @@
         own_ref[:, HEAD:] = dv_scr[...]
 
 
-def wo_kernel(core, group, a_ref, g_ref, *rest):
-    outs, (g_scr, sem) = rest[:-2], rest[-2:]
-    dev, _ = place()
+def wo_kernel(core, a_ref, g_ref, *rest):
+    g_scr, sem = rest[-2:]
+    outs, other_ref = rest[:4], (rest[4] if core else None)
+    dev, n_ctx = place()
     dp = lax.axis_index("dp").astype(jnp.int32)
-    n_half, n_ctx, rows, col = outs[0].shape
-    wide = group * col
-    groups = n_ctx // group
+    _, wide = g_scr.shape[1:]
+    n_half = g_scr.shape[0]
+    col = wide // n_ctx
+    rows = outs[0].shape[1]
+
+    def fetch(i, to, bit, dst, where):
+        start = (((2 * i + bit) ^ dp) * n_ctx + (to ^ dev)) * col
+        src = g_ref.at[:, pl.ds(pl.multiple_of(start, col), col)]
+        return pltpu.make_async_copy(src, dst.at[i, :, pl.ds(to * col, col)], sem.at[where, i * n_ctx + to])
+
+    def each(what, *args):
+        for i in range(n_half):
+            for to in range(n_ctx):
+                getattr(fetch(i, to, *args), what)()
+
+    if core:
+        each("start", 1, g_scr, 0)
+        each("start", 0, other_ref, 1)
     at = jnp.transpose(a_ref[...])
-
-    def fetch(n):
-        i, p = divmod(n, groups)
-        block = ((2 * i + core) ^ dp) * groups + (p ^ (dev // group))
-        start = pl.multiple_of(block * wide, wide)
-        return pltpu.make_async_copy(g_ref.at[:, pl.ds(start, wide)], g_scr.at[n], sem.at[n])
-
-    for n in range(n_half * groups):
-        fetch(n).start()
-    for n in range(n_half * groups):
-        i, p = divmod(n, groups)
-        fetch(n).wait()
-        res = jnp.dot(at, g_scr[n], preferred_element_type=F32).astype(BF16)
-        for j in range(group):
-            to = p * group + (j ^ (dev & (group - 1)))
-            for c, out_ref in enumerate(outs):
-                out_ref[i, to] = res[c * rows : (c + 1) * rows, j * col : (j + 1) * col]
+    for i in range(n_half):
+        if core:
+            for to in range(n_ctx):
+                fetch(i, to, 1, g_scr, 0).wait()
+        block = g_scr[i] if core else g_ref[i]
+        res = jnp.dot(at, block, preferred_element_type=F32).astype(BF16)
+        for to in range(n_ctx):
+            part = res[:, to * col : (to + 1) * col]
+            outs[i & 1][(i >> 1) * n_ctx + to] = part[:rows]
+            outs[2 + ((to >> 1) & 1)][i * (n_ctx // 2) + ((to >> 2) << 1 | (to & 1))] = part[rows:]
+    if core:
+        each("wait", 0, other_ref, 1)
 
 
 def home_kernel(n_in, own_ref, cos_ref, sin_ref, *rest):
@@ -339,30 +363,35 @@
     dv_ref[...] = total[:, HEAD:].astype(BF16)
 
 
-def owner_kernel(owner_ref, lse_ref, out_ref):
+def final_kernel(bits, owner_ref, one_ref, recv_ref, lse_ref, wgrad_ref, out_ref, all_scr):
+    size = one_ref.shape[0]
+    wgrad_ref[...] = one_ref[...].astype(F32) + recv_ref[:size].astype(F32)
     dev, n_ctx = place()
-    heads = out_ref.shape[1]
-    tok = out_ref.shape[0]
+    heads, tok = out_ref.shape
     block_len = tok // n_ctx
-    halves = lse_ref.shape[1]
-    chunks = tok // halves // HEAD
-    for i in range(n_ctx):
-        c = dev ^ i
+    count = lse_ref.shape[0]
+    all_scr[:count] = lse_ref[...].astype(F32)
+    all_scr[count:] = recv_ref[size:].astype(F32)
+    each = 2 * count // n_ctx
+    chunks = tok // 2 // HEAD
+    of_half = heads * chunks
+    for c in range(n_ctx):
+        away = dev ^ c
+        index = jnp.int32(0)
+        for k, b in enumerate(bits):
+            index = index | (((away >> b) & 1) << k)
+        raw = all_scr[pl.ds(pl.multiple_of(index * each, each), each), :]
         mine = jnp.zeros((heads, block_len), F32)
-        lines = lse_ref[i].astype(F32)
-        lines = lines[:, : heads * chunks] + lines[:, heads * chunks :]
         for s in range(n_ctx):
-            half, rest = divmod(s * block_len, tok // halves)
+            half, rest = divmod(s * block_len, tok // 2)
             chunk, lane = divmod(rest, HEAD)
-            part = jnp.concatenate(
-                [
-                    lines[half, h * chunks + chunk : h * chunks + chunk + 1, lane : lane + block_len]
-                    for h in range(heads)
-                ],
-                axis=0,
-            )
-            mine = jnp.where(owner_ref[c * n_ctx + s] == dev, part, mine)
-        out_ref[pl.ds(pl.multiple_of(c * block_len, block_len), block_len), :] = jnp.transpose(mine)
+            parts = []
+            for h in range(heads):
+                row = half * 2 * of_half + h * chunks + chunk
+                line = raw[row : row + 1] + raw[row + of_half : row + of_half + 1]
+                parts.append(line[:, lane : lane + block_len])
+            mine = jnp.where(owner_ref[c * n_ctx + s] == dev, jnp.concatenate(parts, axis=0), mine)
+        out_ref[:, c * block_len : (c + 1) * block_len] = mine
 
 
 SMEM_SPEC = pl.BlockSpec(memory_space=pltpu.SMEM)
@@ -440,12 +469,11 @@
     if paired:
         a1 = shift(kv_home, hop)
         e1 = shift(kv_home, up)
-        d_out = d_out_of(out_grad[0])
-        a1 = after(a1, d_out)
+        q_rot = rotated_queries(queries[0])
         s1 = shift(a1, swap)
         a2 = shift(a1, hop)
-        q_rot = rotated_queries(queries[0])
         o3 = shift(a2, down)
+        d_out = d_out_of(after(out_grad[0], a2))
         blocks = [kv_home, a1, e1, a2, s1, o3]
     else:
         blocks = [kv_home] + [
@@ -463,21 +491,22 @@
     dq_spec = pl.BlockSpec((1, HEAD, heads * qb), lambda i: (i, 0, 0))
     pairs = heads * tok * (tok + reach) // 2
     pack_rows = 2 * heads * qb // HEAD
-    attn, lse, pack = pl.pallas_call(
+    attn_out, attn, lse, pack = pl.pallas_call(
         functools.partial(fwd_kernel, len(blocks), back, kb),
         grid=(tok // qb,),
         out_shape=(
+            sds((tok, width), BF16),
             sds((tok, width), BF16),
             sds((heads, tok), F32),
             sds((tok // qb, pack_rows, HEAD), BF16),
         ),
         in_specs=[SMEM_SPEC, tok_spec] + [ANY_SPEC] * len(blocks),
-        out_specs=(tok_spec, lse_spec, pl.BlockSpec((1, pack_rows, HEAD), lambda i: (i, 0, 0))),
+        out_specs=(tok_spec, tok_spec, lse_spec, pl.BlockSpec((1, pack_rows, HEAD), lambda i: (i, 0, 0))),
         scratch_shapes=[
             pltpu.VMEM((n_keys, 2 * HEAD), BF16),
             pltpu.SemaphoreType.DMA((len(blocks),)),
         ],
-        compiler_params=params(20, "arbitrary"),
+        compiler_params=params(FWD_MIB, "arbitrary"),
         cost_estimate=cost(4 * pairs * HEAD, 4 << 20, pairs),
         name="fwd",
     )(doc_lengths, q_rot, *blocks)
@@ -485,25 +514,38 @@
     col = d_model // (n_dp * n_ctx)
     bits_dp = n_dp.bit_length() - 1
     bits_ctx = n_ctx.bit_length() - 1
-    group = min(n_ctx, max(1, 256 // col))
-    colors = 2
-    rows = width // colors
-    steps = n_dp // 2 * (n_ctx // group)
-
-    def partial_wo(core):
+    rows = width // 2
+    n_half = n_dp // 2
+    wide = n_ctx * col
+
+    def shapes_of(sizes):
+        return [sds((size, rows, col), BF16) for size in sizes]
+
+    sizes = [n_half // 2 * n_ctx] * 2 + [n_half * n_ctx // 2] * 2
+
+    def partial_wo(core, grads):
         return pl.pallas_call(
-            functools.partial(wo_kernel, core, group),
-            out_shape=(sds((n_dp // 2, n_ctx, rows, col), BF16),) * colors,
-            in_specs=[VMEM_SPEC, ANY_SPEC],
-            out_specs=(VMEM_SPEC,) * colors,
+            functools.partial(wo_kernel, core),
+            out_shape=shapes_of(sizes) + ([sds((n_half, tok, wide), BF16)] if core else []),
+            in_specs=[VMEM_SPEC, ANY_SPEC if core else VMEM_SPEC],
+            out_specs=[VMEM_SPEC] * (4 + core),
             scratch_shapes=[
-                pltpu.VMEM((steps, tok, group * col), BF16),
-                pltpu.SemaphoreType.DMA((steps,)),
+                pltpu.VMEM((n_half, tok, wide), BF16),
+                pltpu.SemaphoreType.DMA((2, n_half * n_ctx)),
             ],
-            compiler_params=params(16),
+            compiler_params=params(WO_MIB),
             cost_estimate=cost(tok * width * d_model, 6 << 20),
-            name="wo",
-        )(attn, out_grad[0])
+        )(attn, grads)
+
+    def partial_wo_narrow(core):
+        grads = out_grad[0].reshape(tok, n_dp, n_ctx, col)
+        grads = jnp.take(grads, (2 * jnp.arange(n_half) + core) ^ dp, axis=1)
+        grads = jnp.take(grads, jnp.arange(n_ctx) ^ dev, axis=2)
+        res = jnp.einsum("tr,tabc->abrc", attn, grads, preferred_element_type=F32).astype(BF16)
+        upper = res[:, :, :rows].reshape(n_half // 2, 2, n_ctx, rows, col)
+        lower = res[:, :, rows:].reshape(n_half, n_ctx // 4, 2, 2, rows, col)
+        outs = [upper[:, w].reshape(-1, rows, col) for w in range(2)]
+        return outs + [lower[:, :, w].reshape(-1, rows, col) for w in range(2)]
 
     def exchange(x, axis, bit, size):
         return lax.ppermute(x, axis, [(i, i ^ bit) for i in range(size)])
@@ -512,85 +554,99 @@
     lead = [("dp", b) for b in range(bits_dp - 1, 0, -1)]
     lead += [("ctx", b) for b in range(bits_ctx - 1, -1, -1)]
 
+    def move(x, axis):
+        return exchange(x, axis[0], 1 << axis[1], size_of[axis[0]])
+
     class Parts:
-        def __init__(self, one, two, left):
-            self.one, self.two, self.left = one, two, left
+        def __init__(self, addends, left):
+            self.left = list(left)
+            self.addends = [x.reshape((2,) * len(self.left) + x.shape[-2:]) for x in addends]
 
         def pick(self, axis, which):
             at = self.left.index(axis)
-            one, two = [lax.index_in_dim(x, which, at, keepdims=False) for x in (self.one, self.two)]
-            return (one.astype(F32) + two.astype(F32)).astype(BF16)
+            picked = [lax.index_in_dim(x, which, at, keepdims=False) for x in self.addends]
+            return functools.reduce(jnp.add, [x.astype(F32) for x in picked]).astype(BF16)
 
         def step(self, axis, recv):
-            left = [a for a in self.left if a != axis]
-            return Parts(self.pick(axis, 0), recv, left)
-
-    def move(x, axis):
-        return exchange(x, axis[0], 1 << axis[1], size_of[axis[0]])
-
-    wo_send = partial_wo(1)
-    wo_recv = [exchange(x, "dp", 1, n_dp) for x in wo_send]
-    wo_keep = partial_wo(0)
-    shape = (2,) * len(lead) + (rows, col)
-    color = [Parts(k.reshape(shape), r.reshape(shape), lead) for k, r in zip(wo_keep, wo_recv)]
-    first_dp = [("dp", b) for b in range(1, bits_dp)]
-    ctx_axes = [("ctx", b) for b in range(bits_ctx)]
-    orders = [first_dp + ctx_axes[:1], ctx_axes[:1] + first_dp]
+            at = self.left.index(axis)
+            kept = [lax.index_in_dim(x, 0, at, keepdims=False) for x in self.addends]
+            return Parts(kept + [recv], [a for a in self.left if a != axis])
+
+    firsts = [("dp", 1), ("ctx", 1)]
+    if col % HEAD == 0:
+        *wo_send, grads_keep = partial_wo(1, out_grad[0])
+        wo_recv = [None] * 4
+        for n in (1, 3, 0, 2):
+            wo_recv[n] = exchange(wo_send[n], "dp", 1, n_dp)
+        wo_keep = partial_wo(0, grads_keep)
+    else:
+        wo_recv = [exchange(x, "dp", 1, n_dp) for x in partial_wo_narrow(1)]
+        wo_keep = partial_wo_narrow(0)
+    lefts = [[a for a in lead if a != firsts[c]] for c in range(2)]
+    sends = []
+    color = []
+    for c in range(2):
+        kept, sent = [Parts([wo_keep[2 * c + w], wo_recv[2 * c + w]], lefts[c]) for w in range(2)]
+        color.append(kept)
+        total = functools.reduce(jnp.add, [x.astype(F32) for x in sent.addends]).astype(BF16)
+        sends.append(total)
 
     lines = pack.reshape(-1, col)
 
-    def move_with_lse(x, axis, lse_of):
-        size = x.size // col
-        out = move(jnp.concatenate([x.reshape(size, col), lse_of], axis=0), axis)
-        return out[:size].reshape(x.shape), jnp.concatenate([lse_of, out[size:]], axis=0)
-
-    sends = [color[c].pick(orders[c][0], 1) for c in range(colors)]
-    recvs = [move(sends[0], orders[0][0])]
-    recv, lines = move_with_lse(sends[1], orders[1][0], lines)
-    recvs.append(recv)
-    color = [color[c].step(orders[c][0], recvs[c]) for c in range(colors)]
-
-    def backward_far(lo, hi, lse_in, dq_in):
+    def with_lse(x, lse_of):
+        return jnp.concatenate([x.reshape(-1, col), lse_of], axis=0)
+
+    recv = move(sends[0], firsts[0])
+    color[0] = Parts(color[0].addends + [recv], lefts[0])
+    size = sends[1].size // col
+    recv = move(with_lse(sends[1], lines), firsts[1])
+    color[1] = Parts(color[1].addends + [recv[:size].reshape(sends[1].shape)], lefts[1])
+    lines = jnp.concatenate([lines, recv[size:]], axis=0)
+
+    def backward_far(lo, hi, lse_in, third, dq_in):
         count = hi - lo
+        new = [] if dq_in else [(sds((heads, tok), F32), lse_spec)]
         return pl.pallas_call(
             functools.partial(far_kernel, len(blocks) - 1, back, lo, len(dq_in), kb),
             grid=(tok // qb,),
-            out_shape=(sds((tok // qb, HEAD, heads * qb), F32), sds((count, tok, 2 * HEAD), BF16)),
-            in_specs=[SMEM_SPEC, tok_spec, tok_spec, tok_spec, lse_spec]
+            out_shape=[sds((tok // qb, HEAD, heads * qb), F32), sds((count, tok, 2 * HEAD), BF16)]
+            + [n[0] for n in new],
+            in_specs=[SMEM_SPEC, tok_spec, tok_spec, lse_spec if dq_in else tok_spec, lse_spec]
             + [ANY_SPEC] * (len(blocks) - 1)
             + [dq_spec] * len(dq_in),
-            out_specs=(dq_spec, pl.BlockSpec((count, tok, 2 * HEAD), lambda i: (0, 0, 0))),
+            out_specs=[dq_spec, pl.BlockSpec((count, tok, 2 * HEAD), lambda i: (0, 0, 0))]
+            + [n[1] for n in new],
             scratch_shapes=[
                 pltpu.VMEM((count * tok, 2 * HEAD), BF16),
                 pltpu.VMEM((count * tok, HEAD), F32),
                 pltpu.VMEM((count * tok, HEAD), F32),
                 pltpu.SemaphoreType.DMA((len(blocks) - 1,)),
             ],
-            compiler_params=params(28, "arbitrary"),
+            compiler_params=params(FAR_MIB, "arbitrary"),
             cost_estimate=cost(8 * pairs * HEAD, 8 << 20, pairs),
-            name="far",
-        )(doc_lengths, q_rot, d_out, attn, lse_in, *blocks[1:], *dq_in)
+        )(doc_lengths, q_rot, d_out, third, lse_in, *blocks[1:], *dq_in)
 
     def plus(*xs):
         return functools.reduce(jnp.add, [x.astype(F32) for x in xs]).astype(BF16)
 
     lse_b = after(lse, *sends)
     if paired:
-        dq_far, (d4, d3) = backward_far(0, 2, lse_b, [])
+        dq_far, (d4, d3), delta = backward_far(0, 2, lse_b, attn, [])
         r3 = shift(d3, swap)
-        dq_far, (d2, d1) = backward_far(2, 4, lse_b, [dq_far])
+        dq_far, (d2, d1) = backward_far(2, 4, lse_b, delta, [dq_far])
         none = jnp.zeros_like(r3)
         sum4 = plus(d4, jnp.where(odd, r3, none))
         b2 = shift(sum4, hop_back)
         r1 = shift(d1, swap)
     else:
-        dq_far, far = backward_far(0, back, lse_b, [])
-
-    for c in range(colors):
-        color[c].two = after(color[c].two, dq_far)
+        dq_far, far, delta = backward_far(0, back, lse_b, attn, [])
+
+    seconds = [firsts[1], firsts[0]]
+    extra = [a for a in lead if a[0] == "dp" and a not in firsts]
     sends = []
-    for c in range(colors):
-        for axis in orders[c][1:]:
+    for c in range(2):
+        color[c].addends[-1] = after(color[c].addends[-1], dq_far)
+        for axis in [seconds[c]] + extra:
             sends.append(color[c].pick(axis, 1))
             color[c] = color[c].step(axis, move(sends[-1], axis))
 
@@ -600,24 +656,34 @@
         functools.partial(near_kernel, near_kb),
         grid=(tok // qb,),
         out_shape=(sds((tok, width), BF16), sds((tok, 2 * HEAD), F32)),
-        in_specs=[SMEM_SPEC, tok_spec, tok_spec, tok_spec, lse_spec, dq_spec, VMEM_SPEC, table_spec, table_spec],
+        in_specs=[SMEM_SPEC, tok_spec, tok_spec, lse_spec, lse_spec, dq_spec, VMEM_SPEC, table_spec, table_spec],
         out_specs=(tok_spec, pl.BlockSpec((tok, 2 * HEAD), lambda i: (0, 0))),
         scratch_shapes=[pltpu.VMEM((tok, HEAD), F32), pltpu.VMEM((tok, HEAD), F32)],
-        compiler_params=params(20, "arbitrary"),
+        compiler_params=params(NEAR_MIB, "arbitrary"),
         cost_estimate=cost(8 * heads * tok * tok * HEAD, 4 << 20, heads * tok * tok),
         name="near",
-    )(doc_lengths, q_rot, d_out, attn, lse, dq_near, kv_home, cos, sin)
-
-    left = color[0].left
-    join = len(left)
-    one = jnp.concatenate([color[c].one for c in range(colors)], axis=join)
-    two = jnp.concatenate([color[c].two for c in range(colors)], axis=join)
-    both = Parts(one, two, left)
-    for axis in ctx_axes[1:]:
-        send = after(both.pick(axis, 1), own)
-        recv, lines = move_with_lse(send, axis, lines)
-        both = both.step(axis, recv)
-    wgrad = both.one.astype(F32) + both.two.astype(F32)
+    )(doc_lengths, q_rot, d_out, delta, lse, dq_near, kv_home, cos, sin)
+
+    ctx_axes = [("ctx", 0)] + [("ctx", b) for b in range(2, bits_ctx)]
+    lse_bits = [1, 0] + list(range(2, bits_ctx))
+    both = None
+    for axis in ctx_axes:
+        if both is None:
+            pieces = [jnp.concatenate([color[c].pick(axis, w) for c in range(2)], axis=-2) for w in range(2)]
+            left = [a for a in color[0].left if a != axis]
+            send = after(pieces[1], own)
+            kept = [pieces[0]]
+        else:
+            send = both.pick(axis, 1)
+            left = [a for a in both.left if a != axis]
+            at = both.left.index(axis)
+            kept = [lax.index_in_dim(x, 0, at, keepdims=False) for x in both.addends]
+        size = send.size // col
+        recv = move(with_lse(send, lines), axis)
+        if axis != ctx_axes[-1]:
+            both = Parts(kept + [recv[:size].reshape(send.shape)], left)
+            lines = jnp.concatenate([lines, recv[size:]], axis=0)
+    last = functools.reduce(jnp.add, [x.astype(F32) for x in kept]).astype(BF16)
 
     if paired:
         sum2 = plus(d2, b2, jnp.where(odd, r1, r3))
@@ -636,17 +702,25 @@
         name="home",
     )(own, cos, sin, *arrived)
 
-    owner_lse = pl.pallas_call(
-        owner_kernel,
-        out_shape=sds((tok, heads), F32),
-        in_specs=[SMEM_SPEC, VMEM_SPEC],
-        out_specs=VMEM_SPEC,
-        compiler_params=params(4),
-        cost_estimate=cost(1 << 18, 1 << 18),
-        name="owned",
-    )(owner[0], lines.reshape(n_ctx, tok // qb, pack_rows, HEAD))
-
-    return (attn[None], q_grad[None], k_grad[None], v_grad[None], wgrad, owner_lse[None, None])
+    if col != HEAD:
+        tail_rows = recv[width:].reshape(-1, HEAD)
+        recv = jnp.concatenate([jnp.pad(recv[:width], ((0, 0), (0, HEAD - col))), tail_rows], axis=0)
+        last = jnp.pad(last, ((0, 0), (0, HEAD - col)))
+        lines = lines.reshape(-1, HEAD)
+    wgrad, owner_lse = pl.pallas_call(
+        functools.partial(final_kernel, lse_bits),
+        out_shape=(sds((width, HEAD), F32), sds((heads, tok), F32)),
+        in_specs=[SMEM_SPEC] + [VMEM_SPEC] * 3,
+        out_specs=(VMEM_SPEC,) * 2,
+        scratch_shapes=[pltpu.VMEM((2 * lines.size // HEAD, HEAD), F32)],
+        compiler_params=params(8),
+        cost_estimate=cost(1 << 18, 1 << 20),
+        name="final",
+    )(owner[0], last, recv, lines)
+    wgrad = wgrad[:, :col]
+    owner_lse = jnp.transpose(owner_lse)
+
+    return (attn_out[None], q_grad[None], k_grad[None], v_grad[None], wgrad, owner_lse[None, None])
 
 
 def solution(mesh):
@@ -667,6 +741,7 @@
         P(None, ("dp", "ctx")),
         P("dp", "ctx", None, None),
     )
+
     return jax.shard_map(
         on_device, mesh=mesh, in_specs=in_specs, out_specs=out_specs, check_vma=False
     )

time: 116 us -> 105 us (0.905)
  other arithmetic: 5.65 us -> 1.2 us
  matrix products: 6.62 us -> 2.35 us
  Pallas kernels: 27 us -> 22.9 us
    dot_general x1, matrix products: 6.62 us -> 2.35 us  [d_out_of(): lax.dot_general(grad, out_weight, (((1,), (1,)), ((), ())), preferred_ele...]
    convert_element_type x7 -> x4, other arithmetic: 4.58 us -> 0.53 us  [the longest x1 0.28 us: on_device(): functools.reduce(jnp.add, [x.astype(F32) for x in sent.addends])]
    pallas_call x3, Pallas kernels: 10.1 us -> 6.5 us  [the longest x2 4.73 us: partial_wo(): pl.pallas_call(functools.partial(wo_kernel, core), out_shape=shapes_of(si...]
    ppermute x8 -> x10, waiting for transfers between devices: 17.4 us -> 15 us  [exchange(): return lax.ppermute(x, axis, [(i, i ^ bit) for i in range(size)])]
    ppermute x9, waiting for transfers between devices: 15.3 us -> 16.8 us  [shift(): return lax.ppermute(x, 'ctx', pairs)]
    ppermute x8 -> x10, starting transfers between devices: 18.9 us -> 20 us  [exchange(): return lax.ppermute(x, axis, [(i, i ^ bit) for i in range(size)])]
    unnamed x36 -> x24, local copies, waits for them, and re-layouts: 4.02 us -> 4.95 us
  transfers between devices with their start and end apart: 17 -> 19, of which waited for: 10 -> 9; matrix products, arithmetic and copies ran while one was open for 10% -> 4% of each run, Pallas kernels for 12% -> 10%
where the time goes in v3:
time: 105 us
  starting transfers between devices  40.4 us (38%)
  waiting for transfers between devices  31.8 us (30%)
  Pallas kernels  22.9 us (22%)
  local copies, waits for them, and re-layouts  5.24 us (5%)
  matrix products  2.35 us (2%)
  other arithmetic  1.2 us (1%)
  between operations  1.05 us (1%)
    ppermute x9, starting transfers between devices, shift(): return lax.ppermute(x, 'ctx', pairs)  20.4 us
    ppermute x10, starting transfers between devices, exchange(): return lax.ppermute(x, axis, [(i, i ^ bit) for i in range(size)])  20 us
    ppermute x9, waiting for transfers between devices, shift(): return lax.ppermute(x, 'ctx', pairs)  16.8 us
    ppermute x10, waiting for transfers between devices, exchange(): return lax.ppermute(x, axis, [(i, i ^ bit) for i in range(size)])  15 us
    pallas_call x1, Pallas kernels, on_device(): pl.pallas_call(functools.partial(near_kernel, near_kb), grid=(tok // qb,)...  5.29 us
    unnamed x24, local copies, waits for them, and re-layouts  4.95 us
    pallas_call x2, Pallas kernels, partial_wo(): pl.pallas_call(functools.partial(wo_kernel, core), out_shape=shapes_of(si...  4.73 us
    pallas_call x1, Pallas kernels, on_device(): pl.pallas_call(functools.partial(fwd_kernel, len(blocks), back, kb), grid...  4.5 us
  transfers between devices with their start and end apart: 19, of which 9 were waited for; matrix products, arithmetic and copies ran while one was open for 4% of the time, Pallas kernels for 10%

profile of v3, /device:TPU:0, one launch (start us, length us, event | category | flops | bytes accessed | tf_op | source)
XLA Modules:
  0.0 104.9 jit_solution(10164764601668046678)
XLA Ops:
  0.6 2.6 %prep.1 = (bf16[512,256]{1,0:T(8,128)(2,1)}, f32[512,128]{1,0:T(8,128)}, f32[512,128]{1,0:T(8,128)}) custom-call(s32[1,8]{1,0:T(1,128)} %lens_ref.9, f32[1,128]{1,0:T(1,128)} %constant.22.clone.freq_ref, bf16[512,128]{1,0:T(8,128)(2,1)} %bitcast.101, bf16[512,128]{1,0:T(8,128)(2,1)} %bitcast.102), custom_call_target="tpu_custom_call" | custom-call | flops 4194304 | bytes 1048576 | tf_op jit(solution)/shard_map/prep/pallas_call | solution.py:443
  3.3 5.0 %collective-permute-start = (bf16[512,256]{1,0:T(8,128)(2,1)}, bf16[512,256]{1,0:T(8,128)(2,1)S(1)}, u32[]{:S(2)}, u32[]{:S(2)}) collective-permute-start(bf16[512,256]{1,0:T(8,128)(2,1)} %get-tuple-element.42.rest_0_.kv_ref), channel_id=1, source_target_pairs={{0,2},{1,3},{2,4},{3,5},{4,6},{5,7},{8,10},{9,11},{10,12},{11,13},... | collective-permute-start | bytes 786440 | tf_op jit(solution)/shard_map/ppermute | solution.py:433
  8.2 5.8 %collective-permute-done.rest_1_.rest_0_ = bf16[512,256]{1,0:T(8,128)(2,1)S(1)} collective-permute-done((bf16[512,256]{1,0:T(8,128)(2,1)}, bf16[512,256]{1,0:T(8,128)(2,1)S(1)}, u32[]{:S(2)}, u32[]{:S(2)}) %collective-permute-start) | collective-permute-done | bytes 262176 | tf_op jit(solution)/shard_map/ppermute | solution.py:433
  14.1 4.3 %collective-permute-start.2 = (bf16[512,256]{1,0:T(8,128)(2,1)S(1)}, bf16[512,256]{1,0:T(8,128)(2,1)S(1)}, u32[]{:S(2)}, u32[]{:S(2)}) collective-permute-start(bf16[512,256]{1,0:T(8,128)(2,1)S(1)} %collective-permute-done.rest_1_.rest_0_), channel_id=1, source_target_pairs={{0,2},{1,3},{2,4},{3,5},{4,6},{5,7},{8,10},{9,11},{10,12},{11,13},... | collective-permute-start | bytes 786440 | tf_op jit(solution)/shard_map/ppermute | solution.py:433
  18.4 3.4 %collective-permute-start.1 = (bf16[512,256]{1,0:T(8,128)(2,1)}, bf16[512,256]{1,0:T(8,128)(2,1)S(1)}, u32[]{:S(2)}, u32[]{:S(2)}) collective-permute-start(bf16[512,256]{1,0:T(8,128)(2,1)} %get-tuple-element.42.rest_0_.kv_ref), channel_id=1, source_target_pairs={{0,1},{2,3},{4,5},{6,7},{8,9},{10,11},{12,13},{14,15},{16,17},{18,... | collective-permute-start | bytes 786440 | tf_op jit(solution)/shard_map/ppermute | solution.py:433
  28.8 3.2 %collective-permute-done.3.rest_4_.rest_3_ = bf16[512,256]{1,0:T(8,128)(2,1)S(1)} collective-permute-done((bf16[512,256]{1,0:T(8,128)(2,1)S(1)}, bf16[512,256]{1,0:T(8,128)(2,1)S(1)}, u32[]{:S(2)}, u32[]{:S(2)}) %collective-permute-start.3) | collective-permute-done | bytes 262176 | tf_op jit(solution)/shard_map/ppermute | solution.py:433
  32.1 2.1 %collective-permute-done.4.rest_5_.rest_4_ = bf16[512,256]{1,0:T(8,128)(2,1)S(1)} collective-permute-done((bf16[512,256]{1,0:T(8,128)(2,1)S(1)}, bf16[512,256]{1,0:T(8,128)(2,1)S(1)}, u32[]{:S(2)}, u32[]{:S(2)}) %collective-permute-start.4) | collective-permute-done | bytes 262176 | tf_op jit(solution)/shard_map/ppermute | solution.py:433
  35.8 4.5 %fwd.1 = (bf16[512,512]{1,0:T(8,128)(2,1)}, bf16[512,512]{1,0:T(8,128)(2,1)S(1)}, f32[4,512]{1,0:T(4,128)S(1)}, bf16[2,16,128]{2,1,0:T(8,128)(2,1)S(1)}) custom-call(s32[1,8]{1,0:T(1,128)S(1)} %copy-done.6, bf16[512,512]{1,0:T(8,128)(2,1)S(1)} %rotq.1.q_ref, bf16[512,256]{1,0:T(8,128)(2,1)S(1)} %copy-done.9, ...), custom_call_target="tpu_custom_call" | custom-call | flops 1342177280 | bytes 4194304 | tf_op jit(solution)/shard_map/fwd/pallas_call | solution.py:494
  40.3 3.2 %shard_map.127 = (bf16[8,256,128]{2,1,0:T(8,128)(2,1)S(1)}, bf16[8,256,128]{2,1,0:T(8,128)(2,1)S(1)}, bf16[8,256,128]{2,1,0:T(8,128)(2,1)S(1)}, bf16[8,256,128]{...) custom-call(bf16[512,512]{1,0:T(8,128)(2,1)S(1)} %get-tuple-element.45.a_ref.o_ref, bf16[512,4096]{1,0:T(8,128)(2,1)S(1)} %bitcast.83), custom_call_target="tpu_custom_call" | custom-call | flops 1073741824 | bytes 6291456 | tf_op jit(solution)/shard_map/pallas_call | solution.py:527
  44.0 2.4 %convolution_convert_fusion.dy_ref = bf16[512,512]{1,0:T(8,128)(2,1)S(1)} fusion(bf16[512,4096]{1,0:T(8,128)(2,1)S(1)} %bitcast.84, bf16[512,4096]{1,0:T(8,128)(2,1)S(1)} %copy-done.11), kind=kOutput, calls=%fused_computation | convolution fusion | flops 2147745792 | bytes 8912896 | tf_op jit(solution)/shard_map/dot_general | solution.py:454
  46.9 1.6 %shard_map.128 = (bf16[8,256,128]{2,1,0:T(8,128)(2,1)S(1)}, bf16[8,256,128]{2,1,0:T(8,128)(2,1)S(1)}, bf16[8,256,128]{2,1,0:T(8,128)(2,1)S(1)}, bf16[8,256,128]{2,1,0:T(8,128)(2,1)S(1)}) custom-call(bf16[512,512]{1,0:T(8,128)(2,1)S(1)} %get-tuple-element.45.a_ref.o_ref, bf16[2,512,1024]{2,1,0:T(8,128)(2,1)S(1)} %get-tuple-element.47.g_ref), custom_call_target="tpu_custom_call" | custom-call | flops 1073741824 | bytes 6291456 | tf_op jit(solution)/shard_map/pallas_call | solution.py:527
  49.0 1.6 %collective-permute-start.7 = (bf16[2,2,2,256,128]{4,3,0,2,1:T(8,128)(2,1)S(1)}, bf16[2,2,2,256,128]{4,3,0,2,1:T(8,128)(2,1)S(1)}, u32[]{:S(2)}, u32[]{:S(2)}) collective-permute-start(bf16[2,2,2,256,128]{4,3,0,2,1:T(8,128)(2,1)S(1)} %copy.18), channel_id=1, source_target_pairs={{0,16},{8,24},{16,0},{24,8},{1,17},{9,25},{17,1},{25,9},{2,18},{10... | collective-permute-start | bytes 1572872 | tf_op jit(solution)/shard_map/ppermute | solution.py:551
  50.6 4.0 %collective-permute-start.10 = (bf16[2080,128]{1,0:T(8,128)(2,1)S(1)}, bf16[2080,128]{1,0:T(8,128)(2,1)S(1)}, u32[]{:S(2)}, u32[]{:S(2)}) collective-permute-start(bf16[2080,128]{1,0:T(8,128)(2,1)S(1)} %pad_maximum_fusion), channel_id=1, source_target_pairs={{0,2},{1,3},{2,0},{3,1},{4,6},{5,7},{6,4},{7,5},{8,10},{9,11},{10,... | collective-permute-start | bytes 1597448 | tf_op jit(solution)/shard_map/ppermute | solution.py:551
  54.6 1.6 %shard_map.129 = (f32[2,128,1024]{2,1,0:T(8,128)S(1)}, bf16[2,512,256]{2,1,0:T(8,128)(2,1)S(1)}, f32[4,512]{1,0:T(4,128)S(1)}) custom-call(s32[1,8]{1,0:T(1,128)S(1)} %copy-done.7, bf16[512,512]{1,0:T(8,128)(2,1)S(1)} %rotq.1.q_ref, bf16[512,512]{1,0:T(8,128)(2,1)S(1)} %convolution_convert_fusion.dy_ref, bf16[512,512]{1,0:T(8,128)(2,1)S(1)} %get-tuple-element.45.a_ref.o_ref, ...), custom_call_target="tpu_custom_call" | custom-call | flops 2684354560 | bytes 8388608 | tf_op jit(solution)/shard_map/pallas_call | solution.py:609
  57.9 3.4 %collective-permute-start.13 = (bf16[512,256]{1,0:T(8,128)(2,1)S(1)}, bf16[512,256]{1,0:T(8,128)(2,1)S(1)}, u32[]{:S(2)}, u32[]{:S(2)}) collective-permute-start(bf16[512,256]{1,0:T(8,128)(2,1)S(1)} %slice_bitcast_fusion.3), channel_id=1, source_target_pairs={{0,1},{2,3},{4,5},{6,7},{1,0},{3,2},{5,4},{7,6},{8,9},{10,11},{12,... | collective-permute-start | bytes 786440 | tf_op jit(solution)/shard_map/ppermute | solution.py:433
  61.5 3.6 %collective-permute-done.11 = bf16[512,256]{1,0:T(8,128)(2,1)S(1)} collective-permute-done((bf16[512,256]{1,0:T(8,128)(2,1)S(1)}, bf16[512,256]{1,0:T(8,128)(2,1)S(1)}, u32[]{:S(2)}, u32[]{:S(2)}) %collective-permute-start.11) | collective-permute-done | bytes 262176 | tf_op jit(solution)/shard_map/ppermute | solution.py:433
  65.2 1.3 %collective-permute-start.12 = (bf16[512,256]{1,0:T(8,128)(2,1)S(1)}, bf16[512,256]{1,0:T(8,128)(2,1)S(1)}, u32[]{:S(2)}, u32[]{:S(2)}) collective-permute-start(bf16[512,256]{1,0:T(8,128)(2,1)S(1)} %fusion), channel_id=1, source_target_pairs={{2,0},{3,1},{4,2},{5,3},{6,4},{7,5},{10,8},{11,9},{12,10},{13,11},... | collective-permute-start | bytes 786440 | tf_op jit(solution)/shard_map/ppermute | solution.py:433
  66.6 2.7 %collective-permute-start.15 = (bf16[2,2,256,128]{3,2,0,1:T(8,128)(2,1)S(1)}, bf16[2,2,256,128]{3,2,0,1:T(8,128)(2,1)S(1)}, u32[]{:S(2)}, u32[]{:S(2)}) collective-permute-start(bf16[2,2,256,128]{3,2,0,1:T(8,128)(2,1)S(1)} %fusion.4), channel_id=1, source_target_pairs={{0,2},{1,3},{2,0},{3,1},{4,6},{5,7},{6,4},{7,5},{8,10},{9,11},{10,... | collective-permute-start | bytes 786440 | tf_op jit(solution)/shard_map/ppermute | solution.py:551
  70.0 5.3 %near.1 = (bf16[512,512]{1,0:T(8,128)(2,1)}, f32[512,256]{1,0:T(8,128)S(1)}) custom-call(s32[1,8]{1,0:T(1,128)S(1)} %copy-done.7, bf16[512,512]{1,0:T(8,128)(2,1)S(1)} %rotq.1.q_ref, bf16[512,512]{1,0:T(8,128)(2,1)S(1)} %convolution_convert_fusion.dy_ref, f32[4,512]{1,0:T(4,128)S(1)} %get-tuple-element.51.o_ref.delta_ref, ...), custom_call_target="tpu_custom_call" | custom-call | flops 1073741824 | bytes 4194304 | tf_op jit(solution)/shard_map/near/pallas_call | solution.py:655
  75.3 3.2 %collective-permute-done.15 = bf16[2,2,256,128]{3,2,0,1:T(8,128)(2,1)S(1)} collective-permute-done((bf16[2,2,256,128]{3,2,0,1:T(8,128)(2,1)S(1)}, bf16[2,2,256,128]{3,2,0,1:T(8,128)(2,1)S(1)}, u32[]{:S(2)}, u32[]{:S(2)}) %collective-permute-start.15) | collective-permute-done | bytes 262176 | tf_op jit(solution)/shard_map/ppermute | solution.py:551
  80.8 4.7 %collective-permute-done.17 = bf16[1088,128]{1,0:T(8,128)(2,1)S(1)} collective-permute-done((bf16[1088,128]{1,0:T(8,128)(2,1)S(1)}, bf16[1088,128]{1,0:T(8,128)(2,1)S(1)}, u32[]{:S(2)}, u32[]{:S(2)}) %collective-permute-start.17) | collective-permute-done | bytes 278560 | tf_op jit(solution)/shard_map/ppermute | solution.py:551
  85.6 9.6 %collective-permute-start.18 = (bf16[640,128]{1,0:T(8,128)(2,1)S(1)}, bf16[640,128]{1,0:T(8,128)(2,1)S(1)}, u32[]{:S(2)}, u32[]{:S(2)}) collective-permute-start(bf16[640,128]{1,0:T(8,128)(2,1)S(1)} %pad_maximum_fusion.3), channel_id=1, source_target_pairs={{0,4},{1,5},{2,6},{3,7},{4,0},{5,1},{6,2},{7,3},{8,12},{9,13},{10,... | collective-permute-start | bytes 491528 | tf_op jit(solution)/shard_map/ppermute | solution.py:551
  96.0 7.1 %collective-permute-done.18.recv_ref = bf16[640,128]{1,0:T(8,128)(2,1)S(1)} collective-permute-done((bf16[640,128]{1,0:T(8,128)(2,1)S(1)}, bf16[640,128]{1,0:T(8,128)(2,1)S(1)}, u32[]{:S(2)}, u32[]{:S(2)}) %collective-permute-start.18) | collective-permute-done | bytes 163872 | tf_op jit(solution)/shard_map/ppermute | solution.py:551
  103.1 1.8 %final.1 = (f32[512,128]{1,0:T(8,128)}, f32[4,512]{1,0:T(4,128)}) custom-call(s32[64]{0:T(128)S(1)} %bitcast.91, bf16[512,128]{1,0:T(8,128)(2,1)S(1)} %get-tuple-element.79.one_ref, bf16[640,128]{1,0:T(8,128)(2,1)S(1)} %collective-permute-done.18.recv_ref, bf16[128,128]{1,0:T(8,128)(2,1)S(1)} %pad_maximum_fusion.5.lse_ref), custom_call_target="tpu_custom_call" | custom-call | flops 262144 | bytes 1048576 | tf_op jit(solution)/shard_map/final/pallas_call | solution.py:710
  (77 shorter events, 15.9 us)
Async XLA Ops:
  3.3 10.8 %collective-permute-start = (bf16[512,256]{1,0:T(8,128)(2,1)}, bf16[512,256]{1,0:T(8,128)(2,1)S(1)}, u32[]{:S(2)}, u32[]{:S(2)}) collective-permute-start(bf16[512,256]{1,0:T(8,128)(2,1)} %get-tuple-element.42.rest_0_.kv_ref), channel_id=1, source_target_pairs={{0,2},{1,3},{2,4},{3,5},{4,6},{5,7},{8,10},{9,11},{10,12},{11,13},... | collective-permute-start | bytes 786440 | tf_op jit(solution)/shard_map/ppermute | solution.py:433
  14.1 9.0 %collective-permute-start.2 = (bf16[512,256]{1,0:T(8,128)(2,1)S(1)}, bf16[512,256]{1,0:T(8,128)(2,1)S(1)}, u32[]{:S(2)}, u32[]{:S(2)}) collective-permute-start(bf16[512,256]{1,0:T(8,128)(2,1)S(1)} %collective-permute-done.rest_1_.rest_0_), channel_id=1, source_target_pairs={{0,2},{1,3},{2,4},{3,5},{4,6},{5,7},{8,10},{9,11},{10,12},{11,13},... | collective-permute-start | bytes 786440 | tf_op jit(solution)/shard_map/ppermute | solution.py:433
  18.4 10.4 %collective-permute-start.1 = (bf16[512,256]{1,0:T(8,128)(2,1)}, bf16[512,256]{1,0:T(8,128)(2,1)S(1)}, u32[]{:S(2)}, u32[]{:S(2)}) collective-permute-start(bf16[512,256]{1,0:T(8,128)(2,1)} %get-tuple-element.42.rest_0_.kv_ref), channel_id=1, source_target_pairs={{0,1},{2,3},{4,5},{6,7},{8,9},{10,11},{12,13},{14,15},{16,17},{18,... | collective-permute-start | bytes 786440 | tf_op jit(solution)/shard_map/ppermute | solution.py:433
  21.8 10.2 %collective-permute-start.3 = (bf16[512,256]{1,0:T(8,128)(2,1)S(1)}, bf16[512,256]{1,0:T(8,128)(2,1)S(1)}, u32[]{:S(2)}, u32[]{:S(2)}) collective-permute-start(bf16[512,256]{1,0:T(8,128)(2,1)S(1)} %collective-permute-done.rest_1_.rest_0_), channel_id=1, source_target_pairs={{0,1},{2,3},{4,5},{6,7},{1,0},{3,2},{5,4},{7,6},{8,9},{10,11},{12,... | collective-permute-start | bytes 786440 | tf_op jit(solution)/shard_map/ppermute | solution.py:433
  23.1 11.1 %collective-permute-start.4 = (bf16[512,256]{1,0:T(8,128)(2,1)S(1)}, bf16[512,256]{1,0:T(8,128)(2,1)S(1)}, u32[]{:S(2)}, u32[]{:S(2)}) collective-permute-start(bf16[512,256]{1,0:T(8,128)(2,1)S(1)} %collective-permute-done.2.rest_3_.rest_2_), channel_id=1, source_target_pairs={{1,0},{3,2},{5,4},{7,6},{9,8},{11,10},{13,12},{15,14},{17,16},{19,... | collective-permute-start | bytes 786440 | tf_op jit(solution)/shard_map/ppermute | solution.py:433
  24.4 15.9 %copy-start = (bf16[1,512,4096]{2,1,0:T(8,128)(2,1)S(1)}, bf16[1,512,4096]{2,1,0:T(8,128)(2,1)}, u32[]{:S(2)}) copy-start(bf16[1,512,4096]{2,1,0:T(8,128)(2,1)} %param.14) | copy-start | bytes 12582916
  43.4 5.2 %collective-permute-start.5 = (bf16[8,256,128]{2,1,0:T(8,128)(2,1)S(1)}, bf16[8,256,128]{2,1,0:T(8,128)(2,1)S(1)}, u32[]{:S(2)}, u32[]{:S(2)}) collective-permute-start(bf16[8,256,128]{2,1,0:T(8,128)(2,1)S(1)} %get-tuple-element.49), channel_id=1, source_target_pairs={{0,8},{8,0},{16,24},{24,16},{1,9},{9,1},{17,25},{25,17},{2,10},{10... | collective-permute-start | bytes 1572872 | tf_op jit(solution)/shard_map/ppermute | solution.py:551
  43.5 5.1 %collective-permute-start.9 = (bf16[8,256,128]{2,1,0:T(8,128)(2,1)S(1)}, bf16[8,256,128]{2,1,0:T(8,128)(2,1)S(1)}, u32[]{:S(2)}, u32[]{:S(2)}) collective-permute-start(bf16[8,256,128]{2,1,0:T(8,128)(2,1)S(1)} %get-tuple-element.60), channel_id=1, source_target_pairs={{0,8},{8,0},{16,24},{24,16},{1,9},{9,1},{17,25},{25,17},{2,10},{10... | collective-permute-start | bytes 1572872 | tf_op jit(solution)/shard_map/ppermute | solution.py:551
  46.4 11.5 %collective-permute-start.6 = (bf16[8,256,128]{2,1,0:T(8,128)(2,1)S(1)}, bf16[8,256,128]{2,1,0:T(8,128)(2,1)S(1)}, u32[]{:S(2)}, u32[]{:S(2)}) collective-permute-start(bf16[8,256,128]{2,1,0:T(8,128)(2,1)S(1)} %get-tuple-element.55), channel_id=1, source_target_pairs={{0,8},{8,0},{16,24},{24,16},{1,9},{9,1},{17,25},{25,17},{2,10},{10... | collective-permute-start | bytes 1572872 | tf_op jit(solution)/shard_map/ppermute | solution.py:551
  46.5 14.9 %collective-permute-start.8 = (bf16[8,256,128]{2,1,0:T(8,128)(2,1)S(1)}, bf16[8,256,128]{2,1,0:T(8,128)(2,1)S(1)}, u32[]{:S(2)}, u32[]{:S(2)}) collective-permute-start(bf16[8,256,128]{2,1,0:T(8,128)(2,1)S(1)} %get-tuple-element.58), channel_id=1, source_target_pairs={{0,8},{8,0},{16,24},{24,16},{1,9},{9,1},{17,25},{25,17},{2,10},{10... | collective-permute-start | bytes 1572872 | tf_op jit(solution)/shard_map/ppermute | solution.py:551
  49.0 17.5 %collective-permute-start.7 = (bf16[2,2,2,256,128]{4,3,0,2,1:T(8,128)(2,1)S(1)}, bf16[2,2,2,256,128]{4,3,0,2,1:T(8,128)(2,1)S(1)}, u32[]{:S(2)}, u32[]{:S(2)}) collective-permute-start(bf16[2,2,2,256,128]{4,3,0,2,1:T(8,128)(2,1)S(1)} %copy.18), channel_id=1, source_target_pairs={{0,16},{8,24},{16,0},{24,8},{1,17},{9,25},{17,1},{25,9},{2,18},{10... | collective-permute-start | bytes 1572872 | tf_op jit(solution)/shard_map/ppermute | solution.py:551
  50.6 18.8 %collective-permute-start.10 = (bf16[2080,128]{1,0:T(8,128)(2,1)S(1)}, bf16[2080,128]{1,0:T(8,128)(2,1)S(1)}, u32[]{:S(2)}, u32[]{:S(2)}) collective-permute-start(bf16[2080,128]{1,0:T(8,128)(2,1)S(1)} %pad_maximum_fusion), channel_id=1, source_target_pairs={{0,2},{1,3},{2,0},{3,1},{4,6},{5,7},{6,4},{7,5},{8,10},{9,11},{10,... | collective-permute-start | bytes 1597448 | tf_op jit(solution)/shard_map/ppermute | solution.py:551
  56.2 8.8 %collective-permute-start.11 = (bf16[512,256]{1,0:T(8,128)(2,1)S(1)}, bf16[512,256]{1,0:T(8,128)(2,1)S(1)}, u32[]{:S(2)}, u32[]{:S(2)}) collective-permute-start(bf16[512,256]{1,0:T(8,128)(2,1)S(1)} %slice_bitcast_fusion.4), channel_id=1, source_target_pairs={{0,1},{2,3},{4,5},{6,7},{1,0},{3,2},{5,4},{7,6},{8,9},{10,11},{12,... | collective-permute-start | bytes 786440 | tf_op jit(solution)/shard_map/ppermute | solution.py:433
  57.9 21.5 %collective-permute-start.13 = (bf16[512,256]{1,0:T(8,128)(2,1)S(1)}, bf16[512,256]{1,0:T(8,128)(2,1)S(1)}, u32[]{:S(2)}, u32[]{:S(2)}) collective-permute-start(bf16[512,256]{1,0:T(8,128)(2,1)S(1)} %slice_bitcast_fusion.3), channel_id=1, source_target_pairs={{0,1},{2,3},{4,5},{6,7},{1,0},{3,2},{5,4},{7,6},{8,9},{10,11},{12,... | collective-permute-start | bytes 786440 | tf_op jit(solution)/shard_map/ppermute | solution.py:433
  61.3 8.7 %copy-start.2 = (f32[512,128]{1,0:T(8,128)S(1)}, f32[512,128]{1,0:T(8,128)}, u32[]{:S(2)}) copy-start(f32[512,128]{1,0:T(8,128)} %get-tuple-element.40.cos_ref) | copy-start | bytes 786436
  61.3 8.7 %copy-start.4 = (f32[512,128]{1,0:T(8,128)S(1)}, f32[512,128]{1,0:T(8,128)}, u32[]{:S(2)}) copy-start(f32[512,128]{1,0:T(8,128)} %get-tuple-element.41.sin_ref) | copy-start | bytes 786436
  61.3 8.7 %copy-start.10 = (bf16[512,256]{1,0:T(8,128)(2,1)S(1)}, bf16[512,256]{1,0:T(8,128)(2,1)}, u32[]{:S(2)}) copy-start(bf16[512,256]{1,0:T(8,128)(2,1)} %get-tuple-element.42.rest_0_.kv_ref) | copy-start | bytes 786436
  65.2 14.2 %collective-permute-start.12 = (bf16[512,256]{1,0:T(8,128)(2,1)S(1)}, bf16[512,256]{1,0:T(8,128)(2,1)S(1)}, u32[]{:S(2)}, u32[]{:S(2)}) collective-permute-start(bf16[512,256]{1,0:T(8,128)(2,1)S(1)} %fusion), channel_id=1, source_target_pairs={{2,0},{3,1},{4,2},{5,3},{6,4},{7,5},{10,8},{11,9},{12,10},{13,11},... | collective-permute-start | bytes 786440 | tf_op jit(solution)/shard_map/ppermute | solution.py:433
  66.6 11.9 %collective-permute-start.15 = (bf16[2,2,256,128]{3,2,0,1:T(8,128)(2,1)S(1)}, bf16[2,2,256,128]{3,2,0,1:T(8,128)(2,1)S(1)}, u32[]{:S(2)}, u32[]{:S(2)}) collective-permute-start(bf16[2,2,256,128]{3,2,0,1:T(8,128)(2,1)S(1)} %fusion.4), channel_id=1, source_target_pairs={{0,2},{1,3},{2,0},{3,1},{4,6},{5,7},{6,4},{7,5},{8,10},{9,11},{10,... | collective-permute-start | bytes 786440 | tf_op jit(solution)/shard_map/ppermute | solution.py:551
  69.5 9.2 %collective-permute-start.16 = (bf16[2,2,256,128]{3,2,0,1:T(8,128)(2,1)S(1)}, bf16[2,2,256,128]{3,2,0,1:T(8,128)(2,1)S(1)}, u32[]{:S(2)}, u32[]{:S(2)}) collective-permute-start(bf16[2,2,256,128]{3,2,0,1:T(8,128)(2,1)S(1)} %fusion.3), channel_id=1, source_target_pairs={{0,16},{8,24},{16,0},{24,8},{1,17},{9,25},{17,1},{25,9},{2,18},{10... | collective-permute-start | bytes 786440 | tf_op jit(solution)/shard_map/ppermute | solution.py:551
  75.3 27.9 %copy-start.8 = (s32[1,64]{1,0:T(1,128)S(1)}, s32[1,64]{1,0:T(1,128)}, u32[]{:S(2)}) copy-start(s32[1,64]{1,0:T(1,128)} %param.12) | copy-start | bytes 772
  78.9 6.6 %collective-permute-start.17 = (bf16[1088,128]{1,0:T(8,128)(2,1)S(1)}, bf16[1088,128]{1,0:T(8,128)(2,1)S(1)}, u32[]{:S(2)}, u32[]{:S(2)}) collective-permute-start(bf16[1088,128]{1,0:T(8,128)(2,1)S(1)} %pad_maximum_fusion.1), channel_id=1, source_target_pairs={{0,1},{1,0},{2,3},{3,2},{4,5},{5,4},{6,7},{7,6},{8,9},{9,8},{10,11... | collective-permute-start | bytes 835592 | tf_op jit(solution)/shard_map/ppermute | solution.py:551
  79.5 15.7 %collective-permute-start.14 = (bf16[512,256]{1,0:T(8,128)(2,1)S(1)}, bf16[512,256]{1,0:T(8,128)(2,1)S(1)}, u32[]{:S(2)}, u32[]{:S(2)}) collective-permute-start(bf16[512,256]{1,0:T(8,128)(2,1)S(1)} %fusion.2), channel_id=1, source_target_pairs={{2,0},{3,1},{4,2},{5,3},{6,4},{7,5},{10,8},{11,9},{12,10},{13,11},... | collective-permute-start | bytes 786440 | tf_op jit(solution)/shard_map/ppermute | solution.py:433
  85.6 17.6 %collective-permute-start.18 = (bf16[640,128]{1,0:T(8,128)(2,1)S(1)}, bf16[640,128]{1,0:T(8,128)(2,1)S(1)}, u32[]{:S(2)}, u32[]{:S(2)}) collective-permute-start(bf16[640,128]{1,0:T(8,128)(2,1)S(1)} %pad_maximum_fusion.3), channel_id=1, source_target_pairs={{0,4},{1,5},{2,6},{3,7},{4,0},{5,1},{6,2},{7,3},{8,12},{9,13},{10,... | collective-permute-start | bytes 491528 | tf_op jit(solution)/shard_map/ppermute | solution.py:551
  (7 other events, 19.2 us)

commit v4 on v3

--- a/solution.py
+++ b/solution.py
@@ -169,42 +169,72 @@
     return lax.dot_general(a, b, dims, preferred_element_type=F32)
 
 
-def fwd_kernel(n_refs, back, kb, lens_ref, q_ref, *rest):
-    kv_refs = rest[:n_refs]
-    o_ref, keep_ref, lse_ref, pack_ref, kv_scr, sem = rest[n_refs:]
+def fwd_kernel(picks, back, resume, finish, lens_ref, q_ref, *rest):
+    kv_refs, rest = rest[: len(picks)], rest[len(picks) :]
+    if resume:
+        acc_in_ref, stat_in_ref, *rest = rest
+    *outs, kv_scr, sem = rest
     step = pl.program_id(0)
     qb, width = q_ref.shape
     heads = width // HEAD
     rows = heads * qb
-    tok = kv_refs[0].shape[0]
+    kb = kv_refs[0].shape[0]
     dev, n_ctx = place()
+    slots = [slot_list(dev, n_ctx, back)[p] for p in picks]
 
     @pl.when(step == 0)
     def _():
-        load_slots(slot_list(dev, n_ctx, back), kv_refs, kv_scr, sem, tok)
-
-    base = (dev - back) * tok
-    first = dev * tok + step * qb
+        copies = [
+            pltpu.make_async_copy(ref, kv_scr.at[i], sem.at[i]) for i, ref in enumerate(kv_refs)
+        ]
+        for copy in copies:
+            copy.start()
+        for copy in copies:
+            copy.wait()
+
+    base = (dev - back) * kb
+    first = dev * kb + step * qb
     q = stack_heads(q_ref)
     low, high = query_bounds(lens_ref, first, qb, heads)
     factor = SCALE * LOG2E
-
-    def visit(masked, j, carry):
+    lo, full_lo, full_hi, hi = tile_ranges(lens_ref, first, qb, kb, base, back + 1)
+
+    def visit(masked, i, slot, carry):
         top, total, acc = carry
-        at = pl.multiple_of(j * kb, kb)
-        s = dot(kv_scr[pl.ds(at, kb), :HEAD], q, NT)
+        s = dot(kv_scr[i, :, :HEAD], q, NT)
         if masked:
-            s = masked_scores(s, base, at, low, high)
+            s = masked_scores(s, base, slot * kb, low, high)
         new = jnp.maximum(top, jnp.max(fold(s, jnp.max), axis=0, keepdims=True) * factor)
         alpha = jnp.exp2(top - new)
         p = jnp.exp2(s * factor - new)
         total = total * alpha + fold(p, jnp.sum)
-        acc = acc * alpha + dot(kv_scr[pl.ds(at, kb), HEAD:], p.astype(BF16), TN)
+        acc = acc * alpha + dot(kv_scr[i, :, HEAD:], p.astype(BF16), TN)
         return new, total, acc
 
-    carry = (jnp.full((1, rows), NEG, F32), jnp.zeros((8, rows), F32), jnp.zeros((HEAD, rows), F32))
-    ranges = tile_ranges(lens_ref, first, qb, kb, base, kv_scr.shape[0] // kb)
-    top, total, acc = over_tiles(ranges, visit, carry)
+    def block(i, carry):
+        slot = jnp.int32(slots[0])
+        for n in range(1, len(slots)):
+            slot = jnp.where(i == n, slots[n], slot)
+        seen = (slot >= lo) & (slot < hi)
+        full = seen & (slot >= full_lo) & (slot < full_hi)
+        for masked, go in ((False, full), (True, seen & ~full)):
+            carry = lax.fori_loop(
+                0, go.astype(jnp.int32), lambda _, c, masked=masked: visit(masked, i, slot, c), carry
+            )
+        return carry
+
+    if resume:
+        carry = (stat_in_ref[0, 0:1], stat_in_ref[0, 8:16], acc_in_ref[0])
+    else:
+        carry = (jnp.full((1, rows), NEG, F32), jnp.zeros((8, rows), F32), jnp.zeros((HEAD, rows), F32))
+    top, total, acc = lax.fori_loop(0, len(picks), block, carry)
+    if not finish:
+        acc_ref, stat_ref = outs
+        acc_ref[0] = acc
+        stat_ref[0, 0:8] = jnp.broadcast_to(top, (8, rows))
+        stat_ref[0, 8:16] = total
+        return
+    o_ref, keep_ref, lse_ref, pack_ref = outs
     total = jnp.sum(total, axis=0, keepdims=True)
     lse = (top + jnp.log2(total)) * LN2
     out = acc / total
@@ -466,50 +496,58 @@
             name="rotq",
         )(x, cos, sin)
 
+    qb = tok // 2
+    kb = tok
+    tok_spec = pl.BlockSpec((qb, width), lambda i: (i, 0))
+    lse_spec = pl.BlockSpec((heads, qb), lambda i: (0, i))
+    table_spec = pl.BlockSpec((qb, HEAD), lambda i: (i, 0))
+    dq_spec = pl.BlockSpec((1, HEAD, heads * qb), lambda i: (i, 0, 0))
+    stat_spec = pl.BlockSpec((1, 16, heads * qb), lambda i: (i, 0, 0))
+    pairs = heads * tok * (tok + reach) // 2
+    pack_rows = 2 * heads * qb // HEAD
+    steps = tok // qb
+    state = [(sds((steps, HEAD, heads * qb), F32), dq_spec), (sds((steps, 16, heads * qb), F32), stat_spec)]
+    result = [
+        (sds((tok, width), BF16), tok_spec),
+        (sds((tok, width), BF16), tok_spec),
+        (sds((heads, tok), F32), lse_spec),
+        (sds((steps, pack_rows, HEAD), BF16), pl.BlockSpec((1, pack_rows, HEAD), lambda i: (i, 0, 0))),
+    ]
+
+    def forward(picks, taken, before, finish):
+        outs = result if finish else state
+        return pl.pallas_call(
+            functools.partial(fwd_kernel, picks, back, bool(before), finish),
+            grid=(steps,),
+            out_shape=[o[0] for o in outs],
+            in_specs=[SMEM_SPEC, tok_spec] + [ANY_SPEC] * len(taken) + [s[1] for s in state] * bool(before),
+            out_specs=[o[1] for o in outs],
+            scratch_shapes=[
+                pltpu.VMEM((len(taken), tok, 2 * HEAD), BF16),
+                pltpu.SemaphoreType.DMA((len(taken),)),
+            ],
+            compiler_params=params(FWD_MIB, "arbitrary"),
+            cost_estimate=cost(2 * pairs * HEAD, 4 << 20, pairs // 2),
+        )(doc_lengths, q_rot, *taken, *before)
+
     if paired:
         a1 = shift(kv_home, hop)
         e1 = shift(kv_home, up)
         q_rot = rotated_queries(queries[0])
         s1 = shift(a1, swap)
         a2 = shift(a1, hop)
+        partial = forward((0, 1, 2), [kv_home, a1, e1], [], False)
         o3 = shift(a2, down)
         d_out = d_out_of(after(out_grad[0], a2))
         blocks = [kv_home, a1, e1, a2, s1, o3]
+        attn_out, attn, lse, pack = forward((3, 4, 5), [a2, s1, o3], partial, True)
     else:
         blocks = [kv_home] + [
             shift(kv_home, [(i, i + s) for i in range(n_ctx - s)]) for s in range(1, back + 1)
         ]
         q_rot = rotated_queries(queries[0])
         d_out = d_out_of(out_grad[0])
-
-    n_keys = (back + 1) * tok
-    qb = tok // 2
-    kb = tok
-    tok_spec = pl.BlockSpec((qb, width), lambda i: (i, 0))
-    lse_spec = pl.BlockSpec((heads, qb), lambda i: (0, i))
-    table_spec = pl.BlockSpec((qb, HEAD), lambda i: (i, 0))
-    dq_spec = pl.BlockSpec((1, HEAD, heads * qb), lambda i: (i, 0, 0))
-    pairs = heads * tok * (tok + reach) // 2
-    pack_rows = 2 * heads * qb // HEAD
-    attn_out, attn, lse, pack = pl.pallas_call(
-        functools.partial(fwd_kernel, len(blocks), back, kb),
-        grid=(tok // qb,),
-        out_shape=(
-            sds((tok, width), BF16),
-            sds((tok, width), BF16),
-            sds((heads, tok), F32),
-            sds((tok // qb, pack_rows, HEAD), BF16),
-        ),
-        in_specs=[SMEM_SPEC, tok_spec] + [ANY_SPEC] * len(blocks),
-        out_specs=(tok_spec, tok_spec, lse_spec, pl.BlockSpec((1, pack_rows, HEAD), lambda i: (i, 0, 0))),
-        scratch_shapes=[
-            pltpu.VMEM((n_keys, 2 * HEAD), BF16),
-            pltpu.SemaphoreType.DMA((len(blocks),)),
-        ],
-        compiler_params=params(FWD_MIB, "arbitrary"),
-        cost_estimate=cost(4 * pairs * HEAD, 4 << 20, pairs),
-        name="fwd",
-    )(doc_lengths, q_rot, *blocks)
+        attn_out, attn, lse, pack = forward(tuple(range(back + 1)), blocks, [], True)
 
     col = d_model // (n_dp * n_ctx)
     bits_dp = n_dp.bit_length() - 1
@@ -742,6 +780,4 @@
         P("dp", "ctx", None, None),
     )
 
-    return jax.shard_map(
-        on_device, mesh=mesh, in_specs=in_specs, out_specs=out_specs, check_vma=False
-    )
+    return jax.shard_map(on_device, mesh=mesh, in_specs=in_specs, out_specs=out_specs, check_vma=False)

time: 105 us -> 105 us (level)
  waiting for transfers between devices: 31.8 us -> 26.3 us
  Pallas kernels: 22.9 us -> 25.8 us
  starting transfers between devices: 40.4 us -> 43 us
    ppermute x9, waiting for transfers between devices: 16.8 us -> 11.7 us  [shift(): return lax.ppermute(x, 'ctx', pairs)]
    pallas_call x1 -> x2, Pallas kernels: 4.5 us -> 7.41 us  [forward(): pl.pallas_call(functools.partial(fwd_kernel, picks, back, bool(before), f...]
    ppermute x10, starting transfers between devices: 20 us -> 22.1 us  [exchange(): return lax.ppermute(x, axis, [(i, i ^ bit) for i in range(size)])]
  transfers between devices with their start and end apart: 19 -> 19, of which waited for: 9 -> 7; matrix products, arithmetic and copies ran while one was open for 4% -> 4% of each run, Pallas kernels for 10% -> 15%
where the time goes in v4:
time: 105 us
  starting transfers between devices  43 us (41%)
  waiting for transfers between devices  26.3 us (25%)
  Pallas kernels  25.8 us (25%)
  local copies, waits for them, and re-layouts  5.24 us (5%)
  matrix products  2.36 us (2%)
  other arithmetic  1.21 us (1%)
  between operations  1.08 us (1%)
    ppermute x10, starting transfers between devices, exchange(): return lax.ppermute(x, axis, [(i, i ^ bit) for i in range(size)])  22.1 us
    ppermute x9, starting transfers between devices, shift(): return lax.ppermute(x, 'ctx', pairs)  21 us
    ppermute x10, waiting for transfers between devices, exchange(): return lax.ppermute(x, axis, [(i, i ^ bit) for i in range(size)])  14.6 us
    ppermute x9, waiting for transfers between devices, shift(): return lax.ppermute(x, 'ctx', pairs)  11.7 us
    pallas_call x2, Pallas kernels, forward(): pl.pallas_call(functools.partial(fwd_kernel, picks, back, bool(before), f...  7.41 us
    pallas_call x1, Pallas kernels, on_device(): pl.pallas_call(functools.partial(near_kernel, near_kb), grid=(tok // qb,)...  5.29 us
    unnamed x24, local copies, waits for them, and re-layouts  4.95 us
    pallas_call x2, Pallas kernels, partial_wo(): pl.pallas_call(functools.partial(wo_kernel, core), out_shape=shapes_of(si...  4.73 us
  transfers between devices with their start and end apart: 19, of which 7 were waited for; matrix products, arithmetic and copies ran while one was open for 4% of the time, Pallas kernels for 15%

profile of v4, /device:TPU:0, one launch (start us, length us, event | category | flops | bytes accessed | tf_op | source)
XLA Modules:
  0.0 105.1 jit_solution(8345638848675326530)
XLA Ops:
  0.6 2.6 %prep.1 = (bf16[512,256]{1,0:T(8,128)(2,1)}, f32[512,128]{1,0:T(8,128)}, f32[512,128]{1,0:T(8,128)}) custom-call(s32[1,8]{1,0:T(1,128)} %lens_ref.11, f32[1,128]{1,0:T(1,128)} %constant.22.clone.freq_ref, bf16[512,128]{1,0:T(8,128)(2,1)} %bitcast.101, bf16[512,128]{1,0:T(8,128)(2,1)} %bitcast.102), custom_call_target="tpu_custom_call" | custom-call | flops 4194304 | bytes 1048576 | tf_op jit(solution)/shard_map/prep/pallas_call | solution.py:473
  3.3 5.0 %collective-permute-start = (bf16[512,256]{1,0:T(8,128)(2,1)}, bf16[512,256]{1,0:T(8,128)(2,1)S(1)}, u32[]{:S(2)}, u32[]{:S(2)}) collective-permute-start(bf16[512,256]{1,0:T(8,128)(2,1)} %get-tuple-element.44.rest_0_.kv_ref), channel_id=1, source_target_pairs={{0,2},{1,3},{2,4},{3,5},{4,6},{5,7},{8,10},{9,11},{10,12},{11,13},... | collective-permute-start | bytes 786440 | tf_op jit(solution)/shard_map/ppermute | solution.py:463
  8.2 5.8 %collective-permute-done.rest_1_.rest_0_ = bf16[512,256]{1,0:T(8,128)(2,1)S(1)} collective-permute-done((bf16[512,256]{1,0:T(8,128)(2,1)}, bf16[512,256]{1,0:T(8,128)(2,1)S(1)}, u32[]{:S(2)}, u32[]{:S(2)}) %collective-permute-start) | collective-permute-done | bytes 262176 | tf_op jit(solution)/shard_map/ppermute | solution.py:463
  14.1 4.3 %collective-permute-start.1 = (bf16[512,256]{1,0:T(8,128)(2,1)S(1)}, bf16[512,256]{1,0:T(8,128)(2,1)S(1)}, u32[]{:S(2)}, u32[]{:S(2)}) collective-permute-start(bf16[512,256]{1,0:T(8,128)(2,1)S(1)} %collective-permute-done.rest_1_.rest_0_), channel_id=1, source_target_pairs={{0,2},{1,3},{2,4},{3,5},{4,6},{5,7},{8,10},{9,11},{10,12},{11,13},... | collective-permute-start | bytes 786440 | tf_op jit(solution)/shard_map/ppermute | solution.py:463
  18.4 3.4 %collective-permute-start.4 = (bf16[512,256]{1,0:T(8,128)(2,1)}, bf16[512,256]{1,0:T(8,128)(2,1)S(1)}, u32[]{:S(2)}, u32[]{:S(2)}) collective-permute-start(bf16[512,256]{1,0:T(8,128)(2,1)} %get-tuple-element.44.rest_0_.kv_ref), channel_id=1, source_target_pairs={{0,1},{2,3},{4,5},{6,7},{8,9},{10,11},{12,13},{14,15},{16,17},{18,... | collective-permute-start | bytes 786440 | tf_op jit(solution)/shard_map/ppermute | solution.py:463
  30.4 4.5 %shard_map.127 = (f32[2,128,1024]{2,1,0:T(8,128)S(1)}, f32[2,16,1024]{2,1,0:T(8,128)S(1)}) custom-call(s32[1,8]{1,0:T(1,128)S(1)} %copy-done.6, bf16[512,512]{1,0:T(8,128)(2,1)S(1)} %rotq.1.q_ref, bf16[512,256]{1,0:T(8,128)(2,1)S(1)} %copy-done.9, bf16[512,256]{1,0:T(8,128)(2,1)S(1)} %collective-permute-done.rest_1_.rest_0_, ...), custom_call_target="tpu_custom_call" | custom-call | flops 671088640 | bytes 4194304 | tf_op jit(solution)/shard_map/pallas_call | solution.py:519
  34.9 3.0 %shard_map.128 = (bf16[512,512]{1,0:T(8,128)(2,1)}, bf16[512,512]{1,0:T(8,128)(2,1)S(1)}, f32[4,512]{1,0:T(4,128)S(1)}, bf16[2,16,128]{2,1,0:T(8,128)(2,1)S(1)}) custom-call(s32[1,8]{1,0:T(1,128)S(1)} %copy-done.6, bf16[512,512]{1,0:T(8,128)(2,1)S(1)} %rotq.1.q_ref, bf16[512,256]{1,0:T(8,128)(2,1)S(1)} %collective-permute-done.1.rest_0_.rest_2_, ...), custom_call_target="tpu_custom_call" | custom-call | flops 671088640 | bytes 4194304 | tf_op jit(solution)/shard_map/pallas_call | solution.py:519
  37.9 3.2 %shard_map.129 = (bf16[8,256,128]{2,1,0:T(8,128)(2,1)S(1)}, bf16[8,256,128]{2,1,0:T(8,128)(2,1)S(1)}, bf16[8,256,128]{2,1,0:T(8,128)(2,1)S(1)}, bf16[8,256,128]{...) custom-call(bf16[512,512]{1,0:T(8,128)(2,1)S(1)} %get-tuple-element.49.a_ref.o_ref, bf16[512,4096]{1,0:T(8,128)(2,1)S(1)} %bitcast.83), custom_call_target="tpu_custom_call" | custom-call | flops 1073741824 | bytes 6291456 | tf_op jit(solution)/shard_map/pallas_call | solution.py:565
  41.6 2.4 %convolution_convert_fusion.dy_ref = bf16[512,512]{1,0:T(8,128)(2,1)S(1)} fusion(bf16[512,4096]{1,0:T(8,128)(2,1)S(1)} %bitcast.84, bf16[512,4096]{1,0:T(8,128)(2,1)S(1)} %copy-done.11), kind=kOutput, calls=%fused_computation | convolution fusion | flops 2147745792 | bytes 8912896 | tf_op jit(solution)/shard_map/dot_general | solution.py:484
  44.6 1.6 %shard_map.130 = (bf16[8,256,128]{2,1,0:T(8,128)(2,1)S(1)}, bf16[8,256,128]{2,1,0:T(8,128)(2,1)S(1)}, bf16[8,256,128]{2,1,0:T(8,128)(2,1)S(1)}, bf16[8,256,128]{2,1,0:T(8,128)(2,1)S(1)}) custom-call(bf16[512,512]{1,0:T(8,128)(2,1)S(1)} %get-tuple-element.49.a_ref.o_ref, bf16[2,512,1024]{2,1,0:T(8,128)(2,1)S(1)} %get-tuple-element.51.g_ref), custom_call_target="tpu_custom_call" | custom-call | flops 1073741824 | bytes 6291456 | tf_op jit(solution)/shard_map/pallas_call | solution.py:565
  46.6 1.6 %collective-permute-start.7 = (bf16[2,2,2,256,128]{4,3,0,2,1:T(8,128)(2,1)S(1)}, bf16[2,2,2,256,128]{4,3,0,2,1:T(8,128)(2,1)S(1)}, u32[]{:S(2)}, u32[]{:S(2)}) collective-permute-start(bf16[2,2,2,256,128]{4,3,0,2,1:T(8,128)(2,1)S(1)} %copy.18), channel_id=1, source_target_pairs={{0,16},{8,24},{16,0},{24,8},{1,17},{9,25},{17,1},{25,9},{2,18},{10... | collective-permute-start | bytes 1572872 | tf_op jit(solution)/shard_map/ppermute | solution.py:589
  48.2 4.2 %collective-permute-start.10 = (bf16[2080,128]{1,0:T(8,128)(2,1)S(1)}, bf16[2080,128]{1,0:T(8,128)(2,1)S(1)}, u32[]{:S(2)}, u32[]{:S(2)}) collective-permute-start(bf16[2080,128]{1,0:T(8,128)(2,1)S(1)} %pad_maximum_fusion), channel_id=1, source_target_pairs={{0,2},{1,3},{2,0},{3,1},{4,6},{5,7},{6,4},{7,5},{8,10},{9,11},{10,... | collective-permute-start | bytes 1597448 | tf_op jit(solution)/shard_map/ppermute | solution.py:589
  52.4 1.6 %shard_map.131 = (f32[2,128,1024]{2,1,0:T(8,128)S(1)}, bf16[2,512,256]{2,1,0:T(8,128)(2,1)S(1)}, f32[4,512]{1,0:T(4,128)S(1)}) custom-call(s32[1,8]{1,0:T(1,128)S(1)} %copy-done.7, bf16[512,512]{1,0:T(8,128)(2,1)S(1)} %rotq.1.q_ref, bf16[512,512]{1,0:T(8,128)(2,1)S(1)} %convolution_convert_fusion.dy_ref, bf16[512,512]{1,0:T(8,128)(2,1)S(1)} %get-tuple-element.49.a_ref.o_ref, ...), custom_call_target="tpu_custom_call" | custom-call | flops 2684354560 | bytes 8388608 | tf_op jit(solution)/shard_map/pallas_call | solution.py:647
  54.1 2.7 %collective-permute-start.11 = (bf16[512,256]{1,0:T(8,128)(2,1)S(1)}, bf16[512,256]{1,0:T(8,128)(2,1)S(1)}, u32[]{:S(2)}, u32[]{:S(2)}) collective-permute-start(bf16[512,256]{1,0:T(8,128)(2,1)S(1)} %slice_bitcast_fusion.4), channel_id=1, source_target_pairs={{0,1},{2,3},{4,5},{6,7},{1,0},{3,2},{5,4},{7,6},{8,9},{10,11},{12,... | collective-permute-start | bytes 786440 | tf_op jit(solution)/shard_map/ppermute | solution.py:463
  58.0 1.7 %collective-permute-start.13 = (bf16[512,256]{1,0:T(8,128)(2,1)S(1)}, bf16[512,256]{1,0:T(8,128)(2,1)S(1)}, u32[]{:S(2)}, u32[]{:S(2)}) collective-permute-start(bf16[512,256]{1,0:T(8,128)(2,1)S(1)} %slice_bitcast_fusion.3), channel_id=1, source_target_pairs={{0,1},{2,3},{4,5},{6,7},{1,0},{3,2},{5,4},{7,6},{8,9},{10,11},{12,... | collective-permute-start | bytes 786440 | tf_op jit(solution)/shard_map/ppermute | solution.py:463
  59.9 3.9 %collective-permute-done.11 = bf16[512,256]{1,0:T(8,128)(2,1)S(1)} collective-permute-done((bf16[512,256]{1,0:T(8,128)(2,1)S(1)}, bf16[512,256]{1,0:T(8,128)(2,1)S(1)}, u32[]{:S(2)}, u32[]{:S(2)}) %collective-permute-start.11) | collective-permute-done | bytes 262176 | tf_op jit(solution)/shard_map/ppermute | solution.py:463
  65.3 2.7 %collective-permute-start.15 = (bf16[2,2,256,128]{3,2,0,1:T(8,128)(2,1)S(1)}, bf16[2,2,256,128]{3,2,0,1:T(8,128)(2,1)S(1)}, u32[]{:S(2)}, u32[]{:S(2)}) collective-permute-start(bf16[2,2,256,128]{3,2,0,1:T(8,128)(2,1)S(1)} %fusion.4), channel_id=1, source_target_pairs={{0,2},{1,3},{2,0},{3,1},{4,6},{5,7},{6,4},{7,5},{8,10},{9,11},{10,... | collective-permute-start | bytes 786440 | tf_op jit(solution)/shard_map/ppermute | solution.py:589
  68.4 5.3 %near.1 = (bf16[512,512]{1,0:T(8,128)(2,1)}, f32[512,256]{1,0:T(8,128)S(1)}) custom-call(s32[1,8]{1,0:T(1,128)S(1)} %copy-done.7, bf16[512,512]{1,0:T(8,128)(2,1)S(1)} %rotq.1.q_ref, bf16[512,512]{1,0:T(8,128)(2,1)S(1)} %convolution_convert_fusion.dy_ref, f32[4,512]{1,0:T(4,128)S(1)} %get-tuple-element.55.o_ref.delta_ref, ...), custom_call_target="tpu_custom_call" | custom-call | flops 1073741824 | bytes 4194304 | tf_op jit(solution)/shard_map/near/pallas_call | solution.py:693
  73.7 3.9 %collective-permute-done.15 = bf16[2,2,256,128]{3,2,0,1:T(8,128)(2,1)S(1)} collective-permute-done((bf16[2,2,256,128]{3,2,0,1:T(8,128)(2,1)S(1)}, bf16[2,2,256,128]{3,2,0,1:T(8,128)(2,1)S(1)}, u32[]{:S(2)}, u32[]{:S(2)}) %collective-permute-start.15) | collective-permute-done | bytes 262176 | tf_op jit(solution)/shard_map/ppermute | solution.py:589
  77.9 1.5 %collective-permute-start.17 = (bf16[1088,128]{1,0:T(8,128)(2,1)S(1)}, bf16[1088,128]{1,0:T(8,128)(2,1)S(1)}, u32[]{:S(2)}, u32[]{:S(2)}) collective-permute-start(bf16[1088,128]{1,0:T(8,128)(2,1)S(1)} %pad_maximum_fusion.1), channel_id=1, source_target_pairs={{0,1},{1,0},{2,3},{3,2},{4,5},{5,4},{6,7},{7,6},{8,9},{9,8},{10,11... | collective-permute-start | bytes 835592 | tf_op jit(solution)/shard_map/ppermute | solution.py:589
  80.9 3.6 %collective-permute-done.17 = bf16[1088,128]{1,0:T(8,128)(2,1)S(1)} collective-permute-done((bf16[1088,128]{1,0:T(8,128)(2,1)S(1)}, bf16[1088,128]{1,0:T(8,128)(2,1)S(1)}, u32[]{:S(2)}, u32[]{:S(2)}) %collective-permute-start.17) | collective-permute-done | bytes 278560 | tf_op jit(solution)/shard_map/ppermute | solution.py:589
  84.6 10.7 %collective-permute-start.18 = (bf16[640,128]{1,0:T(8,128)(2,1)S(1)}, bf16[640,128]{1,0:T(8,128)(2,1)S(1)}, u32[]{:S(2)}, u32[]{:S(2)}) collective-permute-start(bf16[640,128]{1,0:T(8,128)(2,1)S(1)} %pad_maximum_fusion.3), channel_id=1, source_target_pairs={{0,4},{1,5},{2,6},{3,7},{4,0},{5,1},{6,2},{7,3},{8,12},{9,13},{10,... | collective-permute-start | bytes 491528 | tf_op jit(solution)/shard_map/ppermute | solution.py:589
  96.2 7.1 %collective-permute-done.18.recv_ref = bf16[640,128]{1,0:T(8,128)(2,1)S(1)} collective-permute-done((bf16[640,128]{1,0:T(8,128)(2,1)S(1)}, bf16[640,128]{1,0:T(8,128)(2,1)S(1)}, u32[]{:S(2)}, u32[]{:S(2)}) %collective-permute-start.18) | collective-permute-done | bytes 163872 | tf_op jit(solution)/shard_map/ppermute | solution.py:589
  103.3 1.8 %final.1 = (f32[512,128]{1,0:T(8,128)}, f32[4,512]{1,0:T(4,128)}) custom-call(s32[64]{0:T(128)S(1)} %bitcast.91, bf16[512,128]{1,0:T(8,128)(2,1)S(1)} %get-tuple-element.83.one_ref, bf16[640,128]{1,0:T(8,128)(2,1)S(1)} %collective-permute-done.18.recv_ref, bf16[128,128]{1,0:T(8,128)(2,1)S(1)} %pad_maximum_fusion.5.lse_ref), custom_call_target="tpu_custom_call" | custom-call | flops 262144 | bytes 1048576 | tf_op jit(solution)/shard_map/final/pallas_call | solution.py:748
  (78 shorter events, 16.1 us)
Async XLA Ops:
  3.3 10.8 %collective-permute-start = (bf16[512,256]{1,0:T(8,128)(2,1)}, bf16[512,256]{1,0:T(8,128)(2,1)S(1)}, u32[]{:S(2)}, u32[]{:S(2)}) collective-permute-start(bf16[512,256]{1,0:T(8,128)(2,1)} %get-tuple-element.44.rest_0_.kv_ref), channel_id=1, source_target_pairs={{0,2},{1,3},{2,4},{3,5},{4,6},{5,7},{8,10},{9,11},{10,12},{11,13},... | collective-permute-start | bytes 786440 | tf_op jit(solution)/shard_map/ppermute | solution.py:463
  14.1 9.0 %collective-permute-start.1 = (bf16[512,256]{1,0:T(8,128)(2,1)S(1)}, bf16[512,256]{1,0:T(8,128)(2,1)S(1)}, u32[]{:S(2)}, u32[]{:S(2)}) collective-permute-start(bf16[512,256]{1,0:T(8,128)(2,1)S(1)} %collective-permute-done.rest_1_.rest_0_), channel_id=1, source_target_pairs={{0,2},{1,3},{2,4},{3,5},{4,6},{5,7},{8,10},{9,11},{10,12},{11,13},... | collective-permute-start | bytes 786440 | tf_op jit(solution)/shard_map/ppermute | solution.py:463
  18.4 10.4 %collective-permute-start.4 = (bf16[512,256]{1,0:T(8,128)(2,1)}, bf16[512,256]{1,0:T(8,128)(2,1)S(1)}, u32[]{:S(2)}, u32[]{:S(2)}) collective-permute-start(bf16[512,256]{1,0:T(8,128)(2,1)} %get-tuple-element.44.rest_0_.kv_ref), channel_id=1, source_target_pairs={{0,1},{2,3},{4,5},{6,7},{8,9},{10,11},{12,13},{14,15},{16,17},{18,... | collective-permute-start | bytes 786440 | tf_op jit(solution)/shard_map/ppermute | solution.py:463
  21.8 13.1 %collective-permute-start.2 = (bf16[512,256]{1,0:T(8,128)(2,1)S(1)}, bf16[512,256]{1,0:T(8,128)(2,1)S(1)}, u32[]{:S(2)}, u32[]{:S(2)}) collective-permute-start(bf16[512,256]{1,0:T(8,128)(2,1)S(1)} %collective-permute-done.rest_1_.rest_0_), channel_id=1, source_target_pairs={{0,1},{2,3},{4,5},{6,7},{1,0},{3,2},{5,4},{7,6},{8,9},{10,11},{12,... | collective-permute-start | bytes 786440 | tf_op jit(solution)/shard_map/ppermute | solution.py:463
  23.1 11.8 %collective-permute-start.3 = (bf16[512,256]{1,0:T(8,128)(2,1)S(1)}, bf16[512,256]{1,0:T(8,128)(2,1)S(1)}, u32[]{:S(2)}, u32[]{:S(2)}) collective-permute-start(bf16[512,256]{1,0:T(8,128)(2,1)S(1)} %collective-permute-done.1.rest_0_.rest_2_), channel_id=1, source_target_pairs={{1,0},{3,2},{5,4},{7,6},{9,8},{11,10},{13,12},{15,14},{17,16},{19,... | collective-permute-start | bytes 786440 | tf_op jit(solution)/shard_map/ppermute | solution.py:463
  24.4 13.5 %copy-start = (bf16[1,512,4096]{2,1,0:T(8,128)(2,1)S(1)}, bf16[1,512,4096]{2,1,0:T(8,128)(2,1)}, u32[]{:S(2)}) copy-start(bf16[1,512,4096]{2,1,0:T(8,128)(2,1)} %param.14) | copy-start | bytes 12582916
  41.1 5.2 %collective-permute-start.5 = (bf16[8,256,128]{2,1,0:T(8,128)(2,1)S(1)}, bf16[8,256,128]{2,1,0:T(8,128)(2,1)S(1)}, u32[]{:S(2)}, u32[]{:S(2)}) collective-permute-start(bf16[8,256,128]{2,1,0:T(8,128)(2,1)S(1)} %get-tuple-element.53), channel_id=1, source_target_pairs={{0,8},{8,0},{16,24},{24,16},{1,9},{9,1},{17,25},{25,17},{2,10},{10... | collective-permute-start | bytes 1572872 | tf_op jit(solution)/shard_map/ppermute | solution.py:589
  41.1 5.1 %collective-permute-start.9 = (bf16[8,256,128]{2,1,0:T(8,128)(2,1)S(1)}, bf16[8,256,128]{2,1,0:T(8,128)(2,1)S(1)}, u32[]{:S(2)}, u32[]{:S(2)}) collective-permute-start(bf16[8,256,128]{2,1,0:T(8,128)(2,1)S(1)} %get-tuple-element.64), channel_id=1, source_target_pairs={{0,8},{8,0},{16,24},{24,16},{1,9},{9,1},{17,25},{25,17},{2,10},{10... | collective-permute-start | bytes 1572872 | tf_op jit(solution)/shard_map/ppermute | solution.py:589
  44.0 14.0 %collective-permute-start.6 = (bf16[8,256,128]{2,1,0:T(8,128)(2,1)S(1)}, bf16[8,256,128]{2,1,0:T(8,128)(2,1)S(1)}, u32[]{:S(2)}, u32[]{:S(2)}) collective-permute-start(bf16[8,256,128]{2,1,0:T(8,128)(2,1)S(1)} %get-tuple-element.59), channel_id=1, source_target_pairs={{0,8},{8,0},{16,24},{24,16},{1,9},{9,1},{17,25},{25,17},{2,10},{10... | collective-permute-start | bytes 1572872 | tf_op jit(solution)/shard_map/ppermute | solution.py:589
  44.1 15.7 %collective-permute-start.8 = (bf16[8,256,128]{2,1,0:T(8,128)(2,1)S(1)}, bf16[8,256,128]{2,1,0:T(8,128)(2,1)S(1)}, u32[]{:S(2)}, u32[]{:S(2)}) collective-permute-start(bf16[8,256,128]{2,1,0:T(8,128)(2,1)S(1)} %get-tuple-element.62), channel_id=1, source_target_pairs={{0,8},{8,0},{16,24},{24,16},{1,9},{9,1},{17,25},{25,17},{2,10},{10... | collective-permute-start | bytes 1572872 | tf_op jit(solution)/shard_map/ppermute | solution.py:589
  46.6 18.6 %collective-permute-start.7 = (bf16[2,2,2,256,128]{4,3,0,2,1:T(8,128)(2,1)S(1)}, bf16[2,2,2,256,128]{4,3,0,2,1:T(8,128)(2,1)S(1)}, u32[]{:S(2)}, u32[]{:S(2)}) collective-permute-start(bf16[2,2,2,256,128]{4,3,0,2,1:T(8,128)(2,1)S(1)} %copy.18), channel_id=1, source_target_pairs={{0,16},{8,24},{16,0},{24,8},{1,17},{9,25},{17,1},{25,9},{2,18},{10... | collective-permute-start | bytes 1572872 | tf_op jit(solution)/shard_map/ppermute | solution.py:589
  48.2 19.8 %collective-permute-start.10 = (bf16[2080,128]{1,0:T(8,128)(2,1)S(1)}, bf16[2080,128]{1,0:T(8,128)(2,1)S(1)}, u32[]{:S(2)}, u32[]{:S(2)}) collective-permute-start(bf16[2080,128]{1,0:T(8,128)(2,1)S(1)} %pad_maximum_fusion), channel_id=1, source_target_pairs={{0,2},{1,3},{2,0},{3,1},{4,6},{5,7},{6,4},{7,5},{8,10},{9,11},{10,... | collective-permute-start | bytes 1597448 | tf_op jit(solution)/shard_map/ppermute | solution.py:589
  54.1 9.7 %collective-permute-start.11 = (bf16[512,256]{1,0:T(8,128)(2,1)S(1)}, bf16[512,256]{1,0:T(8,128)(2,1)S(1)}, u32[]{:S(2)}, u32[]{:S(2)}) collective-permute-start(bf16[512,256]{1,0:T(8,128)(2,1)S(1)} %slice_bitcast_fusion.4), channel_id=1, source_target_pairs={{0,1},{2,3},{4,5},{6,7},{1,0},{3,2},{5,4},{7,6},{8,9},{10,11},{12,... | collective-permute-start | bytes 786440 | tf_op jit(solution)/shard_map/ppermute | solution.py:463
  58.0 21.4 %collective-permute-start.13 = (bf16[512,256]{1,0:T(8,128)(2,1)S(1)}, bf16[512,256]{1,0:T(8,128)(2,1)S(1)}, u32[]{:S(2)}, u32[]{:S(2)}) collective-permute-start(bf16[512,256]{1,0:T(8,128)(2,1)S(1)} %slice_bitcast_fusion.3), channel_id=1, source_target_pairs={{0,1},{2,3},{4,5},{6,7},{1,0},{3,2},{5,4},{7,6},{8,9},{10,11},{12,... | collective-permute-start | bytes 786440 | tf_op jit(solution)/shard_map/ppermute | solution.py:463
  59.7 8.6 %copy-start.2 = (f32[512,128]{1,0:T(8,128)S(1)}, f32[512,128]{1,0:T(8,128)}, u32[]{:S(2)}) copy-start(f32[512,128]{1,0:T(8,128)} %get-tuple-element.42.cos_ref) | copy-start | bytes 786436
  59.7 8.6 %copy-start.4 = (f32[512,128]{1,0:T(8,128)S(1)}, f32[512,128]{1,0:T(8,128)}, u32[]{:S(2)}) copy-start(f32[512,128]{1,0:T(8,128)} %get-tuple-element.43.sin_ref) | copy-start | bytes 786436
  59.7 8.7 %copy-start.10 = (bf16[512,256]{1,0:T(8,128)(2,1)S(1)}, bf16[512,256]{1,0:T(8,128)(2,1)}, u32[]{:S(2)}) copy-start(bf16[512,256]{1,0:T(8,128)(2,1)} %get-tuple-element.44.rest_0_.kv_ref) | copy-start | bytes 786436
  63.9 15.6 %collective-permute-start.12 = (bf16[512,256]{1,0:T(8,128)(2,1)S(1)}, bf16[512,256]{1,0:T(8,128)(2,1)S(1)}, u32[]{:S(2)}, u32[]{:S(2)}) collective-permute-start(bf16[512,256]{1,0:T(8,128)(2,1)S(1)} %fusion), channel_id=1, source_target_pairs={{2,0},{3,1},{4,2},{5,3},{6,4},{7,5},{10,8},{11,9},{12,10},{13,11},... | collective-permute-start | bytes 786440 | tf_op jit(solution)/shard_map/ppermute | solution.py:463
  65.3 12.3 %collective-permute-start.15 = (bf16[2,2,256,128]{3,2,0,1:T(8,128)(2,1)S(1)}, bf16[2,2,256,128]{3,2,0,1:T(8,128)(2,1)S(1)}, u32[]{:S(2)}, u32[]{:S(2)}) collective-permute-start(bf16[2,2,256,128]{3,2,0,1:T(8,128)(2,1)S(1)} %fusion.4), channel_id=1, source_target_pairs={{0,2},{1,3},{2,0},{3,1},{4,6},{5,7},{6,4},{7,5},{8,10},{9,11},{10,... | collective-permute-start | bytes 786440 | tf_op jit(solution)/shard_map/ppermute | solution.py:589
  68.1 9.6 %collective-permute-start.16 = (bf16[2,2,256,128]{3,2,0,1:T(8,128)(2,1)S(1)}, bf16[2,2,256,128]{3,2,0,1:T(8,128)(2,1)S(1)}, u32[]{:S(2)}, u32[]{:S(2)}) collective-permute-start(bf16[2,2,256,128]{3,2,0,1:T(8,128)(2,1)S(1)} %fusion.3), channel_id=1, source_target_pairs={{0,16},{8,24},{16,0},{24,8},{1,17},{9,25},{17,1},{25,9},{2,18},{10... | collective-permute-start | bytes 786440 | tf_op jit(solution)/shard_map/ppermute | solution.py:589
  73.7 29.6 %copy-start.8 = (s32[1,64]{1,0:T(1,128)S(1)}, s32[1,64]{1,0:T(1,128)}, u32[]{:S(2)}) copy-start(s32[1,64]{1,0:T(1,128)} %param.12) | copy-start | bytes 772
  77.9 6.6 %collective-permute-start.17 = (bf16[1088,128]{1,0:T(8,128)(2,1)S(1)}, bf16[1088,128]{1,0:T(8,128)(2,1)S(1)}, u32[]{:S(2)}, u32[]{:S(2)}) collective-permute-start(bf16[1088,128]{1,0:T(8,128)(2,1)S(1)} %pad_maximum_fusion.1), channel_id=1, source_target_pairs={{0,1},{1,0},{2,3},{3,2},{4,5},{5,4},{6,7},{7,6},{8,9},{9,8},{10,11... | collective-permute-start | bytes 835592 | tf_op jit(solution)/shard_map/ppermute | solution.py:589
  79.6 15.8 %collective-permute-start.14 = (bf16[512,256]{1,0:T(8,128)(2,1)S(1)}, bf16[512,256]{1,0:T(8,128)(2,1)S(1)}, u32[]{:S(2)}, u32[]{:S(2)}) collective-permute-start(bf16[512,256]{1,0:T(8,128)(2,1)S(1)} %fusion.2), channel_id=1, source_target_pairs={{2,0},{3,1},{4,2},{5,3},{6,4},{7,5},{10,8},{11,9},{12,10},{13,11},... | collective-permute-start | bytes 786440 | tf_op jit(solution)/shard_map/ppermute | solution.py:463
  84.6 18.7 %collective-permute-start.18 = (bf16[640,128]{1,0:T(8,128)(2,1)S(1)}, bf16[640,128]{1,0:T(8,128)(2,1)S(1)}, u32[]{:S(2)}, u32[]{:S(2)}) collective-permute-start(bf16[640,128]{1,0:T(8,128)(2,1)S(1)} %pad_maximum_fusion.3), channel_id=1, source_target_pairs={{0,4},{1,5},{2,6},{3,7},{4,0},{5,1},{6,2},{7,3},{8,12},{9,13},{10,... | collective-permute-start | bytes 491528 | tf_op jit(solution)/shard_map/ppermute | solution.py:589
  (7 other events, 17.9 us)

commit v5 on v4

--- a/solution.py
+++ b/solution.py
@@ -246,9 +246,7 @@
     lines = jnp.concatenate(
         [lse[:, c * HEAD : (c + 1) * HEAD] for c in range(rows // HEAD)], axis=0
     )
-    coarse = lines.astype(BF16)
-    fine = (lines - coarse.astype(F32)).astype(BF16)
-    pack_ref[0] = jnp.concatenate([coarse, fine], axis=0)
+    pack_ref[0] = lines.astype(BF16)
 
 
 def delta_of(dy_ref, o_ref):
@@ -417,8 +415,8 @@
             chunk, lane = divmod(rest, HEAD)
             parts = []
             for h in range(heads):
-                row = half * 2 * of_half + h * chunks + chunk
-                line = raw[row : row + 1] + raw[row + of_half : row + of_half + 1]
+                row = half * of_half + h * chunks + chunk
+                line = raw[row : row + 1]
                 parts.append(line[:, lane : lane + block_len])
             mine = jnp.where(owner_ref[c * n_ctx + s] == dev, jnp.concatenate(parts, axis=0), mine)
         out_ref[:, c * block_len : (c + 1) * block_len] = mine
@@ -504,7 +502,7 @@
     dq_spec = pl.BlockSpec((1, HEAD, heads * qb), lambda i: (i, 0, 0))
     stat_spec = pl.BlockSpec((1, 16, heads * qb), lambda i: (i, 0, 0))
     pairs = heads * tok * (tok + reach) // 2
-    pack_rows = 2 * heads * qb // HEAD
+    pack_rows = heads * qb // HEAD
     steps = tok // qb
     state = [(sds((steps, HEAD, heads * qb), F32), dq_spec), (sds((steps, 16, heads * qb), F32), stat_spec)]
     result = [

time: 105 us -> 105 us (level)
  no operation moved by 1% of the time
where the time goes in v5:
time: 105 us
  starting transfers between devices  42.9 us (41%)
  Pallas kernels  25.8 us (25%)
  waiting for transfers between devices  25.8 us (25%)
  local copies, waits for them, and re-layouts  5.24 us (5%)
  matrix products  2.56 us (2%)
  other arithmetic  1.22 us (1%)
  between operations  1.08 us (1%)
    ppermute x10, starting transfers between devices, exchange(): return lax.ppermute(x, axis, [(i, i ^ bit) for i in range(size)])  22 us
    ppermute x9, starting transfers between devices, shift(): return lax.ppermute(x, 'ctx', pairs)  20.9 us
    ppermute x10, waiting for transfers between devices, exchange(): return lax.ppermute(x, axis, [(i, i ^ bit) for i in range(size)])  14 us
    ppermute x9, waiting for transfers between devices, shift(): return lax.ppermute(x, 'ctx', pairs)  11.7 us
    pallas_call x2, Pallas kernels, forward(): pl.pallas_call(functools.partial(fwd_kernel, picks, back, bool(before), f...  7.42 us
    pallas_call x1, Pallas kernels, on_device(): pl.pallas_call(functools.partial(near_kernel, near_kb), grid=(tok // qb,)...  5.28 us
    unnamed x24, local copies, waits for them, and re-layouts  4.95 us
    pallas_call x2, Pallas kernels, partial_wo(): pl.pallas_call(functools.partial(wo_kernel, core), out_shape=shapes_of(si...  4.74 us
  transfers between devices with their start and end apart: 19, of which 7 were waited for; matrix products, arithmetic and copies ran while one was open for 4% of the time, Pallas kernels for 15%

profile of v5, /device:TPU:0, one launch (start us, length us, event | category | flops | bytes accessed | tf_op | source)
XLA Modules:
  0.0 104.6 jit_solution(7341054179606056625)
XLA Ops:
  0.6 2.6 %prep.1 = (bf16[512,256]{1,0:T(8,128)(2,1)}, f32[512,128]{1,0:T(8,128)}, f32[512,128]{1,0:T(8,128)}) custom-call(s32[1,8]{1,0:T(1,128)} %lens_ref.11, f32[1,128]{1,0:T(1,128)} %constant.22.clone.freq_ref, bf16[512,128]{1,0:T(8,128)(2,1)} %bitcast.101, bf16[512,128]{1,0:T(8,128)(2,1)} %bitcast.102), custom_call_target="tpu_custom_call" | custom-call | flops 4194304 | bytes 1048576 | tf_op jit(solution)/shard_map/prep/pallas_call | solution.py:471
  3.3 5.0 %collective-permute-start = (bf16[512,256]{1,0:T(8,128)(2,1)}, bf16[512,256]{1,0:T(8,128)(2,1)S(1)}, u32[]{:S(2)}, u32[]{:S(2)}) collective-permute-start(bf16[512,256]{1,0:T(8,128)(2,1)} %get-tuple-element.44.rest_0_.kv_ref), channel_id=1, source_target_pairs={{0,2},{1,3},{2,4},{3,5},{4,6},{5,7},{8,10},{9,11},{10,12},{11,13},... | collective-permute-start | bytes 786440 | tf_op jit(solution)/shard_map/ppermute | solution.py:461
  8.2 5.8 %collective-permute-done.rest_1_.rest_0_ = bf16[512,256]{1,0:T(8,128)(2,1)S(1)} collective-permute-done((bf16[512,256]{1,0:T(8,128)(2,1)}, bf16[512,256]{1,0:T(8,128)(2,1)S(1)}, u32[]{:S(2)}, u32[]{:S(2)}) %collective-permute-start) | collective-permute-done | bytes 262176 | tf_op jit(solution)/shard_map/ppermute | solution.py:461
  14.1 4.3 %collective-permute-start.1 = (bf16[512,256]{1,0:T(8,128)(2,1)S(1)}, bf16[512,256]{1,0:T(8,128)(2,1)S(1)}, u32[]{:S(2)}, u32[]{:S(2)}) collective-permute-start(bf16[512,256]{1,0:T(8,128)(2,1)S(1)} %collective-permute-done.rest_1_.rest_0_), channel_id=1, source_target_pairs={{0,2},{1,3},{2,4},{3,5},{4,6},{5,7},{8,10},{9,11},{10,12},{11,13},... | collective-permute-start | bytes 786440 | tf_op jit(solution)/shard_map/ppermute | solution.py:461
  18.4 3.4 %collective-permute-start.4 = (bf16[512,256]{1,0:T(8,128)(2,1)}, bf16[512,256]{1,0:T(8,128)(2,1)S(1)}, u32[]{:S(2)}, u32[]{:S(2)}) collective-permute-start(bf16[512,256]{1,0:T(8,128)(2,1)} %get-tuple-element.44.rest_0_.kv_ref), channel_id=1, source_target_pairs={{0,1},{2,3},{4,5},{6,7},{8,9},{10,11},{12,13},{14,15},{16,17},{18,... | collective-permute-start | bytes 786440 | tf_op jit(solution)/shard_map/ppermute | solution.py:461
  30.4 4.5 %shard_map.127 = (f32[2,128,1024]{2,1,0:T(8,128)S(1)}, f32[2,16,1024]{2,1,0:T(8,128)S(1)}) custom-call(s32[1,8]{1,0:T(1,128)S(1)} %copy-done.6, bf16[512,512]{1,0:T(8,128)(2,1)S(1)} %rotq.1.q_ref, bf16[512,256]{1,0:T(8,128)(2,1)S(1)} %copy-done.9, bf16[512,256]{1,0:T(8,128)(2,1)S(1)} %collective-permute-done.rest_1_.rest_0_, ...), custom_call_target="tpu_custom_call" | custom-call | flops 671088640 | bytes 4194304 | tf_op jit(solution)/shard_map/pallas_call | solution.py:517
  34.9 3.0 %shard_map.128 = (bf16[512,512]{1,0:T(8,128)(2,1)}, bf16[512,512]{1,0:T(8,128)(2,1)S(1)}, f32[4,512]{1,0:T(4,128)S(1)}, bf16[2,8,128]{2,1,0:T(8,128)(2,1)S(1)}) custom-call(s32[1,8]{1,0:T(1,128)S(1)} %copy-done.6, bf16[512,512]{1,0:T(8,128)(2,1)S(1)} %rotq.1.q_ref, bf16[512,256]{1,0:T(8,128)(2,1)S(1)} %collective-permute-done.1.rest_0_.rest_2_, ...), custom_call_target="tpu_custom_call" | custom-call | flops 671088640 | bytes 4194304 | tf_op jit(solution)/shard_map/pallas_call | solution.py:517
  37.9 3.2 %shard_map.129 = (bf16[8,256,128]{2,1,0:T(8,128)(2,1)S(1)}, bf16[8,256,128]{2,1,0:T(8,128)(2,1)S(1)}, bf16[8,256,128]{2,1,0:T(8,128)(2,1)S(1)}, bf16[8,256,128]{...) custom-call(bf16[512,512]{1,0:T(8,128)(2,1)S(1)} %get-tuple-element.49.a_ref.o_ref, bf16[512,4096]{1,0:T(8,128)(2,1)S(1)} %bitcast.83), custom_call_target="tpu_custom_call" | custom-call | flops 1073741824 | bytes 6291456 | tf_op jit(solution)/shard_map/pallas_call | solution.py:563
  41.6 2.6 %convolution_convert_fusion.dy_ref = bf16[512,512]{1,0:T(8,128)(2,1)S(1)} fusion(bf16[512,4096]{1,0:T(8,128)(2,1)S(1)} %bitcast.84, bf16[512,4096]{1,0:T(8,128)(2,1)S(1)} %copy-done.11), kind=kOutput, calls=%fused_computation | convolution fusion | flops 2147745792 | bytes 8912896 | tf_op jit(solution)/shard_map/dot_general | solution.py:482
  44.8 1.6 %shard_map.130 = (bf16[8,256,128]{2,1,0:T(8,128)(2,1)S(1)}, bf16[8,256,128]{2,1,0:T(8,128)(2,1)S(1)}, bf16[8,256,128]{2,1,0:T(8,128)(2,1)S(1)}, bf16[8,256,128]{2,1,0:T(8,128)(2,1)S(1)}) custom-call(bf16[512,512]{1,0:T(8,128)(2,1)S(1)} %get-tuple-element.49.a_ref.o_ref, bf16[2,512,1024]{2,1,0:T(8,128)(2,1)S(1)} %get-tuple-element.51.g_ref), custom_call_target="tpu_custom_call" | custom-call | flops 1073741824 | bytes 6291456 | tf_op jit(solution)/shard_map/pallas_call | solution.py:563
  46.8 1.6 %collective-permute-start.7 = (bf16[2,2,2,256,128]{4,3,0,2,1:T(8,128)(2,1)S(1)}, bf16[2,2,2,256,128]{4,3,0,2,1:T(8,128)(2,1)S(1)}, u32[]{:S(2)}, u32[]{:S(2)}) collective-permute-start(bf16[2,2,2,256,128]{4,3,0,2,1:T(8,128)(2,1)S(1)} %copy.18), channel_id=1, source_target_pairs={{0,16},{8,24},{16,0},{24,8},{1,17},{9,25},{17,1},{25,9},{2,18},{10... | collective-permute-start | bytes 1572872 | tf_op jit(solution)/shard_map/ppermute | solution.py:587
  48.4 4.3 %collective-permute-start.10 = (bf16[2064,128]{1,0:T(8,128)(2,1)S(1)}, bf16[2064,128]{1,0:T(8,128)(2,1)S(1)}, u32[]{:S(2)}, u32[]{:S(2)}) collective-permute-start(bf16[2064,128]{1,0:T(8,128)(2,1)S(1)} %pad_maximum_fusion), channel_id=1, source_target_pairs={{0,2},{1,3},{2,0},{3,1},{4,6},{5,7},{6,4},{7,5},{8,10},{9,11},{10,... | collective-permute-start | bytes 1585160 | tf_op jit(solution)/shard_map/ppermute | solution.py:587
  52.7 1.6 %shard_map.131 = (f32[2,128,1024]{2,1,0:T(8,128)S(1)}, bf16[2,512,256]{2,1,0:T(8,128)(2,1)S(1)}, f32[4,512]{1,0:T(4,128)S(1)}) custom-call(s32[1,8]{1,0:T(1,128)S(1)} %copy-done.7, bf16[512,512]{1,0:T(8,128)(2,1)S(1)} %rotq.1.q_ref, bf16[512,512]{1,0:T(8,128)(2,1)S(1)} %convolution_convert_fusion.dy_ref, bf16[512,512]{1,0:T(8,128)(2,1)S(1)} %get-tuple-element.49.a_ref.o_ref, ...), custom_call_target="tpu_custom_call" | custom-call | flops 2684354560 | bytes 8388608 | tf_op jit(solution)/shard_map/pallas_call | solution.py:645
  54.4 2.6 %collective-permute-start.11 = (bf16[512,256]{1,0:T(8,128)(2,1)S(1)}, bf16[512,256]{1,0:T(8,128)(2,1)S(1)}, u32[]{:S(2)}, u32[]{:S(2)}) collective-permute-start(bf16[512,256]{1,0:T(8,128)(2,1)S(1)} %slice_bitcast_fusion.4), channel_id=1, source_target_pairs={{0,1},{2,3},{4,5},{6,7},{1,0},{3,2},{5,4},{7,6},{8,9},{10,11},{12,... | collective-permute-start | bytes 786440 | tf_op jit(solution)/shard_map/ppermute | solution.py:461
  58.2 1.7 %collective-permute-start.13 = (bf16[512,256]{1,0:T(8,128)(2,1)S(1)}, bf16[512,256]{1,0:T(8,128)(2,1)S(1)}, u32[]{:S(2)}, u32[]{:S(2)}) collective-permute-start(bf16[512,256]{1,0:T(8,128)(2,1)S(1)} %slice_bitcast_fusion.3), channel_id=1, source_target_pairs={{0,1},{2,3},{4,5},{6,7},{1,0},{3,2},{5,4},{7,6},{8,9},{10,11},{12,... | collective-permute-start | bytes 786440 | tf_op jit(solution)/shard_map/ppermute | solution.py:461
  60.1 3.9 %collective-permute-done.11 = bf16[512,256]{1,0:T(8,128)(2,1)S(1)} collective-permute-done((bf16[512,256]{1,0:T(8,128)(2,1)S(1)}, bf16[512,256]{1,0:T(8,128)(2,1)S(1)}, u32[]{:S(2)}, u32[]{:S(2)}) %collective-permute-start.11) | collective-permute-done | bytes 262176 | tf_op jit(solution)/shard_map/ppermute | solution.py:461
  65.5 2.7 %collective-permute-start.15 = (bf16[2,2,256,128]{3,2,0,1:T(8,128)(2,1)S(1)}, bf16[2,2,256,128]{3,2,0,1:T(8,128)(2,1)S(1)}, u32[]{:S(2)}, u32[]{:S(2)}) collective-permute-start(bf16[2,2,256,128]{3,2,0,1:T(8,128)(2,1)S(1)} %fusion.4), channel_id=1, source_target_pairs={{0,2},{1,3},{2,0},{3,1},{4,6},{5,7},{6,4},{7,5},{8,10},{9,11},{10,... | collective-permute-start | bytes 786440 | tf_op jit(solution)/shard_map/ppermute | solution.py:587
  68.6 5.3 %near.1 = (bf16[512,512]{1,0:T(8,128)(2,1)}, f32[512,256]{1,0:T(8,128)S(1)}) custom-call(s32[1,8]{1,0:T(1,128)S(1)} %copy-done.7, bf16[512,512]{1,0:T(8,128)(2,1)S(1)} %rotq.1.q_ref, bf16[512,512]{1,0:T(8,128)(2,1)S(1)} %convolution_convert_fusion.dy_ref, f32[4,512]{1,0:T(4,128)S(1)} %get-tuple-element.55.o_ref.delta_ref, ...), custom_call_target="tpu_custom_call" | custom-call | flops 1073741824 | bytes 4194304 | tf_op jit(solution)/shard_map/near/pallas_call | solution.py:691
  73.9 3.9 %collective-permute-done.15 = bf16[2,2,256,128]{3,2,0,1:T(8,128)(2,1)S(1)} collective-permute-done((bf16[2,2,256,128]{3,2,0,1:T(8,128)(2,1)S(1)}, bf16[2,2,256,128]{3,2,0,1:T(8,128)(2,1)S(1)}, u32[]{:S(2)}, u32[]{:S(2)}) %collective-permute-start.15) | collective-permute-done | bytes 262176 | tf_op jit(solution)/shard_map/ppermute | solution.py:587
  78.1 1.5 %collective-permute-start.17 = (bf16[1056,128]{1,0:T(8,128)(2,1)S(1)}, bf16[1056,128]{1,0:T(8,128)(2,1)S(1)}, u32[]{:S(2)}, u32[]{:S(2)}) collective-permute-start(bf16[1056,128]{1,0:T(8,128)(2,1)S(1)} %pad_maximum_fusion.1), channel_id=1, source_target_pairs={{0,1},{1,0},{2,3},{3,2},{4,5},{5,4},{6,7},{7,6},{8,9},{9,8},{10,11... | collective-permute-start | bytes 811016 | tf_op jit(solution)/shard_map/ppermute | solution.py:587
  81.1 3.5 %collective-permute-done.17 = bf16[1056,128]{1,0:T(8,128)(2,1)S(1)} collective-permute-done((bf16[1056,128]{1,0:T(8,128)(2,1)S(1)}, bf16[1056,128]{1,0:T(8,128)(2,1)S(1)}, u32[]{:S(2)}, u32[]{:S(2)}) %collective-permute-start.17) | collective-permute-done | bytes 270368 | tf_op jit(solution)/shard_map/ppermute | solution.py:587
  84.8 10.6 %collective-permute-start.18 = (bf16[576,128]{1,0:T(8,128)(2,1)S(1)}, bf16[576,128]{1,0:T(8,128)(2,1)S(1)}, u32[]{:S(2)}, u32[]{:S(2)}) collective-permute-start(bf16[576,128]{1,0:T(8,128)(2,1)S(1)} %pad_maximum_fusion.3), channel_id=1, source_target_pairs={{0,4},{1,5},{2,6},{3,7},{4,0},{5,1},{6,2},{7,3},{8,12},{9,13},{10,... | collective-permute-start | bytes 442376 | tf_op jit(solution)/shard_map/ppermute | solution.py:587
  96.2 6.6 %collective-permute-done.18.recv_ref = bf16[576,128]{1,0:T(8,128)(2,1)S(1)} collective-permute-done((bf16[576,128]{1,0:T(8,128)(2,1)S(1)}, bf16[576,128]{1,0:T(8,128)(2,1)S(1)}, u32[]{:S(2)}, u32[]{:S(2)}) %collective-permute-start.18) | collective-permute-done | bytes 147488 | tf_op jit(solution)/shard_map/ppermute | solution.py:587
  102.8 1.8 %final.1 = (f32[512,128]{1,0:T(8,128)}, f32[4,512]{1,0:T(4,128)}) custom-call(s32[64]{0:T(128)S(1)} %bitcast.91, bf16[512,128]{1,0:T(8,128)(2,1)S(1)} %get-tuple-element.83.one_ref, bf16[576,128]{1,0:T(8,128)(2,1)S(1)} %collective-permute-done.18.recv_ref, bf16[64,128]{1,0:T(8,128)(2,1)S(1)} %pad_maximum_fusion.5.lse_ref), custom_call_target="tpu_custom_call" | custom-call | flops 262144 | bytes 1048576 | tf_op jit(solution)/shard_map/final/pallas_call | solution.py:746
  (78 shorter events, 16.1 us)
Async XLA Ops:
  3.3 10.8 %collective-permute-start = (bf16[512,256]{1,0:T(8,128)(2,1)}, bf16[512,256]{1,0:T(8,128)(2,1)S(1)}, u32[]{:S(2)}, u32[]{:S(2)}) collective-permute-start(bf16[512,256]{1,0:T(8,128)(2,1)} %get-tuple-element.44.rest_0_.kv_ref), channel_id=1, source_target_pairs={{0,2},{1,3},{2,4},{3,5},{4,6},{5,7},{8,10},{9,11},{10,12},{11,13},... | collective-permute-start | bytes 786440 | tf_op jit(solution)/shard_map/ppermute | solution.py:461
  14.1 9.0 %collective-permute-start.1 = (bf16[512,256]{1,0:T(8,128)(2,1)S(1)}, bf16[512,256]{1,0:T(8,128)(2,1)S(1)}, u32[]{:S(2)}, u32[]{:S(2)}) collective-permute-start(bf16[512,256]{1,0:T(8,128)(2,1)S(1)} %collective-permute-done.rest_1_.rest_0_), channel_id=1, source_target_pairs={{0,2},{1,3},{2,4},{3,5},{4,6},{5,7},{8,10},{9,11},{10,12},{11,13},... | collective-permute-start | bytes 786440 | tf_op jit(solution)/shard_map/ppermute | solution.py:461
  18.4 10.4 %collective-permute-start.4 = (bf16[512,256]{1,0:T(8,128)(2,1)}, bf16[512,256]{1,0:T(8,128)(2,1)S(1)}, u32[]{:S(2)}, u32[]{:S(2)}) collective-permute-start(bf16[512,256]{1,0:T(8,128)(2,1)} %get-tuple-element.44.rest_0_.kv_ref), channel_id=1, source_target_pairs={{0,1},{2,3},{4,5},{6,7},{8,9},{10,11},{12,13},{14,15},{16,17},{18,... | collective-permute-start | bytes 786440 | tf_op jit(solution)/shard_map/ppermute | solution.py:461
  21.8 13.1 %collective-permute-start.2 = (bf16[512,256]{1,0:T(8,128)(2,1)S(1)}, bf16[512,256]{1,0:T(8,128)(2,1)S(1)}, u32[]{:S(2)}, u32[]{:S(2)}) collective-permute-start(bf16[512,256]{1,0:T(8,128)(2,1)S(1)} %collective-permute-done.rest_1_.rest_0_), channel_id=1, source_target_pairs={{0,1},{2,3},{4,5},{6,7},{1,0},{3,2},{5,4},{7,6},{8,9},{10,11},{12,... | collective-permute-start | bytes 786440 | tf_op jit(solution)/shard_map/ppermute | solution.py:461
  23.1 11.8 %collective-permute-start.3 = (bf16[512,256]{1,0:T(8,128)(2,1)S(1)}, bf16[512,256]{1,0:T(8,128)(2,1)S(1)}, u32[]{:S(2)}, u32[]{:S(2)}) collective-permute-start(bf16[512,256]{1,0:T(8,128)(2,1)S(1)} %collective-permute-done.1.rest_0_.rest_2_), channel_id=1, source_target_pairs={{1,0},{3,2},{5,4},{7,6},{9,8},{11,10},{13,12},{15,14},{17,16},{19,... | collective-permute-start | bytes 786440 | tf_op jit(solution)/shard_map/ppermute | solution.py:461
  24.4 13.5 %copy-start = (bf16[1,512,4096]{2,1,0:T(8,128)(2,1)S(1)}, bf16[1,512,4096]{2,1,0:T(8,128)(2,1)}, u32[]{:S(2)}) copy-start(bf16[1,512,4096]{2,1,0:T(8,128)(2,1)} %param.14) | copy-start | bytes 12582916
  41.1 5.4 %collective-permute-start.5 = (bf16[8,256,128]{2,1,0:T(8,128)(2,1)S(1)}, bf16[8,256,128]{2,1,0:T(8,128)(2,1)S(1)}, u32[]{:S(2)}, u32[]{:S(2)}) collective-permute-start(bf16[8,256,128]{2,1,0:T(8,128)(2,1)S(1)} %get-tuple-element.53), channel_id=1, source_target_pairs={{0,8},{8,0},{16,24},{24,16},{1,9},{9,1},{17,25},{25,17},{2,10},{10... | collective-permute-start | bytes 1572872 | tf_op jit(solution)/shard_map/ppermute | solution.py:587
  41.1 5.3 %collective-permute-start.9 = (bf16[8,256,128]{2,1,0:T(8,128)(2,1)S(1)}, bf16[8,256,128]{2,1,0:T(8,128)(2,1)S(1)}, u32[]{:S(2)}, u32[]{:S(2)}) collective-permute-start(bf16[8,256,128]{2,1,0:T(8,128)(2,1)S(1)} %get-tuple-element.64), channel_id=1, source_target_pairs={{0,8},{8,0},{16,24},{24,16},{1,9},{9,1},{17,25},{25,17},{2,10},{10... | collective-permute-start | bytes 1572872 | tf_op jit(solution)/shard_map/ppermute | solution.py:587
  44.2 14.0 %collective-permute-start.6 = (bf16[8,256,128]{2,1,0:T(8,128)(2,1)S(1)}, bf16[8,256,128]{2,1,0:T(8,128)(2,1)S(1)}, u32[]{:S(2)}, u32[]{:S(2)}) collective-permute-start(bf16[8,256,128]{2,1,0:T(8,128)(2,1)S(1)} %get-tuple-element.59), channel_id=1, source_target_pairs={{0,8},{8,0},{16,24},{24,16},{1,9},{9,1},{17,25},{25,17},{2,10},{10... | collective-permute-start | bytes 1572872 | tf_op jit(solution)/shard_map/ppermute | solution.py:587
  44.3 15.7 %collective-permute-start.8 = (bf16[8,256,128]{2,1,0:T(8,128)(2,1)S(1)}, bf16[8,256,128]{2,1,0:T(8,128)(2,1)S(1)}, u32[]{:S(2)}, u32[]{:S(2)}) collective-permute-start(bf16[8,256,128]{2,1,0:T(8,128)(2,1)S(1)} %get-tuple-element.62), channel_id=1, source_target_pairs={{0,8},{8,0},{16,24},{24,16},{1,9},{9,1},{17,25},{25,17},{2,10},{10... | collective-permute-start | bytes 1572872 | tf_op jit(solution)/shard_map/ppermute | solution.py:587
  46.8 18.6 %collective-permute-start.7 = (bf16[2,2,2,256,128]{4,3,0,2,1:T(8,128)(2,1)S(1)}, bf16[2,2,2,256,128]{4,3,0,2,1:T(8,128)(2,1)S(1)}, u32[]{:S(2)}, u32[]{:S(2)}) collective-permute-start(bf16[2,2,2,256,128]{4,3,0,2,1:T(8,128)(2,1)S(1)} %copy.18), channel_id=1, source_target_pairs={{0,16},{8,24},{16,0},{24,8},{1,17},{9,25},{17,1},{25,9},{2,18},{10... | collective-permute-start | bytes 1572872 | tf_op jit(solution)/shard_map/ppermute | solution.py:587
  48.4 19.8 %collective-permute-start.10 = (bf16[2064,128]{1,0:T(8,128)(2,1)S(1)}, bf16[2064,128]{1,0:T(8,128)(2,1)S(1)}, u32[]{:S(2)}, u32[]{:S(2)}) collective-permute-start(bf16[2064,128]{1,0:T(8,128)(2,1)S(1)} %pad_maximum_fusion), channel_id=1, source_target_pairs={{0,2},{1,3},{2,0},{3,1},{4,6},{5,7},{6,4},{7,5},{8,10},{9,11},{10,... | collective-permute-start | bytes 1585160 | tf_op jit(solution)/shard_map/ppermute | solution.py:587
  54.4 9.6 %collective-permute-start.11 = (bf16[512,256]{1,0:T(8,128)(2,1)S(1)}, bf16[512,256]{1,0:T(8,128)(2,1)S(1)}, u32[]{:S(2)}, u32[]{:S(2)}) collective-permute-start(bf16[512,256]{1,0:T(8,128)(2,1)S(1)} %slice_bitcast_fusion.4), channel_id=1, source_target_pairs={{0,1},{2,3},{4,5},{6,7},{1,0},{3,2},{5,4},{7,6},{8,9},{10,11},{12,... | collective-permute-start | bytes 786440 | tf_op jit(solution)/shard_map/ppermute | solution.py:461
  58.2 21.5 %collective-permute-start.13 = (bf16[512,256]{1,0:T(8,128)(2,1)S(1)}, bf16[512,256]{1,0:T(8,128)(2,1)S(1)}, u32[]{:S(2)}, u32[]{:S(2)}) collective-permute-start(bf16[512,256]{1,0:T(8,128)(2,1)S(1)} %slice_bitcast_fusion.3), channel_id=1, source_target_pairs={{0,1},{2,3},{4,5},{6,7},{1,0},{3,2},{5,4},{7,6},{8,9},{10,11},{12,... | collective-permute-start | bytes 786440 | tf_op jit(solution)/shard_map/ppermute | solution.py:461
  59.9 8.7 %copy-start.2 = (f32[512,128]{1,0:T(8,128)S(1)}, f32[512,128]{1,0:T(8,128)}, u32[]{:S(2)}) copy-start(f32[512,128]{1,0:T(8,128)} %get-tuple-element.42.cos_ref) | copy-start | bytes 786436
  59.9 8.7 %copy-start.4 = (f32[512,128]{1,0:T(8,128)S(1)}, f32[512,128]{1,0:T(8,128)}, u32[]{:S(2)}) copy-start(f32[512,128]{1,0:T(8,128)} %get-tuple-element.43.sin_ref) | copy-start | bytes 786436
  59.9 8.7 %copy-start.10 = (bf16[512,256]{1,0:T(8,128)(2,1)S(1)}, bf16[512,256]{1,0:T(8,128)(2,1)}, u32[]{:S(2)}) copy-start(bf16[512,256]{1,0:T(8,128)(2,1)} %get-tuple-element.44.rest_0_.kv_ref) | copy-start | bytes 786436
  64.1 15.6 %collective-permute-start.12 = (bf16[512,256]{1,0:T(8,128)(2,1)S(1)}, bf16[512,256]{1,0:T(8,128)(2,1)S(1)}, u32[]{:S(2)}, u32[]{:S(2)}) collective-permute-start(bf16[512,256]{1,0:T(8,128)(2,1)S(1)} %fusion), channel_id=1, source_target_pairs={{2,0},{3,1},{4,2},{5,3},{6,4},{7,5},{10,8},{11,9},{12,10},{13,11},... | collective-permute-start | bytes 786440 | tf_op jit(solution)/shard_map/ppermute | solution.py:461
  65.5 12.3 %collective-permute-start.15 = (bf16[2,2,256,128]{3,2,0,1:T(8,128)(2,1)S(1)}, bf16[2,2,256,128]{3,2,0,1:T(8,128)(2,1)S(1)}, u32[]{:S(2)}, u32[]{:S(2)}) collective-permute-start(bf16[2,2,256,128]{3,2,0,1:T(8,128)(2,1)S(1)} %fusion.4), channel_id=1, source_target_pairs={{0,2},{1,3},{2,0},{3,1},{4,6},{5,7},{6,4},{7,5},{8,10},{9,11},{10,... | collective-permute-start | bytes 786440 | tf_op jit(solution)/shard_map/ppermute | solution.py:587
  68.4 9.6 %collective-permute-start.16 = (bf16[2,2,256,128]{3,2,0,1:T(8,128)(2,1)S(1)}, bf16[2,2,256,128]{3,2,0,1:T(8,128)(2,1)S(1)}, u32[]{:S(2)}, u32[]{:S(2)}) collective-permute-start(bf16[2,2,256,128]{3,2,0,1:T(8,128)(2,1)S(1)} %fusion.3), channel_id=1, source_target_pairs={{0,16},{8,24},{16,0},{24,8},{1,17},{9,25},{17,1},{25,9},{2,18},{10... | collective-permute-start | bytes 786440 | tf_op jit(solution)/shard_map/ppermute | solution.py:587
  73.9 28.9 %copy-start.8 = (s32[1,64]{1,0:T(1,128)S(1)}, s32[1,64]{1,0:T(1,128)}, u32[]{:S(2)}) copy-start(s32[1,64]{1,0:T(1,128)} %param.12) | copy-start | bytes 772
  78.1 6.5 %collective-permute-start.17 = (bf16[1056,128]{1,0:T(8,128)(2,1)S(1)}, bf16[1056,128]{1,0:T(8,128)(2,1)S(1)}, u32[]{:S(2)}, u32[]{:S(2)}) collective-permute-start(bf16[1056,128]{1,0:T(8,128)(2,1)S(1)} %pad_maximum_fusion.1), channel_id=1, source_target_pairs={{0,1},{1,0},{2,3},{3,2},{4,5},{5,4},{6,7},{7,6},{8,9},{9,8},{10,11... | collective-permute-start | bytes 811016 | tf_op jit(solution)/shard_map/ppermute | solution.py:587
  79.8 15.5 %collective-permute-start.14 = (bf16[512,256]{1,0:T(8,128)(2,1)S(1)}, bf16[512,256]{1,0:T(8,128)(2,1)S(1)}, u32[]{:S(2)}, u32[]{:S(2)}) collective-permute-start(bf16[512,256]{1,0:T(8,128)(2,1)S(1)} %fusion.2), channel_id=1, source_target_pairs={{2,0},{3,1},{4,2},{5,3},{6,4},{7,5},{10,8},{11,9},{12,10},{13,11},... | collective-permute-start | bytes 786440 | tf_op jit(solution)/shard_map/ppermute | solution.py:461
  84.8 18.0 %collective-permute-start.18 = (bf16[576,128]{1,0:T(8,128)(2,1)S(1)}, bf16[576,128]{1,0:T(8,128)(2,1)S(1)}, u32[]{:S(2)}, u32[]{:S(2)}) collective-permute-start(bf16[576,128]{1,0:T(8,128)(2,1)S(1)} %pad_maximum_fusion.3), channel_id=1, source_target_pairs={{0,4},{1,5},{2,6},{3,7},{4,0},{5,1},{6,2},{7,3},{8,12},{9,13},{10,... | collective-permute-start | bytes 442376 | tf_op jit(solution)/shard_map/ppermute | solution.py:587
  (7 other events, 18.0 us)
